TPU v7x, 512 devices: a whole 4x4x16 slice. The times are simulated.
512 devices in a mesh: seq: 32 (over z, core), head: 16 (over y, x).
Axes of the slice: x: 4, y: 4, z: 16, core: 2. Of those that a mesh axis runs over, the one named last changes fastest.
Arguments:
- hidden_in: bfloat16 [8192, 4096], P('seq'), may hold values from -6 to 6
- w_qkv: bfloat16 [3, 4096, 4096], P(None, 'seq', 'head'), may hold values from -0.09375 to 0.09375
- doc_starts: int32 [9], replicated, may hold values from 0 to 8191, as said below
- beta_codes: int32 [8192, 32], P('seq', 'head'), may hold values from 0 to 4, as said below
- w_out: bfloat16 [4096, 4096], P('head', 'seq'), may hold values from -0.1875 to 0.1875
Outputs:
- layer_out: bfloat16 [8192, 4096], P('seq', 'head')
Inputs may be any that keep to these rules, and one draw needn't show every extreme that they name: `doc_starts`: strictly rising; the first is 0 and the last is 8191, a one-token final document. `beta_codes`: integer codes of the write strength beta = 1.6 + 0.1 * code.
All inputs are finite; a program needn't handle non-finite values.
Results may differ from a plain program's by a relative error of at most 0.02.
Values may be sent and summed in bfloat16 or wider, within the bound.
No kernel may reach another device: no remote copies, remote signals or barrier semaphores. Data moves between devices by JAX's collectives and lax.ppermute only.
A program may use at most 64 MiB of HBM per device.

v0:
```python
import jax
import jax.numpy as jnp
from jax import lax
from jax.sharding import PartitionSpec as P

highest_accuracy = lax.Precision.HIGHEST


def passed_along(value, axis, steps):
    count = lax.axis_size(axis)
    first, last = (max(0, -steps), min(count, count - steps))
    return lax.ppermute(value, axis, [(source, source + steps) for source in range(first, last)])


def bmatmul(left, right):
    return jnp.einsum("hij,hjk->hik", left, right, precision=highest_accuracy)


def unit_rows(matrix):
    return matrix * lax.rsqrt(jnp.sum(matrix * matrix, axis=-1, keepdims=True) + 1e-06)


def block_terms(query_blk, key_blk, value_blk, beta_blk, doc_blk):
    block_len = query_blk.shape[1]
    head_size = query_blk.shape[2]
    row_ids = lax.broadcasted_iota(jnp.int32, (block_len, block_len), 0)
    col_ids = lax.broadcasted_iota(jnp.int32, (block_len, block_len), 1)
    same_document = doc_blk[:, None] == doc_blk[None, :]
    strict_mask = same_document & (col_ids < row_ids)
    incl_mask = same_document & (col_ids <= row_ids)
    carry_in = (doc_blk == 0).astype(jnp.float32)
    last_doc = (doc_blk == doc_blk[-1]).astype(jnp.float32)
    last_keep = carry_in[-1]
    key_gram = jnp.einsum("hts,hus->htu", key_blk, key_blk, precision=highest_accuracy)
    system = jnp.eye(block_len, dtype=jnp.float32)[None] + jnp.where(
        strict_mask[None], beta_blk[:, :, None] * key_gram, 0.0
    )
    right_side = beta_blk[:, :, None] * jnp.concatenate(
        [value_blk, carry_in[None, :, None] * key_blk], axis=-1
    )
    solved = jax.scipy.linalg.solve_triangular(system, right_side, lower=True, unit_diagonal=True)
    fresh_vals = solved[..., :head_size]
    mixed_keys = solved[..., head_size:]
    query_key = jnp.where(
        incl_mask[None],
        jnp.einsum("hts,hus->htu", query_blk, key_blk, precision=highest_accuracy),
        0.0,
    )
    local_out = bmatmul(query_key, fresh_vals)
    carry_map = carry_in[None, :, None] * query_blk - bmatmul(query_key, mixed_keys)
    tail_keys = last_doc[None, :, None] * key_blk
    trans_map = last_keep * jnp.eye(head_size, dtype=jnp.float32)[None] - jnp.einsum(
        "hts,htu->hsu", tail_keys, mixed_keys, precision=highest_accuracy
    )
    state_add = jnp.einsum("hts,htv->hsv", tail_keys, fresh_vals, precision=highest_accuracy)
    return (carry_map, local_out, trans_map, state_add)


def per_device(hidden_in, w_qkv, doc_starts, beta_codes, w_out):
    tok_rows = hidden_in.shape[0]
    head_count = beta_codes.shape[1]
    feat_width = w_qkv.shape[2]
    head_size = feat_width // head_count
    projected = jnp.einsum(
        "td,pde->pte",
        hidden_in,
        lax.all_gather(w_qkv, "seq", axis=1, tiled=True),
        preferred_element_type=jnp.float32,
    ).astype(jnp.bfloat16)
    block_len = min(128, tok_rows)
    block_count = tok_rows // block_len

    def to_blocks(matrix):
        shaped = matrix.astype(jnp.float32).reshape(block_count, block_len, head_count, head_size)
        return jnp.transpose(shaped, (0, 2, 1, 3))

    queries = to_blocks(
        unit_rows(projected[0].astype(jnp.float32).reshape(tok_rows, head_count, head_size))
    )
    keys_all = to_blocks(
        unit_rows(projected[1].astype(jnp.float32).reshape(tok_rows, head_count, head_size))
    )
    values_all = to_blocks(projected[2])
    betas = 1.6 + 0.1 * beta_codes.astype(jnp.float32)
    betas = jnp.transpose(betas.reshape(block_count, block_len, head_count), (0, 2, 1))
    positions = lax.axis_index("seq") * tok_rows + jnp.arange(tok_rows, dtype=jnp.int32)
    is_start = jnp.any(positions[:, None] == doc_starts[None, :], axis=1).astype(jnp.int32)
    doc_index = jnp.cumsum(is_start.reshape(block_count, block_len), axis=1)
    blocks = (queries, keys_all, values_all, betas, doc_index)
    identity_mat = jnp.broadcast_to(
        jnp.eye(head_size, dtype=jnp.float32), (head_count, head_size, head_size)
    )
    zero_state = jnp.zeros((head_count, head_size, head_size), jnp.float32)

    def local_step(carry, block_in):
        transit, local_state = carry
        carry_map, local_out, trans_map, state_add = block_terms(*block_in)
        partial_out = local_out + bmatmul(carry_map, local_state)
        correction = bmatmul(carry_map, transit)
        return (
            (bmatmul(trans_map, transit), bmatmul(trans_map, local_state) + state_add),
            (partial_out, correction),
        )

    (transit, local_state), (partial_out, correction) = lax.scan(
        local_step, (identity_mat, zero_state), blocks
    )

    def relay(turn_index, incoming):
        return passed_along(
            (bmatmul(transit, incoming) + local_state).astype(jnp.bfloat16), "seq", 1
        ).astype(jnp.float32)

    state_in = lax.fori_loop(0, lax.axis_size("seq") - 1, relay, zero_state)

    def rerun_step(state_now, block_in):
        carry_map, local_out, trans_map, state_add = block_terms(*block_in)
        result = local_out + bmatmul(carry_map, state_now)
        return (bmatmul(trans_map, state_now) + state_add, result)

    final_state, outputs = lax.scan(rerun_step, state_in, blocks)
    outputs = jnp.transpose(outputs, (0, 2, 1, 3)).reshape(tok_rows, head_count, head_size)
    normed = outputs * lax.rsqrt(jnp.mean(outputs * outputs, axis=-1, keepdims=True) + 1e-05)
    normed = normed.astype(jnp.bfloat16).reshape(tok_rows, feat_width)
    terms = jnp.dot(
        normed, lax.all_gather(w_out, "seq", axis=1, tiled=True), preferred_element_type=jnp.float32
    )
    return lax.psum_scatter(terms.astype(jnp.bfloat16), "head", scatter_dimension=1, tiled=True)


def solution(mesh):
    in_specs = (P("seq", None), P(None, "seq", "head"), P(), P("seq", "head"), P("head", "seq"))
    out_specs = P("seq", "head")
    return jax.shard_map(
        per_device, mesh=mesh, in_specs=in_specs, out_specs=out_specs, check_vma=False
    )
```

profile of v0, /device:TPU:1, one launch (start us, length us, event | category | flops | bytes accessed | tf_op | source)
XLA Modules:
  0.0 533.7 jit_solution(8153678685199269172)
XLA Ops:
  11.1 92.6 %all-gather.3.cloned.1.call-done = bf16[3,4096,256]{1,2,0:T(8,128)(2,1)} async-done(((bf16[3,128,256]{1,2,0:T(8,128)(2,1)}), bf16[3,4096,256]{1,2,0:T(8,128)(2,1)}) %all-gather.3.cloned.1.call-update) | async-done | bytes 6291472 | tf_op jit(solution)/shard_map/all_gather | solution.py:67
  103.7 4.6 fusion.77
  115.4 49.7 %while.37 = (s32[]{:T(128)}, f32[2,128,128]{2,1,0:T(8,128)S(1)}, f32[2,128,128]{2,1,0:T(8,128)S(1)}, s32[2,128]{1,0:T(2,128)S(1)}, f32[2,2,128,128]{3,2,1,0:T(8,...) while((s32[]{:T(128)}, f32[2,128,128]{2,1,0:T(8,128)S(1)}, ...), condition=%wide.region_4.6_spmd.clone, body=%wide.region_3.5_spmd.clone.sunk | while | flops 352977536 | bytes 3876507 | solution.py:105
  116.3 19.7 %custom-call.12 = f32[2,1,128,128]{2,3,1,0:T(8,128)S(1)} custom-call(f32[2,1,128,128]{3,2,1,0:T(8,128)S(1)} %fusion.169), custom_call_target="InvertDiagBlocksLowerTriangular" | custom-call | tf_op jit(solution)/shard_map/while/body/eval_jaxpr/jit(_solve_triangular)/vmap()/triangular_solve | solution.py:41
  141.0 19.7 %custom-call.12 = f32[2,1,128,128]{2,3,1,0:T(8,128)S(1)} custom-call(f32[2,1,128,128]{3,2,1,0:T(8,128)S(1)} %fusion.169), custom_call_target="InvertDiagBlocksLowerTriangular" | custom-call | tf_op jit(solution)/shard_map/while/body/eval_jaxpr/jit(_solve_triangular)/vmap()/triangular_solve | solution.py:41
  165.1 197.7 %while.38 = (s32[]{:T(128)}, f32[2,128,128]{2,1,0:T(8,128)S(1)}, f32[2,128,128]{2,1,0:T(8,128)S(1)}, f32[2,128,128]{2,1,0:T(8,128)S(1)}, s32[]{:T(128)}, /*index=5*/s32[]{:T(128)}) while((s32[]{:T(128)}, f32[2,128,128]{2,1,0:T(8,128)S(1)}, f32[2,128,128]{2,1,0:T(8,128)S(1)}, f32[2,128,128]{2,1,0:T(8,128)S(1)}, s32[]{:T(128)}, ...), condition=%wide.region_6.8_spmd.clone, body=%wide.region_5.7_spmd.clone.sunk | while | flops 50462720 | bytes 917623 | solution.py:114
  263.6 5.5 %collective-permute-start = (bf16[2,128,128]{2,1,0:T(8,128)(2,1)S(1)}, bf16[2,128,128]{2,1,0:T(8,128)(2,1)S(1)}, u32[]{:S(2)}, u32[]{:S(2)}) collective-permute-start(bf16[2,128,128]{2,1,0:T(8,128)(2,1)S(1)} %fusion.176), channel_id=1, source_target_pairs={{0,16},{16,32},{32,48},{48,64},{64,80},{80,96},{96,112},{112,128},... | collective-permute-start | bytes 196616 | tf_op jit(solution)/shard_map/while/body/eval_jaxpr/ppermute | solution.py:12
  270.7 5.5 %collective-permute-start = (bf16[2,128,128]{2,1,0:T(8,128)(2,1)S(1)}, bf16[2,128,128]{2,1,0:T(8,128)(2,1)S(1)}, u32[]{:S(2)}, u32[]{:S(2)}) collective-permute-start(bf16[2,128,128]{2,1,0:T(8,128)(2,1)S(1)} %fusion.176), channel_id=1, source_target_pairs={{0,16},{16,32},{32,48},{48,64},{64,80},{80,96},{96,112},{112,128},... | collective-permute-start | bytes 196616 | tf_op jit(solution)/shard_map/while/body/eval_jaxpr/ppermute | solution.py:12
  277.9 5.5 %collective-permute-start = (bf16[2,128,128]{2,1,0:T(8,128)(2,1)S(1)}, bf16[2,128,128]{2,1,0:T(8,128)(2,1)S(1)}, u32[]{:S(2)}, u32[]{:S(2)}) collective-permute-start(bf16[2,128,128]{2,1,0:T(8,128)(2,1)S(1)} %fusion.176), channel_id=1, source_target_pairs={{0,16},{16,32},{32,48},{48,64},{64,80},{80,96},{96,112},{112,128},... | collective-permute-start | bytes 196616 | tf_op jit(solution)/shard_map/while/body/eval_jaxpr/ppermute | solution.py:12
  285.0 5.5 %collective-permute-start = (bf16[2,128,128]{2,1,0:T(8,128)(2,1)S(1)}, bf16[2,128,128]{2,1,0:T(8,128)(2,1)S(1)}, u32[]{:S(2)}, u32[]{:S(2)}) collective-permute-start(bf16[2,128,128]{2,1,0:T(8,128)(2,1)S(1)} %fusion.176), channel_id=1, source_target_pairs={{0,16},{16,32},{32,48},{48,64},{64,80},{80,96},{96,112},{112,128},... | collective-permute-start | bytes 196616 | tf_op jit(solution)/shard_map/while/body/eval_jaxpr/ppermute | solution.py:12
  292.1 5.5 %collective-permute-start = (bf16[2,128,128]{2,1,0:T(8,128)(2,1)S(1)}, bf16[2,128,128]{2,1,0:T(8,128)(2,1)S(1)}, u32[]{:S(2)}, u32[]{:S(2)}) collective-permute-start(bf16[2,128,128]{2,1,0:T(8,128)(2,1)S(1)} %fusion.176), channel_id=1, source_target_pairs={{0,16},{16,32},{32,48},{48,64},{64,80},{80,96},{96,112},{112,128},... | collective-permute-start | bytes 196616 | tf_op jit(solution)/shard_map/while/body/eval_jaxpr/ppermute | solution.py:12
  299.2 5.5 %collective-permute-start = (bf16[2,128,128]{2,1,0:T(8,128)(2,1)S(1)}, bf16[2,128,128]{2,1,0:T(8,128)(2,1)S(1)}, u32[]{:S(2)}, u32[]{:S(2)}) collective-permute-start(bf16[2,128,128]{2,1,0:T(8,128)(2,1)S(1)} %fusion.176), channel_id=1, source_target_pairs={{0,16},{16,32},{32,48},{48,64},{64,80},{80,96},{96,112},{112,128},... | collective-permute-start | bytes 196616 | tf_op jit(solution)/shard_map/while/body/eval_jaxpr/ppermute | solution.py:12
  306.3 5.5 %collective-permute-start = (bf16[2,128,128]{2,1,0:T(8,128)(2,1)S(1)}, bf16[2,128,128]{2,1,0:T(8,128)(2,1)S(1)}, u32[]{:S(2)}, u32[]{:S(2)}) collective-permute-start(bf16[2,128,128]{2,1,0:T(8,128)(2,1)S(1)} %fusion.176), channel_id=1, source_target_pairs={{0,16},{16,32},{32,48},{48,64},{64,80},{80,96},{96,112},{112,128},... | collective-permute-start | bytes 196616 | tf_op jit(solution)/shard_map/while/body/eval_jaxpr/ppermute | solution.py:12
  313.4 5.5 %collective-permute-start = (bf16[2,128,128]{2,1,0:T(8,128)(2,1)S(1)}, bf16[2,128,128]{2,1,0:T(8,128)(2,1)S(1)}, u32[]{:S(2)}, u32[]{:S(2)}) collective-permute-start(bf16[2,128,128]{2,1,0:T(8,128)(2,1)S(1)} %fusion.176), channel_id=1, source_target_pairs={{0,16},{16,32},{32,48},{48,64},{64,80},{80,96},{96,112},{112,128},... | collective-permute-start | bytes 196616 | tf_op jit(solution)/shard_map/while/body/eval_jaxpr/ppermute | solution.py:12
  320.5 5.5 %collective-permute-start = (bf16[2,128,128]{2,1,0:T(8,128)(2,1)S(1)}, bf16[2,128,128]{2,1,0:T(8,128)(2,1)S(1)}, u32[]{:S(2)}, u32[]{:S(2)}) collective-permute-start(bf16[2,128,128]{2,1,0:T(8,128)(2,1)S(1)} %fusion.176), channel_id=1, source_target_pairs={{0,16},{16,32},{32,48},{48,64},{64,80},{80,96},{96,112},{112,128},... | collective-permute-start | bytes 196616 | tf_op jit(solution)/shard_map/while/body/eval_jaxpr/ppermute | solution.py:12
  327.6 5.5 %collective-permute-start = (bf16[2,128,128]{2,1,0:T(8,128)(2,1)S(1)}, bf16[2,128,128]{2,1,0:T(8,128)(2,1)S(1)}, u32[]{:S(2)}, u32[]{:S(2)}) collective-permute-start(bf16[2,128,128]{2,1,0:T(8,128)(2,1)S(1)} %fusion.176), channel_id=1, source_target_pairs={{0,16},{16,32},{32,48},{48,64},{64,80},{80,96},{96,112},{112,128},... | collective-permute-start | bytes 196616 | tf_op jit(solution)/shard_map/while/body/eval_jaxpr/ppermute | solution.py:12
  334.7 5.5 %collective-permute-start = (bf16[2,128,128]{2,1,0:T(8,128)(2,1)S(1)}, bf16[2,128,128]{2,1,0:T(8,128)(2,1)S(1)}, u32[]{:S(2)}, u32[]{:S(2)}) collective-permute-start(bf16[2,128,128]{2,1,0:T(8,128)(2,1)S(1)} %fusion.176), channel_id=1, source_target_pairs={{0,16},{16,32},{32,48},{48,64},{64,80},{80,96},{96,112},{112,128},... | collective-permute-start | bytes 196616 | tf_op jit(solution)/shard_map/while/body/eval_jaxpr/ppermute | solution.py:12
  341.8 5.5 %collective-permute-start = (bf16[2,128,128]{2,1,0:T(8,128)(2,1)S(1)}, bf16[2,128,128]{2,1,0:T(8,128)(2,1)S(1)}, u32[]{:S(2)}, u32[]{:S(2)}) collective-permute-start(bf16[2,128,128]{2,1,0:T(8,128)(2,1)S(1)} %fusion.176), channel_id=1, source_target_pairs={{0,16},{16,32},{32,48},{48,64},{64,80},{80,96},{96,112},{112,128},... | collective-permute-start | bytes 196616 | tf_op jit(solution)/shard_map/while/body/eval_jaxpr/ppermute | solution.py:12
  348.9 5.5 %collective-permute-start = (bf16[2,128,128]{2,1,0:T(8,128)(2,1)S(1)}, bf16[2,128,128]{2,1,0:T(8,128)(2,1)S(1)}, u32[]{:S(2)}, u32[]{:S(2)}) collective-permute-start(bf16[2,128,128]{2,1,0:T(8,128)(2,1)S(1)} %fusion.176), channel_id=1, source_target_pairs={{0,16},{16,32},{32,48},{48,64},{64,80},{80,96},{96,112},{112,128},... | collective-permute-start | bytes 196616 | tf_op jit(solution)/shard_map/while/body/eval_jaxpr/ppermute | solution.py:12
  356.0 5.5 %collective-permute-start = (bf16[2,128,128]{2,1,0:T(8,128)(2,1)S(1)}, bf16[2,128,128]{2,1,0:T(8,128)(2,1)S(1)}, u32[]{:S(2)}, u32[]{:S(2)}) collective-permute-start(bf16[2,128,128]{2,1,0:T(8,128)(2,1)S(1)} %fusion.176), channel_id=1, source_target_pairs={{0,16},{16,32},{32,48},{48,64},{64,80},{80,96},{96,112},{112,128},... | collective-permute-start | bytes 196616 | tf_op jit(solution)/shard_map/while/body/eval_jaxpr/ppermute | solution.py:12
  362.8 52.2 %while.36 = (s32[]{:T(128)}, f32[2,128,128]{2,1,0:T(8,128)S(1)}, f32[2,2,128,128]{3,2,1,0:T(8,128)}, s32[2,128]{1,0:T(2,128)S(1)}, f32[2,2,128,128]{3,2,1,0:T(8,...) while((s32[]{:T(128)}, f32[2,128,128]{2,1,0:T(8,128)S(1)}, ...), condition=%wide.region_9.11_spmd, body=%wide.region_8.10_spmd.sunk | while | flops 504103552 | bytes 7187665 | solution.py:121
  363.4 19.7 %custom-call.11 = f32[2,1,128,128]{2,3,1,0:T(8,128)S(1)} custom-call(f32[2,1,128,128]{3,2,1,0:T(8,128)S(1)} %fusion.154), custom_call_target="InvertDiagBlocksLowerTriangular" | custom-call | tf_op jit(solution)/shard_map/while/body/eval_jaxpr/jit(_solve_triangular)/vmap()/triangular_solve | solution.py:41
  389.5 19.7 %custom-call.11 = f32[2,1,128,128]{2,3,1,0:T(8,128)S(1)} custom-call(f32[2,1,128,128]{3,2,1,0:T(8,128)S(1)} %fusion.154), custom_call_target="InvertDiagBlocksLowerTriangular" | custom-call | tf_op jit(solution)/shard_map/while/body/eval_jaxpr/jit(_solve_triangular)/vmap()/triangular_solve | solution.py:41
  421.5 105.7 %reduce-scatter.2.cloned.1.call-done = bf16[256,256]{1,0:T(8,128)(2,1)} async-done(((bf16[256,4096]{1,0:T(8,128)(2,1)}), bf16[256,256]{1,0:T(8,128)(2,1)}) %reduce-scatter.2.cloned.1.call-update) | async-done | bytes 131088 | tf_op jit(solution)/shard_map/reduce_scatter | solution.py:128
  (235 shorter events, 160.2 us)
Async XLA Ops:
  6.5 97.2 %all-gather.3.cloned.1.call-start = ((), (), s32[]{:S(2)}) async-start(), calls=%async_computation.1 | async-start | bytes 6488064 | tf_op jit(solution)/shard_map/all_gather | solution.py:67
  8.5 409.0 %all-gather.5.cloned.1.call-start = ((), (), s32[]{:S(2)}) async-start(), calls=%async_computation.2 | async-start | bytes 2162688 | tf_op jit(solution)/shard_map/all_gather | solution.py:126
  9.2 518.0 %reduce-scatter.2.cloned.1.call-start = ((), (), s32[]{:S(2)}) async-start(), calls=%async_computation.3 | async-start | bytes 2228224 | tf_op jit(solution)/shard_map/reduce_scatter | solution.py:128
  186.9 5.6 %collective-permute-start = (bf16[2,128,128]{2,1,0:T(8,128)(2,1)S(1)}, bf16[2,128,128]{2,1,0:T(8,128)(2,1)S(1)}, u32[]{:S(2)}, u32[]{:S(2)}) collective-permute-start(bf16[2,128,128]{2,1,0:T(8,128)(2,1)S(1)} %fusion.176), channel_id=1, source_target_pairs={{0,16},{16,32},{32,48},{48,64},{64,80},{80,96},{96,112},{112,128},... | collective-permute-start | bytes 196616 | tf_op jit(solution)/shard_map/while/body/eval_jaxpr/ppermute | solution.py:12
  192.8 5.6 %collective-permute-start = (bf16[2,128,128]{2,1,0:T(8,128)(2,1)S(1)}, bf16[2,128,128]{2,1,0:T(8,128)(2,1)S(1)}, u32[]{:S(2)}, u32[]{:S(2)}) collective-permute-start(bf16[2,128,128]{2,1,0:T(8,128)(2,1)S(1)} %fusion.176), channel_id=1, source_target_pairs={{0,16},{16,32},{32,48},{48,64},{64,80},{80,96},{96,112},{112,128},... | collective-permute-start | bytes 196616 | tf_op jit(solution)/shard_map/while/body/eval_jaxpr/ppermute | solution.py:12
  210.5 5.6 %collective-permute-start = (bf16[2,128,128]{2,1,0:T(8,128)(2,1)S(1)}, bf16[2,128,128]{2,1,0:T(8,128)(2,1)S(1)}, u32[]{:S(2)}, u32[]{:S(2)}) collective-permute-start(bf16[2,128,128]{2,1,0:T(8,128)(2,1)S(1)} %fusion.176), channel_id=1, source_target_pairs={{0,16},{16,32},{32,48},{48,64},{64,80},{80,96},{96,112},{112,128},... | collective-permute-start | bytes 196616 | tf_op jit(solution)/shard_map/while/body/eval_jaxpr/ppermute | solution.py:12
  216.4 5.6 %collective-permute-start = (bf16[2,128,128]{2,1,0:T(8,128)(2,1)S(1)}, bf16[2,128,128]{2,1,0:T(8,128)(2,1)S(1)}, u32[]{:S(2)}, u32[]{:S(2)}) collective-permute-start(bf16[2,128,128]{2,1,0:T(8,128)(2,1)S(1)} %fusion.176), channel_id=1, source_target_pairs={{0,16},{16,32},{32,48},{48,64},{64,80},{80,96},{96,112},{112,128},... | collective-permute-start | bytes 196616 | tf_op jit(solution)/shard_map/while/body/eval_jaxpr/ppermute | solution.py:12
  222.3 5.6 %collective-permute-start = (bf16[2,128,128]{2,1,0:T(8,128)(2,1)S(1)}, bf16[2,128,128]{2,1,0:T(8,128)(2,1)S(1)}, u32[]{:S(2)}, u32[]{:S(2)}) collective-permute-start(bf16[2,128,128]{2,1,0:T(8,128)(2,1)S(1)} %fusion.176), channel_id=1, source_target_pairs={{0,16},{16,32},{32,48},{48,64},{64,80},{80,96},{96,112},{112,128},... | collective-permute-start | bytes 196616 | tf_op jit(solution)/shard_map/while/body/eval_jaxpr/ppermute | solution.py:12
  251.7 5.6 %collective-permute-start = (bf16[2,128,128]{2,1,0:T(8,128)(2,1)S(1)}, bf16[2,128,128]{2,1,0:T(8,128)(2,1)S(1)}, u32[]{:S(2)}, u32[]{:S(2)}) collective-permute-start(bf16[2,128,128]{2,1,0:T(8,128)(2,1)S(1)} %fusion.176), channel_id=1, source_target_pairs={{0,16},{16,32},{32,48},{48,64},{64,80},{80,96},{96,112},{112,128},... | collective-permute-start | bytes 196616 | tf_op jit(solution)/shard_map/while/body/eval_jaxpr/ppermute | solution.py:12
  257.6 5.7 %collective-permute-start = (bf16[2,128,128]{2,1,0:T(8,128)(2,1)S(1)}, bf16[2,128,128]{2,1,0:T(8,128)(2,1)S(1)}, u32[]{:S(2)}, u32[]{:S(2)}) collective-permute-start(bf16[2,128,128]{2,1,0:T(8,128)(2,1)S(1)} %fusion.176), channel_id=1, source_target_pairs={{0,16},{16,32},{32,48},{48,64},{64,80},{80,96},{96,112},{112,128},... | collective-permute-start | bytes 196616 | tf_op jit(solution)/shard_map/while/body/eval_jaxpr/ppermute | solution.py:12
  263.6 6.8 %collective-permute-start = (bf16[2,128,128]{2,1,0:T(8,128)(2,1)S(1)}, bf16[2,128,128]{2,1,0:T(8,128)(2,1)S(1)}, u32[]{:S(2)}, u32[]{:S(2)}) collective-permute-start(bf16[2,128,128]{2,1,0:T(8,128)(2,1)S(1)} %fusion.176), channel_id=1, source_target_pairs={{0,16},{16,32},{32,48},{48,64},{64,80},{80,96},{96,112},{112,128},... | collective-permute-start | bytes 196616 | tf_op jit(solution)/shard_map/while/body/eval_jaxpr/ppermute | solution.py:12
  270.7 6.8 %collective-permute-start = (bf16[2,128,128]{2,1,0:T(8,128)(2,1)S(1)}, bf16[2,128,128]{2,1,0:T(8,128)(2,1)S(1)}, u32[]{:S(2)}, u32[]{:S(2)}) collective-permute-start(bf16[2,128,128]{2,1,0:T(8,128)(2,1)S(1)} %fusion.176), channel_id=1, source_target_pairs={{0,16},{16,32},{32,48},{48,64},{64,80},{80,96},{96,112},{112,128},... | collective-permute-start | bytes 196616 | tf_op jit(solution)/shard_map/while/body/eval_jaxpr/ppermute | solution.py:12
  277.9 6.8 %collective-permute-start = (bf16[2,128,128]{2,1,0:T(8,128)(2,1)S(1)}, bf16[2,128,128]{2,1,0:T(8,128)(2,1)S(1)}, u32[]{:S(2)}, u32[]{:S(2)}) collective-permute-start(bf16[2,128,128]{2,1,0:T(8,128)(2,1)S(1)} %fusion.176), channel_id=1, source_target_pairs={{0,16},{16,32},{32,48},{48,64},{64,80},{80,96},{96,112},{112,128},... | collective-permute-start | bytes 196616 | tf_op jit(solution)/shard_map/while/body/eval_jaxpr/ppermute | solution.py:12
  285.0 6.8 %collective-permute-start = (bf16[2,128,128]{2,1,0:T(8,128)(2,1)S(1)}, bf16[2,128,128]{2,1,0:T(8,128)(2,1)S(1)}, u32[]{:S(2)}, u32[]{:S(2)}) collective-permute-start(bf16[2,128,128]{2,1,0:T(8,128)(2,1)S(1)} %fusion.176), channel_id=1, source_target_pairs={{0,16},{16,32},{32,48},{48,64},{64,80},{80,96},{96,112},{112,128},... | collective-permute-start | bytes 196616 | tf_op jit(solution)/shard_map/while/body/eval_jaxpr/ppermute | solution.py:12
  292.1 6.8 %collective-permute-start = (bf16[2,128,128]{2,1,0:T(8,128)(2,1)S(1)}, bf16[2,128,128]{2,1,0:T(8,128)(2,1)S(1)}, u32[]{:S(2)}, u32[]{:S(2)}) collective-permute-start(bf16[2,128,128]{2,1,0:T(8,128)(2,1)S(1)} %fusion.176), channel_id=1, source_target_pairs={{0,16},{16,32},{32,48},{48,64},{64,80},{80,96},{96,112},{112,128},... | collective-permute-start | bytes 196616 | tf_op jit(solution)/shard_map/while/body/eval_jaxpr/ppermute | solution.py:12
  299.2 6.8 %collective-permute-start = (bf16[2,128,128]{2,1,0:T(8,128)(2,1)S(1)}, bf16[2,128,128]{2,1,0:T(8,128)(2,1)S(1)}, u32[]{:S(2)}, u32[]{:S(2)}) collective-permute-start(bf16[2,128,128]{2,1,0:T(8,128)(2,1)S(1)} %fusion.176), channel_id=1, source_target_pairs={{0,16},{16,32},{32,48},{48,64},{64,80},{80,96},{96,112},{112,128},... | collective-permute-start | bytes 196616 | tf_op jit(solution)/shard_map/while/body/eval_jaxpr/ppermute | solution.py:12
  306.3 6.8 %collective-permute-start = (bf16[2,128,128]{2,1,0:T(8,128)(2,1)S(1)}, bf16[2,128,128]{2,1,0:T(8,128)(2,1)S(1)}, u32[]{:S(2)}, u32[]{:S(2)}) collective-permute-start(bf16[2,128,128]{2,1,0:T(8,128)(2,1)S(1)} %fusion.176), channel_id=1, source_target_pairs={{0,16},{16,32},{32,48},{48,64},{64,80},{80,96},{96,112},{112,128},... | collective-permute-start | bytes 196616 | tf_op jit(solution)/shard_map/while/body/eval_jaxpr/ppermute | solution.py:12
  313.4 6.8 %collective-permute-start = (bf16[2,128,128]{2,1,0:T(8,128)(2,1)S(1)}, bf16[2,128,128]{2,1,0:T(8,128)(2,1)S(1)}, u32[]{:S(2)}, u32[]{:S(2)}) collective-permute-start(bf16[2,128,128]{2,1,0:T(8,128)(2,1)S(1)} %fusion.176), channel_id=1, source_target_pairs={{0,16},{16,32},{32,48},{48,64},{64,80},{80,96},{96,112},{112,128},... | collective-permute-start | bytes 196616 | tf_op jit(solution)/shard_map/while/body/eval_jaxpr/ppermute | solution.py:12
  320.5 6.8 %collective-permute-start = (bf16[2,128,128]{2,1,0:T(8,128)(2,1)S(1)}, bf16[2,128,128]{2,1,0:T(8,128)(2,1)S(1)}, u32[]{:S(2)}, u32[]{:S(2)}) collective-permute-start(bf16[2,128,128]{2,1,0:T(8,128)(2,1)S(1)} %fusion.176), channel_id=1, source_target_pairs={{0,16},{16,32},{32,48},{48,64},{64,80},{80,96},{96,112},{112,128},... | collective-permute-start | bytes 196616 | tf_op jit(solution)/shard_map/while/body/eval_jaxpr/ppermute | solution.py:12
  327.6 6.8 %collective-permute-start = (bf16[2,128,128]{2,1,0:T(8,128)(2,1)S(1)}, bf16[2,128,128]{2,1,0:T(8,128)(2,1)S(1)}, u32[]{:S(2)}, u32[]{:S(2)}) collective-permute-start(bf16[2,128,128]{2,1,0:T(8,128)(2,1)S(1)} %fusion.176), channel_id=1, source_target_pairs={{0,16},{16,32},{32,48},{48,64},{64,80},{80,96},{96,112},{112,128},... | collective-permute-start | bytes 196616 | tf_op jit(solution)/shard_map/while/body/eval_jaxpr/ppermute | solution.py:12
  334.7 6.8 %collective-permute-start = (bf16[2,128,128]{2,1,0:T(8,128)(2,1)S(1)}, bf16[2,128,128]{2,1,0:T(8,128)(2,1)S(1)}, u32[]{:S(2)}, u32[]{:S(2)}) collective-permute-start(bf16[2,128,128]{2,1,0:T(8,128)(2,1)S(1)} %fusion.176), channel_id=1, source_target_pairs={{0,16},{16,32},{32,48},{48,64},{64,80},{80,96},{96,112},{112,128},... | collective-permute-start | bytes 196616 | tf_op jit(solution)/shard_map/while/body/eval_jaxpr/ppermute | solution.py:12
  341.8 6.8 %collective-permute-start = (bf16[2,128,128]{2,1,0:T(8,128)(2,1)S(1)}, bf16[2,128,128]{2,1,0:T(8,128)(2,1)S(1)}, u32[]{:S(2)}, u32[]{:S(2)}) collective-permute-start(bf16[2,128,128]{2,1,0:T(8,128)(2,1)S(1)} %fusion.176), channel_id=1, source_target_pairs={{0,16},{16,32},{32,48},{48,64},{64,80},{80,96},{96,112},{112,128},... | collective-permute-start | bytes 196616 | tf_op jit(solution)/shard_map/while/body/eval_jaxpr/ppermute | solution.py:12
  348.9 6.8 %collective-permute-start = (bf16[2,128,128]{2,1,0:T(8,128)(2,1)S(1)}, bf16[2,128,128]{2,1,0:T(8,128)(2,1)S(1)}, u32[]{:S(2)}, u32[]{:S(2)}) collective-permute-start(bf16[2,128,128]{2,1,0:T(8,128)(2,1)S(1)} %fusion.176), channel_id=1, source_target_pairs={{0,16},{16,32},{32,48},{48,64},{64,80},{80,96},{96,112},{112,128},... | collective-permute-start | bytes 196616 | tf_op jit(solution)/shard_map/while/body/eval_jaxpr/ppermute | solution.py:12
  356.0 6.8 %collective-permute-start = (bf16[2,128,128]{2,1,0:T(8,128)(2,1)S(1)}, bf16[2,128,128]{2,1,0:T(8,128)(2,1)S(1)}, u32[]{:S(2)}, u32[]{:S(2)}) collective-permute-start(bf16[2,128,128]{2,1,0:T(8,128)(2,1)S(1)} %fusion.176), channel_id=1, source_target_pairs={{0,16},{16,32},{32,48},{48,64},{64,80},{80,96},{96,112},{112,128},... | collective-permute-start | bytes 196616 | tf_op jit(solution)/shard_map/while/body/eval_jaxpr/ppermute | solution.py:12
  (16 other events, 359.7 us)
Sparse Core Ops, SparseCore 0:
  9.4 94.2 all-gather.2
  105.7 69.5 all-gather.4
  421.6 105.5 reduce-scatter.1
where the time goes:
time: 535 us; the launch traced here: 534 us
  waiting for transfers between devices  240 us (45%)
  starting transfers between devices  147 us (27%)
  other arithmetic  90.8 us (17%)
  matrix products  27.9 us (5%)
  between operations  13.3 us (2%)
  local copies, waits for them, and re-layouts  12.8 us (2%)
    ppermute x31, starting transfers between devices, passed_along(): lax.ppermute(value, axis, [(source, source + steps) for source in range(f...  147 us
    reduce_scatter x1, waiting for transfers between devices, per_device(): lax.psum_scatter(terms.astype(jnp.bfloat16), 'head', scatter_dimension=1,...  106 us
    all_gather x1, waiting for transfers between devices, per_device(): lax.all_gather(w_qkv, 'seq', axis=1, tiled=True)  92.6 us
    another operation x10, other arithmetic, block_terms(): jax.scipy.linalg.solve_triangular(system, right_side, lower=True, unit_di...  78.9 us
    ppermute x31, waiting for transfers between devices, passed_along(): lax.ppermute(value, axis, [(source, source + steps) for source in range(f...  40.6 us
    dot_general x43, matrix products, bmatmul(): return jnp.einsum('hij,hjk->hik', left, right, precision=highest_accuracy)  11.6 us
  transfers between devices with their start and end apart: 34, of which 33 were waited for; matrix products, arithmetic and copies ran while one was open for 24% of the time, Pallas kernels for 0%

commit v1 on v0

v1 whole, which is shorter than its diff:
```python
import jax
import jax.numpy as jnp
import numpy as np
from jax import lax
from jax.experimental import pallas as pl
from jax.experimental.pallas import tpu as pltpu
from jax.sharding import Mesh
from jax.sharding import PartitionSpec as P

F32 = jnp.float32
BF16 = jnp.bfloat16
F16 = jnp.float16
HD = 128
TOK = 512
W_SCALE = 2.0**19
L_SCALE = 2.0**-6
NN = (((1,), (0,)), ((), ()))


def split(a):
    hi = a.astype(BF16)
    return hi, (a - hi.astype(F32)).astype(BF16)


def dot(a, b):
    return lax.dot_general(a, b, NN, preferred_element_type=F32)


def mm3s(a, b):
    (ah, al), (bh, bl) = a, b
    return dot(
        jnp.concatenate([ah, ah, al], axis=1), jnp.concatenate([bh, bl, bh], axis=0)
    )


def mm3(a, b):
    return mm3s(split(a), split(b))


def unit_rows(m):
    return m * lax.rsqrt(jnp.sum(m * m, axis=-1, keepdims=True) + 1e-06)


def count_le(ds_ref, pos):
    total = jnp.zeros(jnp.shape(pos), jnp.int32)
    for j in range(ds_ref.shape[0]):
        total = total + (ds_ref[j] <= pos).astype(jnp.int32)
    return total


def local_kernel(meta_ref, ds_ref, own_ref, sib_ref, beta_ref, tl_ref, b_ref):
    pos0 = meta_ref[0] * TOK
    first = meta_ref[1] == 0
    half = TOK // 2

    def tokens(p):
        own = own_ref[p].astype(F32)
        sib = sib_ref[p].astype(F32)
        return jnp.concatenate(
            [jnp.where(first, own, sib), jnp.where(first, sib, own)], axis=0
        )

    query = unit_rows(tokens(0))
    key = unit_rows(tokens(1))
    value = tokens(2)
    beta = 1.6 + 0.1 * beta_ref[...]
    doc_col = count_le(ds_ref, pos0 + lax.broadcasted_iota(jnp.int32, (TOK, 1), 0))
    doc_row = count_le(ds_ref, pos0 + lax.broadcasted_iota(jnp.int32, (1, TOK), 1))
    prev_doc = count_le(ds_ref, pos0 - 1)
    last_doc = count_le(ds_ref, pos0 + TOK - 1)
    carry_in = (doc_col == prev_doc).astype(F32)
    tail_row = (doc_row == last_doc).astype(F32)
    last_keep = (last_doc == prev_doc).astype(F32)

    key_s = split(key)
    key_t = jnp.transpose(key)
    key_ts = split(key_t)

    def part(pair, rows, cols):
        return pair[0][rows, cols], pair[1][rows, cols]

    every = slice(None)

    def system(rows, cols, inclusive=False, left=None, scale=None):
        gram = mm3s(part(left, rows, every), part(key_ts, every, cols))
        shape = gram.shape
        r = lax.broadcasted_iota(jnp.int32, shape, 0) + rows.start
        c = lax.broadcasted_iota(jnp.int32, shape, 1) + cols.start
        keep = (c <= r) if inclusive else (c < r)
        keep = keep & (doc_col[rows] == doc_row[:, cols])
        if scale is not None:
            gram = scale[rows] * gram
        return jnp.where(keep, gram, 0.0)

    quarter = [slice(128 * i, 128 * i + 128) for i in range(4)]
    rows128 = lax.broadcasted_iota(jnp.int32, (128, 128), 0)
    cols128 = lax.broadcasted_iota(jnp.int32, (128, 128), 1)
    eye128 = (rows128 == cols128).astype(F32)
    diag = [system(s, s, left=key_s, scale=beta) for s in quarter]
    inv = []
    for a in diag:
        m = ((rows128 >> 1) == (cols128 >> 1)) & (rows128 != cols128)
        inv.append(eye128 - jnp.where(m, a, 0.0))
    for lev in range(1, 7):
        m = ((rows128 >> (lev + 1)) == (cols128 >> (lev + 1))) & (
            (rows128 >> lev) != (cols128 >> lev)
        )
        xs = [split(x) for x in inv]
        ys = [mm3s(x, split(jnp.where(m, a, 0.0))) for x, a in zip(xs, diag)]
        inv = [x - mm3s(split(y), s) for x, y, s in zip(inv, ys, xs)]
    pair_inv = []
    for i in (0, 2):
        off = system(quarter[i + 1], quarter[i], left=key_s, scale=beta)
        low = -mm3(mm3(inv[i + 1], off), inv[i])
        top = jnp.concatenate([inv[i], jnp.zeros((128, 128), F32)], axis=1)
        bottom = jnp.concatenate([low, inv[i + 1]], axis=1)
        pair_inv.append(jnp.concatenate([top, bottom], axis=0))
    lo, hi = slice(0, half), slice(half, TOK)
    right = beta * jnp.concatenate([carry_in * key, value], axis=1)
    cross = system(hi, lo, left=key_s, scale=beta)
    wu_lo = mm3(pair_inv[0], right[lo])
    wu_lo_s = split(wu_lo)
    wu_hi = mm3(pair_inv[1], right[hi] - mm3s(split(cross), wu_lo_s))
    wu_s = (
        jnp.concatenate([wu_lo_s[0], split(wu_hi)[0]], axis=0),
        jnp.concatenate([wu_lo_s[1], split(wu_hi)[1]], axis=0),
    )
    tail = split(tail_row * key_t)
    tl = mm3s(tail, wu_s)
    trans = last_keep * eye128 - tl[:, :HD]
    tl_ref[0:HD, :] = trans
    tl_ref[HD : 2 * HD, :] = tl[:, HD:] * L_SCALE

    query_s = split(query)
    p_ll = split(system(lo, lo, inclusive=True, left=query_s))
    p_h = split(
        jnp.concatenate(
            [
                mm_masked
                for mm_masked in (
                    system(hi, lo, inclusive=True, left=query_s),
                    system(hi, hi, inclusive=True, left=query_s),
                )
            ],
            axis=1,
        )
    )
    out_lo = mm3s(p_ll, part(wu_s, lo, every))
    out_hi = mm3s(p_h, wu_s)
    b_ref[0, lo, :] = carry_in[lo] * query[lo] - out_lo[:, :HD]
    b_ref[0, hi, :] = carry_in[hi] * query[hi] - out_hi[:, :HD]
    b_ref[1, lo, :] = out_lo[:, HD:]
    b_ref[1, hi, :] = out_hi[:, HD:]


def finish_kernel(meta_ref, ds_ref, tl_ref, b_ref, out_ref):
    here = meta_ref[0]
    start = jnp.int32(0)
    for j in range(ds_ref.shape[0]):
        pos = ds_ref[j]
        start = jnp.where(pos < here * TOK, jnp.maximum(start, pos // TOK), start)

    def fold(j, state):
        block = tl_ref[j]
        sh, sl = split(state)
        left = block[:HD]
        add = block[HD:].astype(F32) * (1.0 / L_SCALE)
        return dot(jnp.concatenate([left, left], axis=1), jnp.concatenate([sh, sl], axis=0)) + add

    state = lax.fori_loop(start, here, fold, jnp.zeros((HD, HD), F32))
    out = mm3(b_ref[0], state) + b_ref[1]
    out = out * lax.rsqrt(jnp.mean(out * out, axis=-1, keepdims=True) + 1e-05)
    out_ref[...] = out.astype(BF16)


SMEM = pl.BlockSpec(memory_space=pltpu.SMEM)
VMEM = pl.BlockSpec(memory_space=pltpu.VMEM)


def local_terms(meta, doc_starts, own, sib, beta):
    return pl.pallas_call(
        local_kernel,
        out_shape=(
            jax.ShapeDtypeStruct((2 * HD, HD), F32),
            jax.ShapeDtypeStruct((2, TOK, HD), F32),
        ),
        in_specs=[SMEM, SMEM, VMEM, VMEM, VMEM],
        out_specs=(VMEM, VMEM),
        compiler_params=pltpu.CompilerParams(vmem_limit_bytes=48 << 20),
    )(meta, doc_starts, own, sib, beta)


def finish(meta, doc_starts, tl, b):
    return pl.pallas_call(
        finish_kernel,
        out_shape=jax.ShapeDtypeStruct((TOK, HD), BF16),
        in_specs=[SMEM, SMEM, VMEM, VMEM],
        out_specs=VMEM,
        compiler_params=pltpu.CompilerParams(vmem_limit_bytes=32 << 20),
    )(meta, doc_starts, tl, b)


def swap(value):
    return lax.ppermute(value, "c", [(0, 1), (1, 0)])


def per_device(hidden_in, w_qkv, doc_starts, beta_codes, w_out):
    z = lax.axis_index("z")
    c = lax.axis_index("c")
    first = c == 0
    half = hidden_in.shape[0]
    meta = jnp.stack([z, c]).astype(jnp.int32)

    def pick(array, axis, index):
        return lax.dynamic_slice_in_dim(array, index * HD, HD, axis=axis)

    codes = beta_codes.astype(BF16)
    give = jnp.concatenate(
        [
            pick(w_qkv, 2, 1 - c).reshape(3 * HD, HD),
            pick(w_out, 0, 1 - c),
            lax.dynamic_slice_in_dim(codes, 1 - c, 1, axis=1).reshape(half // HD, HD),
            jnp.zeros((16 - half // HD, HD), BF16),
        ],
        axis=0,
    )
    got = swap(give)
    hidden_sib = swap(hidden_in)

    def ordered(mine, other, axis=0):
        return jnp.concatenate(
            [jnp.where(first, mine, other), jnp.where(first, other, mine)], axis=axis
        )

    w_mine = pick(w_qkv, 2, c).reshape(1, 3, HD, HD)
    w_chip = ordered(w_mine, got[: 3 * HD].reshape(1, 3, HD, HD))
    w_f16 = (w_chip.astype(F32) * W_SCALE).astype(F16)
    w_all = lax.all_gather(w_f16, "z", axis=0)
    w_all = (w_all.astype(F32) * (1.0 / W_SCALE)).astype(BF16)

    wo_chip = ordered(pick(w_out, 0, c), got[3 * HD : 4 * HD], axis=1)
    wo_rows = lax.all_gather(wo_chip, "z", axis=0)
    wo_cols = lax.all_to_all(wo_rows, "h", 0, 0)

    beta_mine = lax.dynamic_slice_in_dim(codes, c, 1, axis=1)
    beta = ordered(beta_mine, got[4 * HD : 4 * HD + half // HD].reshape(half, 1)).astype(F32)

    def project(hid):
        return jnp.einsum(
            "tzcd,zcpde->pte",
            hid.reshape(half, w_all.shape[0], 2, HD),
            w_all,
            preferred_element_type=F32,
        ).astype(BF16)

    tl, b = local_terms(meta, doc_starts, project(hidden_in), project(hidden_sib), beta)
    tl_all = lax.all_gather(tl.astype(F16), "z", axis=0).astype(BF16)
    normed = finish(meta, doc_starts, tl_all, b)
    normed_all = lax.all_gather(normed.astype(F16), "h", axis=0).astype(BF16)
    terms = jnp.einsum("htf,hfn->tn", normed_all, wo_cols, preferred_element_type=F32)
    mine = lax.dynamic_slice_in_dim(terms, c * half, half, axis=0)
    other = lax.dynamic_slice_in_dim(terms, (1 - c) * half, half, axis=0)
    return (mine + swap(other)).astype(BF16)


def solution(mesh):
    seq, head = mesh.devices.shape
    fine = Mesh(mesh.devices.reshape(seq // 2, 2, head), ("z", "c", "h"))
    tokens = ("z", "c")
    in_specs = (P(tokens, None), P(None, tokens, "h"), P(), P(tokens, "h"), P("h", tokens))
    return jax.shard_map(
        per_device, mesh=fine, in_specs=in_specs, out_specs=P(tokens, "h"), check_vma=False
    )
```

time: 535 us -> 184 us (0.34)
  waiting for transfers between devices: 240 us -> 1.18 us
  starting transfers between devices: 147 us -> 39.3 us
  blocking collectives: 0 us -> 103 us
  other arithmetic: 90.8 us -> 3.67 us
  matrix products: 27.9 us -> 6.24 us
  Pallas kernels: 0 us -> 6.22 us
    ppermute x31 -> x3, starting transfers between devices: 147 us -> 32.3 us  [swap(): return lax.ppermute(value, 'c', [(0, 1), (1, 0)])]
    reduce_scatter x1 -> x0, waiting for transfers between devices: 106 us -> none  [per_device(): lax.psum_scatter(terms.astype(jnp.bfloat16), 'head', scatter_dimension=1,...]
    all_gather x0 -> x3, blocking collectives: none -> 103 us  [the longest x1 52.9 us: per_device(): w_all = lax.all_gather(w_f16, 'z', axis=0)]
    all_gather x2 -> x1, waiting for transfers between devices: 92.6 us -> 0.02 us  [per_device(): wo_rows = lax.all_gather(wo_chip, 'z', axis=0)]
    another operation x11 -> x1, other arithmetic: 79.2 us -> 0.08 us  [per_device(): meta = jnp.stack([z, c]).astype(jnp.int32)]
    ppermute x31 -> x3, waiting for transfers between devices: 40.6 us -> 1.14 us  [swap(): return lax.ppermute(value, 'c', [(0, 1), (1, 0)])]
    dot_general x59 -> x3, matrix products: 26 us -> 6.24 us  [the longest x2 4.74 us: project(): jnp.einsum('tzcd,zcpde->pte', hid.reshape(half, w_all.shape[0], 2, HD), w...]
    all_to_all x0 -> x1, starting transfers between devices: none -> 7 us  [per_device(): wo_cols = lax.all_to_all(wo_rows, 'h', 0, 0)]
  transfers between devices with their start and end apart: 34 -> 5, of which waited for: 33 -> 1; matrix products, arithmetic and copies ran while one was open for 24% -> 7% of each run, Pallas kernels for 0% -> 3%
where the time goes in v1:
time: 184 us; the launch traced here: 183 us
  blocking collectives  103 us (56%)
  starting transfers between devices  39.3 us (21%)
  between operations  13.7 us (7%)
  local copies, waits for them, and re-layouts  10 us (5%)
  matrix products  6.24 us (3%)
  Pallas kernels  6.22 us (3%)
  other arithmetic  3.67 us (2%)
    all_gather x1, blocking collectives, per_device(): w_all = lax.all_gather(w_f16, 'z', axis=0)  52.9 us
    ppermute x3, starting transfers between devices, swap(): return lax.ppermute(value, 'c', [(0, 1), (1, 0)])  32.3 us
    all_gather x1, blocking collectives, per_device(): tl_all = lax.all_gather(tl.astype(F16), 'z', axis=0).astype(BF16)  28.4 us
    all_gather x1, blocking collectives, per_device(): normed_all = lax.all_gather(normed.astype(F16), 'h', axis=0).astype(BF16)  21.7 us
    all_to_all x1, starting transfers between devices, per_device(): wo_cols = lax.all_to_all(wo_rows, 'h', 0, 0)  7 us
    pallas_call x1, Pallas kernels, local_terms(): pl.pallas_call(local_kernel, out_shape=(jax.ShapeDtypeStruct((2 * HD, HD)...  5.24 us
    dot_general x2, matrix products, project(): jnp.einsum('tzcd,zcpde->pte', hid.reshape(half, w_all.shape[0], 2, HD), w...  4.74 us
    unnamed x11, local copies, waits for them, and re-layouts  4.23 us
  transfers between devices with their start and end apart: 5, of which 1 were waited for; matrix products, arithmetic and copies ran while one was open for 7% of the time, Pallas kernels for 3%

profile of v1, /device:TPU:1, one launch (start us, length us, event | category | flops | bytes accessed | tf_op | source)
XLA Modules:
  0.0 183.3 jit_solution(2001156439066870475)
XLA Ops:
  6.5 0.7 convert_element_type.57
  7.2 0.8 constant_dynamic-slice_fusion.3
  8.0 1.0 constant_dynamic-slice_fusion.5
  9.0 0.1 maximum_maximum_fusion
  9.2 8.9 %collective-permute-start = (bf16[528,128]{1,0:T(8,128)(2,1)S(1)}, bf16[528,128]{1,0:T(8,128)(2,1)S(1)}, u32[]{:S(2)}, u32[]{:S(2)}) collective-permute-start(bf16[528,128]{1,0:T(8,128)(2,1)S(1)} %maximum_maximum_fusion), channel_id=1, source_target_pairs={{0,16},{16,0},{1,17},{17,1},{2,18},{18,2},{3,19},{19,3},{4,20},{20... | collective-permute-start | bytes 405512 | tf_op jit(solution)/shard_map/ppermute | solution.py:204
  18.1 4.1 %copy.40 = bf16[256,4096]{0,1:T(8,128)(2,1)} copy(bf16[256,4096]{1,0:T(8,128)(2,1)} %param.5) | data formatting | bytes 4194304 | tf_op args[0]
  22.2 1.9 %collective-permute-start.1 = (bf16[256,4096]{0,1:T(8,128)(2,1)}, bf16[256,4096]{0,1:T(8,128)(2,1)}, u32[]{:S(2)}, u32[]{:S(2)}) collective-permute-start(bf16[256,4096]{0,1:T(8,128)(2,1)} %copy.40), channel_id=1, source_target_pairs={{0,16},{16,0},{1,17},{17,1},{2,18},{18,2},{3,19},{19,3},{4,20},{20... | collective-permute-start | bytes 6291464 | tf_op jit(solution)/shard_map/ppermute | solution.py:204
  24.2 2.7 %reshape.91 = bf16[256,16,2,128]{3,2,1,0:T(2,128)(2,1)} reshape(bf16[256,4096]{1,0:T(8,128)(2,1)S(1)} %copy-done.1) | data formatting | bytes 4194304 | tf_op jit(solution)/shard_map/reshape | solution.py:251
  27.3 0.1 copy.43.beta_ref
  27.5 0.6 pad_maximum_fusion
  28.2 52.9 %all-gather.9 = f16[16,2,3,128,128]{3,4,0,2,1:T(8,128)(2,1)S(1)} all-gather(f16[1,2,3,128,128]{3,4,0,2,1:T(8,128)(2,1)S(1)} %multiply_convert_fusion.15), channel_id=1, replica_groups=mesh['z'=16,'c'=2,'h'=16] {'z'}, dimensions={0}, use_global_device_ids=true | all-gather | bytes 3342336 | tf_op jit(solution)/shard_map/all_gather | solution.py:238
  81.2 1.8 %fusion.16.own_ref = bf16[3,256,128]{2,1,0:T(8,128)(2,1)S(1)} fusion(bf16[256,16,2,128,1]{3,2,1,0,4:T(2,128)(2,1)S(1)} %bitcast.46, f16[16,2,3,128,128]{3,4,0,2,1:T(8,128)(2,1)S(1)} %all-gather.9), kind=kOutput, calls=%fused_computation.10 | convolution fusion | flops 810123264 | bytes 5439488 | tf_op jit(solution)/shard_map/tzcd,zcpde->pte/dot_general | solution.py:249
  83.1 2.9 %fusion.19.sib_ref = bf16[3,256,128]{2,1,0:T(8,128)(2,1)S(1)} fusion(bf16[256,16,2,128,1]{0,3,2,1,4:T(8,128)(2,1)} %bitcast.11, f16[16,2,3,128,128]{3,4,0,2,1:T(8,128)(2,1)S(1)} %all-gather.9), kind=kOutput, calls=%fused_computation.11 | convolution fusion | flops 810123264 | bytes 5439488 | tf_op jit(solution)/shard_map/tzcd,zcpde->pte/dot_general | solution.py:249
  86.0 5.2 %shard_map.55 = (f32[256,128]{1,0:T(8,128)S(1)}, f32[2,512,128]{2,1,0:T(8,128)S(1)}) custom-call(s32[2]{0:T(128)S(1)} %pad_add_fusion.meta_ref, s32[9]{0:T(128)S(1)} %copy-done, bf16[3,256,128]{2,1,0:T(8,128)(2,1)S(1)} %fusion.16.own_ref, bf16[3,256,128]{2,1,0:T(8,128)(2,1)S(1)} %fusion.19.sib_ref, f32[512,1]{1,0:T(8,128)S(1)} %copy.43.beta_ref), custom_call_target="tpu_custom_call" | custom-call | tf_op jit(solution)/shard_map/pallas_call | solution.py:181
  91.3 7.0 %all-to-all-start = ((bf16[16,128,256]{2,1,0:T(8,128)(2,1)}), bf16[16,128,256]{2,1,0:T(8,128)(2,1)S(1)}, u32[]{:S(2)}, u32[]{:S(2)}) async-start(bf16[16,128,256]{2,1,0:T(8,128)(2,1)} %bitcast.48), calls=%async_computation | async-start | bytes 2097152 | tf_op jit(solution)/shard_map/all_to_all | solution.py:243
  98.3 28.4 %all-gather.10 = f16[4096,128]{1,0:T(8,128)(2,1)S(1)} all-gather(f16[256,128]{1,0:T(8,128)(2,1)S(1)} %convert_element_type.67), channel_id=2, replica_groups=mesh['z'=16,'c'=2,'h'=16] {'z'}, dimensions={0}, use_global_device_ids=true | all-gather | bytes 1114112 | tf_op jit(solution)/shard_map/all_gather | solution.py:257
  126.8 1.0 shard_map.56
  127.8 21.7 %all-gather.11 = f16[8192,128]{1,0:T(8,128)(2,1)S(1)} all-gather(f16[512,128]{1,0:T(8,128)(2,1)S(1)} %convert_element_type.69), channel_id=3, replica_groups=mesh['z'=16,'c'=2,'h'=16] {'h'}, dimensions={0}, use_global_device_ids=true | all-gather | bytes 2228224 | tf_op jit(solution)/shard_map/all_gather | solution.py:259
  149.5 0.2 convert_element_type.73
  149.7 1.5 convolution_bitcast_fusion
  151.2 1.0 constant_dynamic-slice_fusion
  152.2 21.5 %collective-permute-start.2 = (f32[256,256]{1,0:T(8,128)S(1)}, f32[256,256]{1,0:T(8,128)S(1)}, u32[]{:S(2)}, u32[]{:S(2)}) collective-permute-start(f32[256,256]{1,0:T(8,128)S(1)} %constant_dynamic-slice_fusion), channel_id=1, source_target_pairs={{0,16},{16,0},{1,17},{17,1},{2,18},{18,2},{3,19},{19,3},{4,20},{20... | collective-permute-start | bytes 786440 | tf_op jit(solution)/shard_map/ppermute | solution.py:204
  173.7 1.1 collective-permute-done.2
  174.8 1.6 add_convert_fusion
  (30 shorter events, 0.8 us)
Async XLA Ops:
  6.5 84.7 %all-gather.8.cloned.1.call-start = ((), (), s32[]{:S(2)}) async-start(), calls=%async_computation.1 | async-start | bytes 1114112 | tf_op jit(solution)/shard_map/all_gather | solution.py:242
  9.2 14.9 %copy-start.1 = (bf16[256,4096]{1,0:T(8,128)(2,1)S(1)}, bf16[256,4096]{1,0:T(8,128)(2,1)}, u32[]{:S(2)}) copy-start(bf16[256,4096]{1,0:T(8,128)(2,1)} %param.5) | copy-start | bytes 6291460
  9.2 17.9 %collective-permute-start = (bf16[528,128]{1,0:T(8,128)(2,1)S(1)}, bf16[528,128]{1,0:T(8,128)(2,1)S(1)}, u32[]{:S(2)}, u32[]{:S(2)}) collective-permute-start(bf16[528,128]{1,0:T(8,128)(2,1)S(1)} %maximum_maximum_fusion), channel_id=1, source_target_pairs={{0,16},{16,0},{1,17},{17,1},{2,18},{18,2},{3,19},{19,3},{4,20},{20... | collective-permute-start | bytes 405512 | tf_op jit(solution)/shard_map/ppermute | solution.py:204
  22.2 60.8 %collective-permute-start.1 = (bf16[256,4096]{0,1:T(8,128)(2,1)}, bf16[256,4096]{0,1:T(8,128)(2,1)}, u32[]{:S(2)}, u32[]{:S(2)}) collective-permute-start(bf16[256,4096]{0,1:T(8,128)(2,1)} %copy.40), channel_id=1, source_target_pairs={{0,16},{16,0},{1,17},{17,1},{2,18},{18,2},{3,19},{19,3},{4,20},{20... | collective-permute-start | bytes 6291464 | tf_op jit(solution)/shard_map/ppermute | solution.py:204
  24.1 3.3 %copy-start.3 = (bf16[256,128]{1,0:T(8,128)(2,1)S(1)}, bf16[256,128]{1,0:T(8,128)(2,1)}, u32[]{:S(2)}) copy-start(bf16[256,128]{1,0:T(8,128)(2,1)} %param.9) | copy-start | bytes 196612
  28.1 53.1 %copy-start.2 = (bf16[256,16,2,128]{3,2,1,0:T(2,128)(2,1)S(1)}, bf16[256,16,2,128]{3,2,1,0:T(2,128)(2,1)}, u32[]{:S(2)}) copy-start(bf16[256,16,2,128]{3,2,1,0:T(2,128)(2,1)} %reshape.91) | copy-start | bytes 6291460
  83.0 2.9 %copy-start = (s32[9]{0:T(128)S(1)}, s32[9]{0:T(128)}, u32[]{:S(2)}) copy-start(s32[9]{0:T(128)} %ds_ref.3) | copy-start | bytes 112
  91.3 58.4 %all-to-all-start = ((bf16[16,128,256]{2,1,0:T(8,128)(2,1)}), bf16[16,128,256]{2,1,0:T(8,128)(2,1)S(1)}, u32[]{:S(2)}, u32[]{:S(2)}) async-start(bf16[16,128,256]{2,1,0:T(8,128)(2,1)} %bitcast.48), calls=%async_computation | async-start | bytes 2097152 | tf_op jit(solution)/shard_map/all_to_all | solution.py:243
  152.2 22.6 %collective-permute-start.2 = (f32[256,256]{1,0:T(8,128)S(1)}, f32[256,256]{1,0:T(8,128)S(1)}, u32[]{:S(2)}, u32[]{:S(2)}) collective-permute-start(f32[256,256]{1,0:T(8,128)S(1)} %constant_dynamic-slice_fusion), channel_id=1, source_target_pairs={{0,16},{16,0},{1,17},{17,1},{2,18},{18,2},{3,19},{19,3},{4,20},{20... | collective-permute-start | bytes 786440 | tf_op jit(solution)/shard_map/ppermute | solution.py:204
Sparse Core Ops, SparseCore 0:
  28.3 62.1 all-gather.7

commit v2 on v1

v2 whole, which is shorter than its diff:
```python
import jax
import jax.numpy as jnp
from jax import lax
from jax.experimental import pallas as pl
from jax.experimental.pallas import tpu as pltpu
from jax.sharding import Mesh
from jax.sharding import PartitionSpec as P

F32 = jnp.float32
BF16 = jnp.bfloat16
F16 = jnp.float16
HD = 128
TOK = 512
W_SCALE = 2.0**19
N_SCALE = 2.0**12
NN = (((1,), (0,)), ((), ()))


def split(a):
    hi = a.astype(BF16)
    return hi, (a - hi.astype(F32)).astype(BF16)


def dot(a, b):
    return lax.dot_general(a, b, NN, preferred_element_type=F32)


def mm3s(a, b):
    (ah, al), (bh, bl) = a, b
    return dot(
        jnp.concatenate([ah, ah, al], axis=1), jnp.concatenate([bh, bl, bh], axis=0)
    )


def mm3(a, b):
    return mm3s(split(a), split(b))


def unit_rows(m):
    return m * lax.rsqrt(jnp.sum(m * m, axis=-1, keepdims=True) + 1e-06)


def count_le(ds_ref, pos):
    total = jnp.zeros(jnp.shape(pos), jnp.int32)
    for j in range(ds_ref.shape[0]):
        total = total + (ds_ref[j] <= pos).astype(jnp.int32)
    return total


def doc_info(meta_ref, ds_ref):
    pos0 = meta_ref[0] * TOK
    doc_col = count_le(ds_ref, pos0 + lax.broadcasted_iota(jnp.int32, (TOK, 1), 0))
    doc_row = count_le(ds_ref, pos0 + lax.broadcasted_iota(jnp.int32, (1, TOK), 1))
    return doc_col, doc_row, count_le(ds_ref, pos0 - 1), count_le(ds_ref, pos0 + TOK - 1)


def in_order(first, own, sib):
    return jnp.concatenate([jnp.where(first, own, sib), jnp.where(first, sib, own)], axis=0)


def part(pair, rows, cols):
    return pair[0][rows, cols], pair[1][rows, cols]


EVERY = slice(None)


def masked_gram(left, right_t, doc_col, doc_row, rows, cols, inclusive=False, scale=None):
    gram = mm3s(part(left, rows, EVERY), part(right_t, EVERY, cols))
    r = lax.broadcasted_iota(jnp.int32, gram.shape, 0) + rows.start
    c = lax.broadcasted_iota(jnp.int32, gram.shape, 1) + cols.start
    keep = (c <= r) if inclusive else (c < r)
    keep = keep & (doc_col[rows] == doc_row[:, cols])
    if scale is not None:
        gram = scale[rows] * gram
    return jnp.where(keep, gram, 0.0)


def pack_kernel(meta_ref, w_ref, wo_ref, codes_ref, give_ref, mine_ref):
    first = meta_ref[1] == 0

    def halves(x):
        left, right = x[:, :HD], x[:, HD:]
        return jnp.where(first, left, right), jnp.where(first, right, left)

    for p in range(3):
        mine, other = halves(w_ref[p].astype(F32))
        mine_ref[:, HD * p : HD * p + HD] = mine.astype(BF16)
        give_ref[:, HD * p : HD * p + HD] = other.astype(BF16)
    top, bottom = wo_ref[:HD].astype(F32), wo_ref[HD:].astype(F32)
    mine_ref[:, 3 * HD :] = jnp.where(first, top, bottom).astype(BF16)
    give_ref[:, 3 * HD : 4 * HD] = jnp.where(first, bottom, top).astype(BF16)
    codes = codes_ref[...].astype(F32)
    other = jnp.where(first, codes[:, 1:2], codes[:, 0:1])
    lane = lax.broadcasted_iota(jnp.int32, (HD, HD), 1)
    give_ref[:, 4 * HD :] = jnp.where(lane == 0, other[:HD], other[HD:]).astype(BF16)


def local_kernel(meta_ref, ds_ref, own_ref, sib_ref, codes_ref, got_ref, tl_ref, wu_ref, kt_ref):
    first = meta_ref[1] == 0
    half = TOK // 2
    kv = in_order(first, own_ref[...].astype(F32), sib_ref[...].astype(F32))
    key = unit_rows(kv[:, :HD])
    value = kv[:, HD:]
    codes = codes_ref[...].astype(F32)
    own_codes = jnp.where(first, codes[:, 0:1], codes[:, 1:2])
    got = got_ref[:, 4 * HD :].astype(F32)
    sib_codes = jnp.concatenate([got[:, 0:1], got[:, 1:2]], axis=0)
    beta = 1.6 + 0.1 * in_order(first, own_codes, sib_codes)
    doc_col, doc_row, prev_doc, last_doc = doc_info(meta_ref, ds_ref)
    carry_in = (doc_col == prev_doc).astype(F32)
    tail_row = (doc_row == last_doc).astype(F32)
    last_keep = (last_doc == prev_doc).astype(F32)

    key_s = split(key)
    key_t = jnp.transpose(key)
    kt_ref[...] = key_t
    key_ts = split(key_t)

    def system(rows, cols):
        return masked_gram(key_s, key_ts, doc_col, doc_row, rows, cols, scale=beta)

    quarter = [slice(128 * i, 128 * i + 128) for i in range(4)]
    rows128 = lax.broadcasted_iota(jnp.int32, (128, 128), 0)
    cols128 = lax.broadcasted_iota(jnp.int32, (128, 128), 1)
    eye128 = (rows128 == cols128).astype(F32)
    diag = [system(s, s) for s in quarter]
    inv = []
    for a in diag:
        m = ((rows128 >> 1) == (cols128 >> 1)) & (rows128 != cols128)
        inv.append(eye128 - jnp.where(m, a, 0.0))
    for lev in range(1, 7):
        m = ((rows128 >> (lev + 1)) == (cols128 >> (lev + 1))) & (
            (rows128 >> lev) != (cols128 >> lev)
        )
        xs = [split(x) for x in inv]
        ys = [mm3s(x, split(jnp.where(m, a, 0.0))) for x, a in zip(xs, diag)]
        inv = [x - mm3s(split(y), s) for x, y, s in zip(inv, ys, xs)]
    pair_inv = []
    for i in (0, 2):
        off = system(quarter[i + 1], quarter[i])
        low = -mm3(mm3(inv[i + 1], off), inv[i])
        top = jnp.concatenate([inv[i], jnp.zeros((128, 128), F32)], axis=1)
        bottom = jnp.concatenate([low, inv[i + 1]], axis=1)
        pair_inv.append(jnp.concatenate([top, bottom], axis=0))
    lo, hi = slice(0, half), slice(half, TOK)
    right = beta * jnp.concatenate([carry_in * key, value], axis=1)
    cross = system(hi, lo)
    wu_lo = mm3(pair_inv[0], right[lo])
    wu_lo_s = split(wu_lo)
    wu_hi = mm3(pair_inv[1], right[hi] - mm3s(split(cross), wu_lo_s))
    wu_hi_s = split(wu_hi)
    wu_ref[lo, :] = wu_lo
    wu_ref[hi, :] = wu_hi
    wu_s = tuple(jnp.concatenate([x, y], axis=0) for x, y in zip(wu_lo_s, wu_hi_s))
    tl = mm3s(split(tail_row * key_t), wu_s)
    tl_ref[0:HD, :] = (last_keep * eye128 - tl[:, :HD]).astype(BF16)
    tl_ref[HD:, :] = tl[:, HD:].astype(BF16)


def query_kernel(meta_ref, ds_ref, own_ref, sib_ref, kt_ref, wu_ref, b_ref):
    first = meta_ref[1] == 0
    half = TOK // 2
    query = unit_rows(in_order(first, own_ref[...].astype(F32), sib_ref[...].astype(F32)))
    doc_col, doc_row, prev_doc, _ = doc_info(meta_ref, ds_ref)
    carry_in = (doc_col == prev_doc).astype(F32)
    query_s = split(query)
    key_ts = split(kt_ref[...])
    wu_s = split(wu_ref[...])
    lo, hi = slice(0, half), slice(half, TOK)

    def probs(rows, cols):
        return masked_gram(query_s, key_ts, doc_col, doc_row, rows, cols, inclusive=True)

    out_lo = mm3s(split(probs(lo, lo)), part(wu_s, lo, EVERY))
    out_hi = mm3s(split(probs(hi, slice(0, TOK))), wu_s)
    b_ref[0, lo, :] = carry_in[lo] * query[lo] - out_lo[:, :HD]
    b_ref[0, hi, :] = carry_in[hi] * query[hi] - out_hi[:, :HD]
    b_ref[1, lo, :] = out_lo[:, HD:]
    b_ref[1, hi, :] = out_hi[:, HD:]


def apply_block(block, state):
    hi, lo = split(state)
    left = block[:HD]
    return dot(jnp.concatenate([left, left], axis=1), jnp.concatenate([hi, lo], axis=0))


def group_kernel(meta_ref, tl_ref, comp_ref, pre_ref):
    place = meta_ref[0] & 3
    eye = (
        lax.broadcasted_iota(jnp.int32, (HD, HD), 0)
        == lax.broadcasted_iota(jnp.int32, (HD, HD), 1)
    ).astype(F32)
    zero = jnp.zeros((HD, HD), F32)
    comp = jnp.concatenate([eye, zero], axis=1)
    pre = comp
    for j in range(4):
        pre = jnp.where(place == j, comp, pre)
        add = jnp.concatenate([zero, tl_ref[j, HD:].astype(F32)], axis=1)
        comp = apply_block(tl_ref[j], comp) + add
    pre_ref[...] = pre
    comp_b = jnp.concatenate([comp[:, :HD], comp[:, HD:]], axis=0).astype(BF16)
    for j in range(4):
        comp_ref[j] = comp_b


def finish_kernel(meta_ref, comp_ref, pre_ref, b_ref, out_ref):
    group = meta_ref[0] >> 2
    first = meta_ref[1] == 0
    half = TOK // 2
    state = jnp.zeros((HD, HD), F32)
    for j in range(3):
        new = apply_block(comp_ref[j], state) + comp_ref[j, HD:].astype(F32)
        state = jnp.where(j < group, new, state)
    state = mm3(pre_ref[:, :HD], state) + pre_ref[:, HD:]
    out = mm3(b_ref[0], state) + b_ref[1]
    out = out * lax.rsqrt(jnp.mean(out * out, axis=-1, keepdims=True) + 1e-05)
    low, high = out[:half], out[half:]
    out_ref[:half, :] = jnp.where(first, high, low).astype(BF16)
    out_ref[half:, :] = jnp.where(first, low, high).astype(BF16)


SMEM = pl.BlockSpec(memory_space=pltpu.SMEM)
VMEM = pl.BlockSpec(memory_space=pltpu.VMEM)


def call(kernel, scalars, arrays, outs, flops):
    return pl.pallas_call(
        kernel,
        out_shape=tuple(jax.ShapeDtypeStruct(s, d) for s, d in outs),
        in_specs=[SMEM] * len(scalars) + [VMEM] * len(arrays),
        out_specs=(VMEM,) * len(outs),
        compiler_params=pltpu.CompilerParams(vmem_limit_bytes=40 << 20),
        cost_estimate=pl.CostEstimate(flops=flops, bytes_accessed=1 << 20, transcendentals=0),
    )(*scalars, *arrays)


def swap(value):
    return lax.ppermute(value, "c", [(0, 1), (1, 0)])


def exchange(blocks, groups):
    return lax.all_to_all(blocks, "z", 0, 0, axis_index_groups=groups)


def per_device(hidden_in, w_qkv, doc_starts, beta_codes, w_out):
    z = lax.axis_index("z")
    c = lax.axis_index("c")
    first = c == 0
    chips = lax.axis_size("z")
    half, width = hidden_in.shape
    meta = jnp.stack([z, c]).astype(jnp.int32)
    near = [[4 * i + j for j in range(4)] for i in range(chips // 4)]
    far = [[4 * i + j for i in range(4)] for j in range(chips // 4)]

    give, mine = call(
        pack_kernel,
        (meta,),
        (w_qkv, w_out, beta_codes),
        [((HD, 5 * HD), BF16), ((HD, 4 * HD), BF16)],
        1 << 20,
    )
    got = swap(give)
    hidden_sib = swap(hidden_in)

    def ordered(a, b, axis=0):
        return jnp.concatenate([jnp.where(first, a, b), jnp.where(first, b, a)], axis=axis)

    w_chip = ordered(mine[:, : 3 * HD], got[:, : 3 * HD])
    w_f16 = (w_chip.astype(F32) * W_SCALE).astype(F16)
    w_all = lax.all_gather(w_f16, "z", axis=0, tiled=True)
    w_all = (w_all.astype(F32) * (1.0 / W_SCALE)).astype(BF16)

    wo_chip = ordered(mine[:, 3 * HD :], got[:, 3 * HD : 4 * HD], axis=1)
    wo_rows = lax.all_gather(wo_chip, "z", axis=0)
    wo_cols = lax.all_to_all(wo_rows, "h", 0, 0)

    def project(hid, cols):
        return jnp.dot(hid, w_all[:, cols], preferred_element_type=F32).astype(BF16)

    q_cols, kv_cols = slice(0, HD), slice(HD, 3 * HD)
    tl, wu, key_t = call(
        local_kernel,
        (meta, doc_starts),
        (project(hidden_in, kv_cols), project(hidden_sib, kv_cols), beta_codes, got),
        [((2 * HD, HD), BF16), ((TOK, 2 * HD), F32), ((HD, TOK), F32)],
        3 << 30,
    )
    near_all = exchange(jnp.broadcast_to(tl[None], (4, 2 * HD, HD)), near)
    comp, pre = call(
        group_kernel,
        (meta,),
        (near_all,),
        [((4, 2 * HD, HD), BF16), ((HD, 2 * HD), F32)],
        1 << 28,
    )
    far_all = exchange(comp, far)
    (b,) = call(
        query_kernel,
        (meta, doc_starts),
        (project(hidden_in, q_cols), project(hidden_sib, q_cols), key_t, wu),
        [((2, TOK, HD), F32)],
        3 << 30,
    )
    (normed,) = call(
        finish_kernel,
        (meta,),
        (far_all, pre, b),
        [((TOK, HD), BF16)],
        1 << 28,
    )
    normed = (normed.astype(F32) * N_SCALE).astype(F16)
    normed_all = lax.all_gather(normed, "h", axis=0)
    normed_all = (normed_all.astype(F32) * (1.0 / N_SCALE)).astype(BF16)

    def output(rows):
        return jnp.einsum("htf,hfn->tn", rows, wo_cols, preferred_element_type=F32)

    sent = swap(output(normed_all[:, :half]))
    return (output(normed_all[:, half:]) + sent).astype(BF16)


def solution(mesh):
    seq, head = mesh.devices.shape
    fine = Mesh(mesh.devices.reshape(seq // 2, 2, head), ("z", "c", "h"))
    tokens = ("z", "c")
    in_specs = (P(tokens, None), P(None, tokens, "h"), P(), P(tokens, "h"), P("h", tokens))
    return jax.shard_map(
        per_device, mesh=fine, in_specs=in_specs, out_specs=P(tokens, "h"), check_vma=False
    )
```

time: 184 us -> 200 us (1.087)
  waiting for transfers between devices: 1.18 us -> 36 us
  blocking collectives: 103 us -> 85.7 us
  local copies, waits for them, and re-layouts: 10 us -> 3.47 us
  Pallas kernels: 6.22 us -> 10.6 us
  matrix products: 6.24 us -> 9.14 us
  starting transfers between devices: 39.3 us -> 37.2 us
    all_gather x1, waiting for transfers between devices: 0.02 us -> 34.8 us  [per_device(): wo_rows = lax.all_gather(wo_chip, 'z', axis=0)]
    all_gather x3 -> x2, blocking collectives: 103 us -> 77.2 us  [the longest x1 48.5 us: per_device(): w_all = lax.all_gather(w_f16, 'z', axis=0, tiled=True)]
    ppermute x3, starting transfers between devices: 32.3 us -> 22 us  [swap(): return lax.ppermute(value, 'c', [(0, 1), (1, 0)])]
    all_to_all x0 -> x1, blocking collectives: none -> 8.47 us  [exchange(): return lax.all_to_all(blocks, 'z', 0, 0, axis_index_groups=groups)]
    all_to_all x0 -> x1, starting transfers between devices: none -> 8.09 us  [exchange(): return lax.all_to_all(blocks, 'z', 0, 0, axis_index_groups=groups)]
    pallas_call x2 -> x5, Pallas kernels: 6.22 us -> 10.6 us  [call(): pl.pallas_call(kernel, out_shape=tuple((jax.ShapeDtypeStruct(s, d) for s,...]
    dot_general x3 -> x6, matrix products: 6.24 us -> 9.14 us  [the longest x4 7.6 us: project(): return jnp.dot(hid, w_all[:, cols], preferred_element_type=F32).astype(BF16)]
    reshape x2 -> x0, local copies, waits for them, and re-layouts: 2.86 us -> none  [the longest x1 2.73 us: project(): hid.reshape(half, w_all.shape[0], 2, HD)]
  transfers between devices with their start and end apart: 5 -> 6, of which waited for: 1 -> 2; matrix products, arithmetic and copies ran while one was open for 7% -> 6% of each run, Pallas kernels for 3% -> 5%
where the time goes in v2:
time: 200 us
  blocking collectives  85.7 us (43%)
  starting transfers between devices  37.2 us (19%)
  waiting for transfers between devices  36 us (18%)
  between operations  13.6 us (7%)
  Pallas kernels  10.6 us (5%)
  matrix products  9.14 us (5%)
  other arithmetic  4.07 us (2%)
  local copies, waits for them, and re-layouts  3.47 us (2%)
    all_gather x1, blocking collectives, per_device(): w_all = lax.all_gather(w_f16, 'z', axis=0, tiled=True)  48.5 us
    all_gather x1, waiting for transfers between devices, per_device(): wo_rows = lax.all_gather(wo_chip, 'z', axis=0)  34.8 us
    all_gather x1, blocking collectives, per_device(): normed_all = lax.all_gather(normed, 'h', axis=0)  28.7 us
    ppermute x3, starting transfers between devices, swap(): return lax.ppermute(value, 'c', [(0, 1), (1, 0)])  22 us
    pallas_call x5, Pallas kernels, call(): pl.pallas_call(kernel, out_shape=tuple((jax.ShapeDtypeStruct(s, d) for s,...  10.6 us
    all_to_all x1, blocking collectives, exchange(): return lax.all_to_all(blocks, 'z', 0, 0, axis_index_groups=groups)  8.47 us
    all_to_all x1, starting transfers between devices, exchange(): return lax.all_to_all(blocks, 'z', 0, 0, axis_index_groups=groups)  8.09 us
    dot_general x4, matrix products, project(): return jnp.dot(hid, w_all[:, cols], preferred_element_type=F32).astype(BF16)  7.6 us
  transfers between devices with their start and end apart: 6, of which 2 were waited for; matrix products, arithmetic and copies ran while one was open for 6% of the time, Pallas kernels for 5%

profile of v2, /device:TPU:1, one launch (start us, length us, event | category | flops | bytes accessed | tf_op | source)
XLA Modules:
  0.0 199.7 jit_solution(15748909100268383339)
XLA Ops:
  6.5 0.8 copy.6.codes_ref
  7.4 0.9 copy-done
  8.4 0.8 copy-done.1
  9.9 8.8 %collective-permute-start = (bf16[128,640]{1,0:T(8,128)(2,1)S(1)}, bf16[128,640]{1,0:T(8,128)(2,1)S(1)}, u32[]{:S(2)}, u32[]{:S(2)}) collective-permute-start(bf16[128,640]{1,0:T(8,128)(2,1)S(1)} %get-tuple-element.13), channel_id=1, source_target_pairs={{0,16},{16,0},{1,17},{17,1},{2,18},{18,2},{3,19},{19,3},{4,20},{20... | collective-permute-start | bytes 491528 | tf_op jit(solution)/shard_map/ppermute | solution.py:240
  18.7 1.9 collective-permute-start.1
  20.7 48.5 %all-gather.7 = f16[4096,384]{1,0:T(8,128)(2,1)} all-gather(f16[256,384]{1,0:T(8,128)(2,1)S(1)} %multiply_convert_fusion.2), channel_id=1, replica_groups=mesh['z'=16,'c'=2,'h'=16] {'z'}, dimensions={0}, use_global_device_ids=true | all-gather | bytes 3342336 | tf_op jit(solution)/shard_map/all_gather | solution.py:272
  69.9 2.8 %multiply_convert_fusion = bf16[4096,384]{1,0:T(8,128)(2,1)S(1)} fusion(f16[4096,384]{1,0:T(8,128)(2,1)} %all-gather.7), kind=kLoop, calls=%fused_computation | loop fusion | flops 4718592 | bytes 6291456 | tf_op jit(solution)/shard_map/convert_element_type | solution.py:273
  72.7 0.8 fusion.12.own_ref
  73.5 0.8 copy-done.3
  74.3 2.3 %fusion.15.sib_ref = bf16[256,256]{1,0:T(8,128)(2,1)S(1)} fusion(bf16[256,4096]{1,0:T(8,128)(2,1)} %collective-permute-done.1, bf16[4096,384]{1,0:T(8,128)(2,1)S(1)} %multiply_convert_fusion), kind=kOutput, calls=%fused_computation.13 | convolution fusion | flops 536936448 | bytes 4325376 | tf_op jit(solution)/shard_map/dot_general | solution.py:280
  76.7 4.7 %shard_map.56 = (bf16[256,128]{1,0:T(8,128)(2,1)S(1)}, f32[512,256]{1,0:T(8,128)S(1)}, f32[128,512]{1,0:T(8,128)S(1)}) custom-call(s32[2]{0:T(128)S(1)} %pad_add_fusion.meta_ref, s32[9]{0:T(128)S(1)} %copy-done.2, bf16[256,256]{1,0:T(8,128)(2,1)S(1)} %fusion.12.own_ref, bf16[256,256]{1,0:T(8,128)(2,1)S(1)} %fusion.15.sib_ref, s32[256,2]{1,0:T(8,128)S(1)} %copy.6.codes_ref, ...), custom_call_target="tpu_custom_call" | custom-call | flops 3221225472 | bytes 1048576 | tf_op jit(solution)/shard_map/pallas_call | solution.py:229
  81.4 8.5 %all_to_all.15.tl_ref = bf16[4,256,128]{2,1,0:T(8,128)(2,1)S(1)} all-to-all(bf16[4,256,128]{2,1,0:T(8,128)(2,1)S(1)} %broadcast_in_dim.2), channel_id=1, replica_groups={{0,32,64,96},{128,160,192,224},{256,288,320,352},{384,416,448,480},{1,3..., dimensions={0} | all-to-all | bytes 524288 | tf_op jit(solution)/shard_map/all_to_all | solution.py:244
  89.9 1.9 shard_map.57
  91.8 8.1 %all-to-all-start.1 = ((bf16[4,256,128]{2,1,0:T(8,128)(2,1)}), bf16[4,256,128]{2,1,0:T(8,128)(2,1)S(1)}, u32[]{:S(2)}, u32[]{:S(2)}) async-start(bf16[4,256,128]{2,1,0:T(8,128)(2,1)} %get-tuple-element.15), calls=%async_computation.1 | async-start | bytes 524288 | tf_op jit(solution)/shard_map/all_to_all | solution.py:244
  99.9 2.0 fusion.18.own_ref
  101.9 2.6 %fusion.19.sib_ref = bf16[256,128]{1,0:T(8,128)(2,1)S(1)} fusion(bf16[256,4096]{1,0:T(8,128)(2,1)} %collective-permute-done.1, bf16[4096,384]{1,0:T(8,128)(2,1)} %copy-done.3), kind=kOutput, calls=%fused_computation.17 | convolution fusion | flops 268468224 | bytes 3211264 | tf_op jit(solution)/shard_map/dot_general | solution.py:280
  104.5 1.7 shard_map.58.b_ref
  106.2 34.8 %all-gather.6.cloned.1.call-done = bf16[2048,256]{1,0:T(8,128)(2,1)} async-done(((bf16[128,256]{1,0:T(8,128)(2,1)}), bf16[2048,256]{1,0:T(8,128)(2,1)}) %all-gather.6.cloned.1.call-update) | async-done | bytes 1048592 | tf_op jit(solution)/shard_map/all_gather | solution.py:276
  141.0 7.1 %all-to-all-start.2 = ((bf16[16,128,256]{2,1,0:T(8,128)(2,1)}), bf16[16,128,256]{2,1,0:T(8,128)(2,1)S(1)}, u32[]{:S(2)}, u32[]{:S(2)}) async-start(bf16[16,128,256]{2,1,0:T(8,128)(2,1)} %bitcast.28), calls=%async_computation.2 | async-start | bytes 2097152 | tf_op jit(solution)/shard_map/all_to_all | solution.py:277
  148.1 1.5 shard_map.59
  149.7 28.7 %all-gather.8 = f16[8192,128]{1,0:T(8,128)(2,1)S(1)} all-gather(f16[512,128]{1,0:T(8,128)(2,1)S(1)} %multiply_convert_fusion.3), channel_id=2, replica_groups=mesh['z'=16,'c'=2,'h'=16] {'h'}, dimensions={0}, use_global_device_ids=true | all-gather | bytes 2228224 | tf_op jit(solution)/shard_map/all_gather | solution.py:314
  179.4 11.2 %collective-permute-start.2 = (f32[256,256]{1,0:T(8,128)S(1)}, f32[256,256]{1,0:T(8,128)S(1)}, u32[]{:S(2)}, u32[]{:S(2)}) collective-permute-start(f32[256,256]{1,0:T(8,128)S(1)} %convolution_bitcast_fusion), channel_id=1, source_target_pairs={{0,16},{16,0},{1,17},{17,1},{2,18},{18,2},{3,19},{19,3},{4,20},{20... | collective-permute-start | bytes 786440 | tf_op jit(solution)/shard_map/ppermute | solution.py:240
  190.6 1.1 collective-permute-done.2
  191.8 1.1 fusion.5
  (23 shorter events, 2.5 us)
Async XLA Ops:
  6.5 134.5 %all-gather.6.cloned.1.call-start = ((), (), s32[]{:S(2)}) async-start(), calls=%async_computation.3 | async-start | bytes 1114112 | tf_op jit(solution)/shard_map/all_gather | solution.py:276
  7.4 0.9 copy-start
  8.4 0.8 copy-start.1
  9.9 10.7 %collective-permute-start = (bf16[128,640]{1,0:T(8,128)(2,1)S(1)}, bf16[128,640]{1,0:T(8,128)(2,1)S(1)}, u32[]{:S(2)}, u32[]{:S(2)}) collective-permute-start(bf16[128,640]{1,0:T(8,128)(2,1)S(1)} %get-tuple-element.13), channel_id=1, source_target_pairs={{0,16},{16,0},{1,17},{17,1},{2,18},{18,2},{3,19},{19,3},{4,20},{20... | collective-permute-start | bytes 491528 | tf_op jit(solution)/shard_map/ppermute | solution.py:240
  18.7 54.8 %collective-permute-start.1 = (bf16[256,4096]{1,0:T(8,128)(2,1)}, bf16[256,4096]{1,0:T(8,128)(2,1)}, u32[]{:S(2)}, u32[]{:S(2)}) collective-permute-start(bf16[256,4096]{1,0:T(8,128)(2,1)} %param.5), channel_id=1, source_target_pairs={{0,16},{16,0},{1,17},{17,1},{2,18},{18,2},{3,19},{19,3},{4,20},{20... | collective-permute-start | bytes 6291464 | tf_op jit(solution)/shard_map/ppermute | solution.py:240
  69.9 2.8 %copy-start.4 = (bf16[256,4096]{1,0:T(8,128)(2,1)S(1)}, bf16[256,4096]{1,0:T(8,128)(2,1)}, u32[]{:S(2)}) copy-start(bf16[256,4096]{1,0:T(8,128)(2,1)} %param.5) | copy-start | bytes 6291460
  72.7 1.6 copy-start.3
  73.4 3.2 %copy-start.2 = (s32[9]{0:T(128)S(1)}, s32[9]{0:T(128)}, u32[]{:S(2)}) copy-start(s32[9]{0:T(128)} %ds_ref.3) | copy-start | bytes 112
  91.8 49.2 %all-to-all-start.1 = ((bf16[4,256,128]{2,1,0:T(8,128)(2,1)}), bf16[4,256,128]{2,1,0:T(8,128)(2,1)S(1)}, u32[]{:S(2)}, u32[]{:S(2)}) async-start(bf16[4,256,128]{2,1,0:T(8,128)(2,1)} %get-tuple-element.15), calls=%async_computation.1 | async-start | bytes 524288 | tf_op jit(solution)/shard_map/all_to_all | solution.py:244
  141.0 37.9 %all-to-all-start.2 = ((bf16[16,128,256]{2,1,0:T(8,128)(2,1)}), bf16[16,128,256]{2,1,0:T(8,128)(2,1)S(1)}, u32[]{:S(2)}, u32[]{:S(2)}) async-start(bf16[16,128,256]{2,1,0:T(8,128)(2,1)} %bitcast.28), calls=%async_computation.2 | async-start | bytes 2097152 | tf_op jit(solution)/shard_map/all_to_all | solution.py:277
  179.4 12.4 %collective-permute-start.2 = (f32[256,256]{1,0:T(8,128)S(1)}, f32[256,256]{1,0:T(8,128)S(1)}, u32[]{:S(2)}, u32[]{:S(2)}) collective-permute-start(f32[256,256]{1,0:T(8,128)S(1)} %convolution_bitcast_fusion), channel_id=1, source_target_pairs={{0,16},{16,0},{1,17},{17,1},{2,18},{18,2},{3,19},{19,3},{4,20},{20... | collective-permute-start | bytes 786440 | tf_op jit(solution)/shard_map/ppermute | solution.py:240
Sparse Core Ops, SparseCore 0:
  70.0 70.9 all-gather.5

commit v3 on v2

--- a/solution.py
+++ b/solution.py
@@ -12,7 +12,6 @@
 HD = 128
 TOK = 512
 W_SCALE = 2.0**19
-N_SCALE = 2.0**12
 NN = (((1,), (0,)), ((), ()))
 
 
@@ -76,24 +75,18 @@
     return jnp.where(keep, gram, 0.0)
 
 
-def pack_kernel(meta_ref, w_ref, wo_ref, codes_ref, give_ref, mine_ref):
-    first = meta_ref[1] == 0
-
-    def halves(x):
-        left, right = x[:, :HD], x[:, HD:]
-        return jnp.where(first, left, right), jnp.where(first, right, left)
-
-    for p in range(3):
-        mine, other = halves(w_ref[p].astype(F32))
-        mine_ref[:, HD * p : HD * p + HD] = mine.astype(BF16)
-        give_ref[:, HD * p : HD * p + HD] = other.astype(BF16)
-    top, bottom = wo_ref[:HD].astype(F32), wo_ref[HD:].astype(F32)
-    mine_ref[:, 3 * HD :] = jnp.where(first, top, bottom).astype(BF16)
-    give_ref[:, 3 * HD : 4 * HD] = jnp.where(first, bottom, top).astype(BF16)
+def pack_kernel(meta_ref, w_ref, codes_ref, give_ref, mine_ref):
+    first = meta_ref[1] == 0
+    for place, p in enumerate((1, 2, 0)):
+        left = w_ref[p, :, :HD].astype(F32)
+        right = w_ref[p, :, HD:].astype(F32)
+        cols = slice(HD * place, HD * place + HD)
+        mine_ref[:, cols] = jnp.where(first, left, right).astype(BF16)
+        give_ref[:, cols] = jnp.where(first, right, left).astype(BF16)
     codes = codes_ref[...].astype(F32)
-    other = jnp.where(first, codes[:, 1:2], codes[:, 0:1])
-    lane = lax.broadcasted_iota(jnp.int32, (HD, HD), 1)
-    give_ref[:, 4 * HD :] = jnp.where(lane == 0, other[:HD], other[HD:]).astype(BF16)
+    other = jnp.where(first, codes[1:2], codes[0:1])
+    row = lax.broadcasted_iota(jnp.int32, (HD, HD), 0)
+    give_ref[:, 3 * HD :] = jnp.where(row == 0, other[:, :HD], other[:, HD:]).astype(BF16)
 
 
 def local_kernel(meta_ref, ds_ref, own_ref, sib_ref, codes_ref, got_ref, tl_ref, wu_ref, kt_ref):
@@ -103,10 +96,13 @@
     key = unit_rows(kv[:, :HD])
     value = kv[:, HD:]
     codes = codes_ref[...].astype(F32)
-    own_codes = jnp.where(first, codes[:, 0:1], codes[:, 1:2])
-    got = got_ref[:, 4 * HD :].astype(F32)
-    sib_codes = jnp.concatenate([got[:, 0:1], got[:, 1:2]], axis=0)
-    beta = 1.6 + 0.1 * in_order(first, own_codes, sib_codes)
+    own_codes = jnp.where(first, codes[0:1], codes[1:2])
+    got = got_ref[0:8, 3 * HD :].astype(F32)
+    sib_codes = jnp.concatenate([got[0:1], got[1:2]], axis=1)
+    codes = jnp.concatenate(
+        [jnp.where(first, own_codes, sib_codes), jnp.where(first, sib_codes, own_codes)], axis=1
+    )
+    beta = 1.6 + 0.1 * jnp.transpose(jnp.broadcast_to(codes, (8, TOK)))[:, 0:1]
     doc_col, doc_row, prev_doc, last_doc = doc_info(meta_ref, ds_ref)
     carry_in = (doc_col == prev_doc).astype(F32)
     tail_row = (doc_row == last_doc).astype(F32)
@@ -221,6 +217,20 @@
     out_ref[half:, :] = jnp.where(first, low, high).astype(BF16)
 
 
+def terms_kernel(meta_ref, own_ref, got_ref, own_w_ref, sib_w_ref, out_ref):
+    first = meta_ref[1] == 0
+    own = own_ref[TOK // 2 :].astype(F32)
+    got = got_ref[...].astype(F32)
+    rows = jnp.concatenate(
+        [jnp.where(first, own, got), jnp.where(first, got, own)], axis=1
+    ).astype(BF16)
+    for j in range(own_w_ref.shape[0]):
+        mine = dot(rows, own_w_ref[j])
+        other = dot(rows, sib_w_ref[j])
+        out_ref[j, :, :HD] = jnp.where(first, mine, other).astype(BF16)
+        out_ref[j, :, HD:] = jnp.where(first, other, mine).astype(BF16)
+
+
 SMEM = pl.BlockSpec(memory_space=pltpu.SMEM)
 VMEM = pl.BlockSpec(memory_space=pltpu.VMEM)
 
@@ -231,7 +241,7 @@
         out_shape=tuple(jax.ShapeDtypeStruct(s, d) for s, d in outs),
         in_specs=[SMEM] * len(scalars) + [VMEM] * len(arrays),
         out_specs=(VMEM,) * len(outs),
-        compiler_params=pltpu.CompilerParams(vmem_limit_bytes=40 << 20),
+        compiler_params=pltpu.CompilerParams(vmem_limit_bytes=16 << 20),
         cost_estimate=pl.CostEstimate(flops=flops, bytes_accessed=1 << 20, transcendentals=0),
     )(*scalars, *arrays)
 
@@ -254,36 +264,35 @@
     near = [[4 * i + j for j in range(4)] for i in range(chips // 4)]
     far = [[4 * i + j for i in range(4)] for j in range(chips // 4)]
 
+    codes = beta_codes.T
     give, mine = call(
         pack_kernel,
         (meta,),
-        (w_qkv, w_out, beta_codes),
-        [((HD, 5 * HD), BF16), ((HD, 4 * HD), BF16)],
+        (w_qkv, codes),
+        [((HD, 4 * HD), BF16), ((HD, 3 * HD), BF16)],
         1 << 20,
     )
     got = swap(give)
     hidden_sib = swap(hidden_in)
 
-    def ordered(a, b, axis=0):
-        return jnp.concatenate([jnp.where(first, a, b), jnp.where(first, b, a)], axis=axis)
-
-    w_chip = ordered(mine[:, : 3 * HD], got[:, : 3 * HD])
-    w_f16 = (w_chip.astype(F32) * W_SCALE).astype(F16)
-    w_all = lax.all_gather(w_f16, "z", axis=0, tiled=True)
-    w_all = (w_all.astype(F32) * (1.0 / W_SCALE)).astype(BF16)
-
-    wo_chip = ordered(mine[:, 3 * HD :], got[:, 3 * HD : 4 * HD], axis=1)
-    wo_rows = lax.all_gather(wo_chip, "z", axis=0)
-    wo_cols = lax.all_to_all(wo_rows, "h", 0, 0)
-
-    def project(hid, cols):
-        return jnp.dot(hid, w_all[:, cols], preferred_element_type=F32).astype(BF16)
-
-    q_cols, kv_cols = slice(0, HD), slice(HD, 3 * HD)
+    def chip(cols):
+        a, b = mine[:, cols], got[:, cols]
+        return jnp.concatenate([jnp.where(first, a, b), jnp.where(first, b, a)], axis=0)
+
+    kv_f16 = (chip(slice(0, 2 * HD)).astype(F32) * W_SCALE).astype(F16)
+    qo = jnp.concatenate([chip(slice(2 * HD, 3 * HD)), w_out], axis=1)
+    kv_f16, qo = lax.optimization_barrier((kv_f16, qo))
+    qo_all = lax.all_gather(qo, "z", axis=0, tiled=True)
+    kv_all = lax.all_gather(kv_f16, "z", axis=0, tiled=True)
+    kv_all = (kv_all.astype(F32) * (1.0 / W_SCALE)).astype(BF16)
+
+    def project(hid, weights):
+        return jnp.dot(hid, weights, preferred_element_type=F32).astype(BF16)
+
     tl, wu, key_t = call(
         local_kernel,
         (meta, doc_starts),
-        (project(hidden_in, kv_cols), project(hidden_sib, kv_cols), beta_codes, got),
+        (project(hidden_in, kv_all), project(hidden_sib, kv_all), codes, got),
         [((2 * HD, HD), BF16), ((TOK, 2 * HD), F32), ((HD, TOK), F32)],
         3 << 30,
     )
@@ -296,10 +305,14 @@
         1 << 28,
     )
     far_all = exchange(comp, far)
+    qo_all, _ = lax.optimization_barrier((qo_all, comp))
+    q_all = qo_all[:, :HD]
+    wo_own = qo_all[:, HD:].reshape(chips, 2 * HD, HD)
+    wo_sib = swap(wo_own)
     (b,) = call(
         query_kernel,
         (meta, doc_starts),
-        (project(hidden_in, q_cols), project(hidden_sib, q_cols), key_t, wu),
+        (project(hidden_in, q_all), project(hidden_sib, q_all), key_t, wu),
         [((2, TOK, HD), F32)],
         3 << 30,
     )
@@ -310,15 +323,15 @@
         [((TOK, HD), BF16)],
         1 << 28,
     )
-    normed = (normed.astype(F32) * N_SCALE).astype(F16)
-    normed_all = lax.all_gather(normed, "h", axis=0)
-    normed_all = (normed_all.astype(F32) * (1.0 / N_SCALE)).astype(BF16)
-
-    def output(rows):
-        return jnp.einsum("htf,hfn->tn", rows, wo_cols, preferred_element_type=F32)
-
-    sent = swap(output(normed_all[:, :half]))
-    return (output(normed_all[:, half:]) + sent).astype(BF16)
+    (terms,) = call(
+        terms_kernel,
+        (meta,),
+        (normed, swap(normed[:half]), wo_own, wo_sib),
+        [((chips, half, 2 * HD), BF16)],
+        1 << 29,
+    )
+    shares = lax.all_to_all(terms, "h", 0, 0)
+    return jnp.sum(shares.astype(F32), axis=0).astype(BF16)
 
 
 def solution(mesh):

time: 200 us -> 177 us (0.89)
  waiting for transfers between devices: 36 us -> 11.2 us
  blocking collectives: 85.7 us -> 93.4 us
  starting transfers between devices: 37.2 us -> 32.1 us
  matrix products: 9.14 us -> 6.57 us
    all_to_all x0 -> x1, blocking collectives: none -> 35.5 us  [per_device(): shares = lax.all_to_all(terms, 'h', 0, 0)]
    all_gather x1, waiting for transfers between devices: 34.8 us -> 0.01 us  [per_device(): qo_all = lax.all_gather(qo, 'z', axis=0, tiled=True)]
    all_gather x2 -> x1, blocking collectives: 77.2 us -> 48.1 us  [per_device(): kv_all = lax.all_gather(kv_f16, 'z', axis=0, tiled=True)]
    all_to_all x1, waiting for transfers between devices: 0.01 us -> 9.31 us  [exchange(): return lax.all_to_all(blocks, 'z', 0, 0, axis_index_groups=groups)]
    all_to_all x1 -> x0, starting transfers between devices: 7.11 us -> none  [per_device(): wo_cols = lax.all_to_all(wo_rows, 'h', 0, 0)]
    ppermute x3 -> x4, starting transfers between devices: 22 us -> 26.6 us  [swap(): return lax.ppermute(value, 'c', [(0, 1), (1, 0)])]
    convert_element_type x4 -> x1, other arithmetic: 3.32 us -> 0.03 us  [per_device(): kv_f16 = (chip(slice(0, 2 * HD)).astype(F32) * W_SCALE).astype(F16)]
    all_to_all x1, starting transfers between devices: 8.09 us -> 5.51 us  [exchange(): return lax.all_to_all(blocks, 'z', 0, 0, axis_index_groups=groups)]
  transfers between devices with their start and end apart: 6 -> 6, of which waited for: 2 -> 3; matrix products, arithmetic and copies ran while one was open for 6% -> 4% of each run, Pallas kernels for 5% -> 6%
where the time goes in v3:
time: 177 us; the launch traced here: 176 us
  blocking collectives  93.4 us (53%)
  starting transfers between devices  32.1 us (18%)
  between operations  13.6 us (8%)
  Pallas kernels  12.3 us (7%)
  waiting for transfers between devices  11.2 us (6%)
  matrix products  6.57 us (4%)
  local copies, waits for them, and re-layouts  4.22 us (2%)
  other arithmetic  2.61 us (1%)
    all_gather x1, blocking collectives, per_device(): kv_all = lax.all_gather(kv_f16, 'z', axis=0, tiled=True)  48.1 us
    all_to_all x1, blocking collectives, per_device(): shares = lax.all_to_all(terms, 'h', 0, 0)  35.5 us
    ppermute x4, starting transfers between devices, swap(): return lax.ppermute(value, 'c', [(0, 1), (1, 0)])  26.6 us
    pallas_call x6, Pallas kernels, call(): pl.pallas_call(kernel, out_shape=tuple((jax.ShapeDtypeStruct(s, d) for s,...  12.3 us
    all_to_all x1, blocking collectives, exchange(): return lax.all_to_all(blocks, 'z', 0, 0, axis_index_groups=groups)  9.86 us
    all_to_all x1, waiting for transfers between devices, exchange(): return lax.all_to_all(blocks, 'z', 0, 0, axis_index_groups=groups)  9.31 us
    dot_general x4, matrix products, project(): return jnp.dot(hid, weights, preferred_element_type=F32).astype(BF16)  6.57 us
    all_to_all x1, starting transfers between devices, exchange(): return lax.all_to_all(blocks, 'z', 0, 0, axis_index_groups=groups)  5.51 us
  transfers between devices with their start and end apart: 6, of which 3 were waited for; matrix products, arithmetic and copies ran while one was open for 4% of the time, Pallas kernels for 6%

profile of v3, /device:TPU:1, one launch (start us, length us, event | category | flops | bytes accessed | tf_op | source)
XLA Modules:
  0.0 176.0 jit_solution(18193004781901592148)
XLA Ops:
  6.6 0.9 copy-done
  8.8 8.9 %collective-permute-start = (bf16[128,512]{1,0:T(8,128)(2,1)S(1)}, bf16[128,512]{1,0:T(8,128)(2,1)S(1)}, u32[]{:S(2)}, u32[]{:S(2)}) collective-permute-start(bf16[128,512]{1,0:T(8,128)(2,1)S(1)} %get-tuple-element.16), channel_id=1, source_target_pairs={{0,16},{16,0},{1,17},{17,1},{2,18},{18,2},{3,19},{19,3},{4,20},{20... | collective-permute-start | bytes 393224 | tf_op jit(solution)/shard_map/ppermute | solution.py:250
  17.8 1.0 collective-permute-done.got_ref
  18.8 1.5 pad_maximum_fusion
  20.3 2.3 %collective-permute-start.1 = (bf16[256,4096]{1,0:T(8,128)(2,1)}, bf16[256,4096]{1,0:T(8,128)(2,1)S(1)}, u32[]{:S(2)}, u32[]{:S(2)}) collective-permute-start(bf16[256,4096]{1,0:T(8,128)(2,1)} %param.5), channel_id=1, source_target_pairs={{0,16},{16,0},{1,17},{17,1},{2,18},{18,2},{3,19},{19,3},{4,20},{20... | collective-permute-start | bytes 6291464 | tf_op jit(solution)/shard_map/ppermute | solution.py:250
  22.6 48.1 %all-gather.4 = f16[4096,256]{1,0:T(8,128)(2,1)S(1)} all-gather(f16[256,256]{1,0:T(8,128)(2,1)S(1)} %multiply_convert_fusion.11), channel_id=1, replica_groups=mesh['z'=16,'c'=2,'h'=16] {'z'}, dimensions={0}, use_global_device_ids=true | all-gather | bytes 2228224 | tf_op jit(solution)/shard_map/all_gather | solution.py:286
  70.7 0.8 fusion.4.own_ref
  71.5 0.8 fusion.5.sib_ref
  72.8 4.7 %shard_map.56 = (bf16[256,128]{1,0:T(8,128)(2,1)S(1)}, f32[512,256]{1,0:T(8,128)S(1)}, f32[128,512]{1,0:T(8,128)S(1)}) custom-call(s32[2]{0:T(128)S(1)} %pad_add_fusion.meta_ref, s32[9]{0:T(128)S(1)} %copy-done.3, bf16[256,256]{1,0:T(8,128)(2,1)S(1)} %fusion.4.own_ref, bf16[256,256]{1,0:T(8,128)(2,1)S(1)} %fusion.5.sib_ref, s32[2,256]{1,0:T(2,128)S(1)} %bitcast.19, ...), custom_call_target="tpu_custom_call" | custom-call | flops 3221225472 | bytes 1048576 | tf_op jit(solution)/shard_map/pallas_call | solution.py:239
  78.3 9.9 %all_to_all.15.tl_ref = bf16[4,256,128]{2,1,0:T(8,128)(2,1)S(1)} all-to-all(bf16[4,256,128]{2,1,0:T(8,128)(2,1)S(1)} %broadcast_in_dim.2), channel_id=1, replica_groups={{0,32,64,96},{128,160,192,224},{256,288,320,352},{384,416,448,480},{1,3..., dimensions={0} | all-to-all | bytes 524288 | tf_op jit(solution)/shard_map/all_to_all | solution.py:254
  88.2 2.0 %shard_map.57 = (bf16[4,256,128]{2,1,0:T(8,128)(2,1)}, f32[128,256]{1,0:T(8,128)S(1)}) custom-call(s32[2]{0:T(128)S(1)} %pad_add_fusion.meta_ref, bf16[4,256,128]{2,1,0:T(8,128)(2,1)S(1)} %all_to_all.15.tl_ref), custom_call_target="tpu_custom_call" | custom-call | flops 268435456 | bytes 1048576 | tf_op jit(solution)/shard_map/pallas_call | solution.py:239
  90.1 1.3 slice.27
  91.4 10.2 %collective-permute-start.3 = (bf16[16,256,128]{2,1,0:T(8,128)(2,1)S(1)}, bf16[16,256,128]{2,1,0:T(8,128)(2,1)S(1)}, u32[]{:S(2)}, u32[]{:S(2)}) collective-permute-start(bf16[16,256,128]{2,1,0:T(8,128)(2,1)S(1)} %bitcast.16), channel_id=1, source_target_pairs={{0,16},{16,0},{1,17},{17,1},{2,18},{18,2},{3,19},{19,3},{4,20},{20... | collective-permute-start | bytes 3145736 | tf_op jit(solution)/shard_map/ppermute | solution.py:250
  101.6 5.5 %all-to-all-start.1 = ((bf16[4,256,128]{2,1,0:T(8,128)(2,1)}), bf16[4,256,128]{2,1,0:T(8,128)(2,1)S(1)}, u32[]{:S(2)}, u32[]{:S(2)}) async-start(bf16[4,256,128]{2,1,0:T(8,128)(2,1)} %get-tuple-element.19), calls=%async_computation.1 | async-start | bytes 524288 | tf_op jit(solution)/shard_map/all_to_all | solution.py:254
  107.1 2.7 %fusion.6.own_ref = bf16[256,128]{1,0:T(8,128)(2,1)S(1)} fusion(bf16[256,4096]{1,0:T(8,128)(2,1)} %param.5, bf16[4096,256]{1,0:T(8,128)(2,1)} %all-gather.3.cloned.1.call-done), kind=kOutput, calls=%fused_computation.9 | convolution fusion | flops 268468224 | bytes 3211264 | tf_op jit(solution)/shard_map/dot_general | solution.py:290
  109.8 2.3 %fusion.7.sib_ref = bf16[256,128]{1,0:T(8,128)(2,1)S(1)} fusion(bf16[256,4096]{1,0:T(8,128)(2,1)} %copy-done.8, bf16[4096,256]{1,0:T(8,128)(2,1)S(1)} %copy-done.6), kind=kOutput, calls=%fused_computation.10 | convolution fusion | flops 268468224 | bytes 3211264 | tf_op jit(solution)/shard_map/dot_general | solution.py:290
  112.2 1.7 shard_map.58.b_ref
  113.9 9.3 %all-to-all-done.1.comp_ref = bf16[4,256,128]{2,1,0:T(8,128)(2,1)S(1)} async-done(((bf16[4,256,128]{2,1,0:T(8,128)(2,1)}), bf16[4,256,128]{2,1,0:T(8,128)(2,1)S(1)}, u32[]{:S(2)}, u32[]{:S(2)}) %all-to-all-start.1) | async-done | bytes 262176 | tf_op jit(solution)/shard_map/all_to_all | solution.py:254
  123.3 1.5 shard_map.59.own_ref
  124.8 5.2 %collective-permute-start.2 = (bf16[256,128]{1,0:T(8,128)(2,1)S(1)}, bf16[256,128]{1,0:T(8,128)(2,1)S(1)}, u32[]{:S(2)}, u32[]{:S(2)}) collective-permute-start(bf16[256,128]{1,0:T(8,128)(2,1)S(1)} %slice.30), channel_id=1, source_target_pairs={{0,16},{16,0},{1,17},{17,1},{2,18},{18,2},{3,19},{19,3},{4,20},{20... | collective-permute-start | bytes 196616 | tf_op jit(solution)/shard_map/ppermute | solution.py:250
  130.1 0.9 collective-permute-done.2.got_ref
  130.9 1.8 %shard_map.60 = bf16[16,256,256]{2,1,0:T(8,128)(2,1)S(1)} custom-call(s32[2]{0:T(128)S(1)} %pad_add_fusion.meta_ref, bf16[512,128]{1,0:T(8,128)(2,1)S(1)} %shard_map.59.own_ref, bf16[256,128]{1,0:T(8,128)(2,1)S(1)} %collective-permute-done.2.got_ref, bf16[16,256,128]{2,1,0:T(8,128)(2,1)S(1)} %bitcast.17, ...), custom_call_target="tpu_custom_call" | custom-call | flops 536870912 | bytes 1048576 | tf_op jit(solution)/shard_map/pallas_call | solution.py:239
  132.7 35.5 %all_to_all.16 = bf16[16,256,256]{2,1,0:T(8,128)(2,1)S(1)} all-to-all(bf16[16,256,256]{2,1,0:T(8,128)(2,1)S(1)} %shard_map.60), channel_id=1, replica_groups=mesh['z'=16,'c'=2,'h'=16] {'h'}, dimensions={0} | all-to-all | bytes 4194304 | tf_op jit(solution)/shard_map/all_to_all | solution.py:333
  168.2 1.0 reduce_sum.12
  (29 shorter events, 2.8 us)
Async XLA Ops:
  6.5 83.6 %all-gather.3.cloned.1.call-start = ((), (), s32[]{:S(2)}) async-start(), calls=%async_computation.3 | async-start | bytes 2228224 | tf_op jit(solution)/shard_map/all_gather | solution.py:285
  6.6 0.9 copy-start
  7.5 0.7 copy-start.1
  8.2 62.4 %copy-start.7 = (bf16[256,4096]{1,0:T(8,128)(2,1)S(1)}, bf16[256,4096]{1,0:T(8,128)(2,1)}, u32[]{:S(2)}) copy-start(bf16[256,4096]{1,0:T(8,128)(2,1)} %param.5) | copy-start | bytes 6291460
  8.8 9.9 %collective-permute-start = (bf16[128,512]{1,0:T(8,128)(2,1)S(1)}, bf16[128,512]{1,0:T(8,128)(2,1)S(1)}, u32[]{:S(2)}, u32[]{:S(2)}) collective-permute-start(bf16[128,512]{1,0:T(8,128)(2,1)S(1)} %get-tuple-element.16), channel_id=1, source_target_pairs={{0,16},{16,0},{1,17},{17,1},{2,18},{18,2},{3,19},{19,3},{4,20},{20... | collective-permute-start | bytes 393224 | tf_op jit(solution)/shard_map/ppermute | solution.py:250
  20.3 51.2 %collective-permute-start.1 = (bf16[256,4096]{1,0:T(8,128)(2,1)}, bf16[256,4096]{1,0:T(8,128)(2,1)S(1)}, u32[]{:S(2)}, u32[]{:S(2)}) collective-permute-start(bf16[256,4096]{1,0:T(8,128)(2,1)} %param.5), channel_id=1, source_target_pairs={{0,16},{16,0},{1,17},{17,1},{2,18},{18,2},{3,19},{19,3},{4,20},{20... | collective-permute-start | bytes 6291464 | tf_op jit(solution)/shard_map/ppermute | solution.py:250
  71.5 1.3 copy-start.2
  71.5 1.3 copy-start.3
  71.5 1.3 copy-start.8
  77.5 0.7 copy-start.4
  91.4 39.5 %collective-permute-start.3 = (bf16[16,256,128]{2,1,0:T(8,128)(2,1)S(1)}, bf16[16,256,128]{2,1,0:T(8,128)(2,1)S(1)}, u32[]{:S(2)}, u32[]{:S(2)}) collective-permute-start(bf16[16,256,128]{2,1,0:T(8,128)(2,1)S(1)} %bitcast.16), channel_id=1, source_target_pairs={{0,16},{16,0},{1,17},{17,1},{2,18},{18,2},{3,19},{19,3},{4,20},{20... | collective-permute-start | bytes 3145736 | tf_op jit(solution)/shard_map/ppermute | solution.py:250
  101.6 21.7 %all-to-all-start.1 = ((bf16[4,256,128]{2,1,0:T(8,128)(2,1)}), bf16[4,256,128]{2,1,0:T(8,128)(2,1)S(1)}, u32[]{:S(2)}, u32[]{:S(2)}) async-start(bf16[4,256,128]{2,1,0:T(8,128)(2,1)} %get-tuple-element.19), calls=%async_computation.1 | async-start | bytes 524288 | tf_op jit(solution)/shard_map/all_to_all | solution.py:254
  107.1 2.7 %copy-start.6 = (bf16[4096,256]{1,0:T(8,128)(2,1)S(1)}, bf16[4096,256]{1,0:T(8,128)(2,1)}, u32[]{:S(2)}) copy-start(bf16[4096,256]{1,0:T(8,128)(2,1)} %all-gather.3.cloned.1.call-done) | copy-start | bytes 6291460
  109.8 2.4 %copy-start.5 = (f32[128,512]{1,0:T(8,128)S(1)}, f32[128,512]{1,0:T(8,128)}, u32[]{:S(2)}) copy-start(f32[128,512]{1,0:T(8,128)} %copy-done.4) | copy-start | bytes 786436
  124.8 6.1 %collective-permute-start.2 = (bf16[256,128]{1,0:T(8,128)(2,1)S(1)}, bf16[256,128]{1,0:T(8,128)(2,1)S(1)}, u32[]{:S(2)}, u32[]{:S(2)}) collective-permute-start(bf16[256,128]{1,0:T(8,128)(2,1)S(1)} %slice.30), channel_id=1, source_target_pairs={{0,16},{16,0},{1,17},{17,1},{2,18},{18,2},{3,19},{19,3},{4,20},{20... | collective-permute-start | bytes 196616 | tf_op jit(solution)/shard_map/ppermute | solution.py:250
Sparse Core Ops, SparseCore 0:
  20.4 66.2 all-gather.2

commit v4 on v2

v4 whole, which is shorter than its diff:
```python
import jax
import jax.numpy as jnp
from jax import lax
from jax.experimental import pallas as pl
from jax.experimental.pallas import tpu as pltpu
from jax.sharding import Mesh
from jax.sharding import PartitionSpec as P

F32 = jnp.float32
BF16 = jnp.bfloat16
F16 = jnp.float16
HD = 128
TOK = 512
W_SCALE = 2.0**19
WO_SCALE = 2.0**18
L_SCALE = 2.0**-6
N_SCALE = 2.0**12
NN = (((1,), (0,)), ((), ()))


def split(a):
    hi = a.astype(BF16)
    return hi, (a - hi.astype(F32)).astype(BF16)


def dot(a, b):
    return lax.dot_general(a, b, NN, preferred_element_type=F32)


def mm3s(a, b):
    (ah, al), (bh, bl) = a, b
    return dot(
        jnp.concatenate([ah, ah, al], axis=1), jnp.concatenate([bh, bl, bh], axis=0)
    )


def mm3(a, b):
    return mm3s(split(a), split(b))


def unit_rows(m):
    return m * lax.rsqrt(jnp.sum(m * m, axis=-1, keepdims=True) + 1e-06)


def count_le(ds_ref, pos):
    total = jnp.zeros(jnp.shape(pos), jnp.int32)
    for j in range(ds_ref.shape[0]):
        total = total + (ds_ref[j] <= pos).astype(jnp.int32)
    return total


def doc_info(meta_ref, ds_ref):
    pos0 = meta_ref[0] * TOK
    doc_col = count_le(ds_ref, pos0 + lax.broadcasted_iota(jnp.int32, (TOK, 1), 0))
    doc_row = count_le(ds_ref, pos0 + lax.broadcasted_iota(jnp.int32, (1, TOK), 1))
    return doc_col, doc_row, count_le(ds_ref, pos0 - 1), count_le(ds_ref, pos0 + TOK - 1)


def in_order(first, own, sib):
    return jnp.concatenate([jnp.where(first, own, sib), jnp.where(first, sib, own)], axis=0)


def part(pair, rows, cols):
    return pair[0][rows, cols], pair[1][rows, cols]


EVERY = slice(None)


def masked_gram(left, right_t, doc_col, doc_row, rows, cols, inclusive=False, scale=None):
    gram = mm3s(part(left, rows, EVERY), part(right_t, EVERY, cols))
    r = lax.broadcasted_iota(jnp.int32, gram.shape, 0) + rows.start
    c = lax.broadcasted_iota(jnp.int32, gram.shape, 1) + cols.start
    keep = (c <= r) if inclusive else (c < r)
    keep = keep & (doc_col[rows] == doc_row[:, cols])
    if scale is not None:
        gram = scale[rows] * gram
    return jnp.where(keep, gram, 0.0)


def pack_kernel(meta_ref, w_ref, wo_ref, codes_ref, give_ref, mine_ref):
    first = meta_ref[1] == 0

    def put(place, mine, other):
        cols = slice(HD * place, HD * place + HD)
        mine_ref[:, cols] = jnp.where(first, mine, other).astype(BF16)
        give_ref[:, cols] = jnp.where(first, other, mine).astype(BF16)

    for p in range(3):
        put(p, w_ref[p, :, :HD].astype(F32), w_ref[p, :, HD:].astype(F32))
    put(3, wo_ref[:HD].astype(F32), wo_ref[HD:].astype(F32))
    codes = codes_ref[...].astype(F32)
    other = jnp.where(first, codes[1:2], codes[0:1])
    row = lax.broadcasted_iota(jnp.int32, (HD, HD), 0)
    give_ref[:, 4 * HD :] = jnp.where(row == 0, other[:, :HD], other[:, HD:]).astype(BF16)


def local_kernel(meta_ref, ds_ref, own_ref, sib_ref, codes_ref, got_ref, tl_ref, b_ref):
    first = meta_ref[1] == 0
    half = TOK // 2
    qkv = in_order(first, own_ref[...].astype(F32), sib_ref[...].astype(F32))
    query = unit_rows(qkv[:, :HD])
    key = unit_rows(qkv[:, HD : 2 * HD])
    value = qkv[:, 2 * HD :]
    codes = codes_ref[...].astype(F32)
    own_codes = jnp.where(first, codes[0:1], codes[1:2])
    got = got_ref[0:8, 4 * HD :].astype(F32)
    sib_codes = jnp.concatenate([got[0:1], got[1:2]], axis=1)
    codes = jnp.concatenate(
        [jnp.where(first, own_codes, sib_codes), jnp.where(first, sib_codes, own_codes)], axis=1
    )
    beta = 1.6 + 0.1 * jnp.transpose(jnp.broadcast_to(codes, (8, TOK)))[:, 0:1]
    doc_col, doc_row, prev_doc, last_doc = doc_info(meta_ref, ds_ref)
    carry_in = (doc_col == prev_doc).astype(F32)
    tail_row = (doc_row == last_doc).astype(F32)
    last_keep = (last_doc == prev_doc).astype(F32)

    key_s = split(key)
    key_t = jnp.transpose(key)
    key_ts = split(key_t)

    def system(rows, cols):
        return masked_gram(key_s, key_ts, doc_col, doc_row, rows, cols, scale=beta)

    quarter = [slice(128 * i, 128 * i + 128) for i in range(4)]
    rows128 = lax.broadcasted_iota(jnp.int32, (128, 128), 0)
    cols128 = lax.broadcasted_iota(jnp.int32, (128, 128), 1)
    eye128 = (rows128 == cols128).astype(F32)
    diag = [system(s, s) for s in quarter]
    inv = []
    for a in diag:
        m = ((rows128 >> 1) == (cols128 >> 1)) & (rows128 != cols128)
        inv.append(eye128 - jnp.where(m, a, 0.0))
    for lev in range(1, 7):
        m = ((rows128 >> (lev + 1)) == (cols128 >> (lev + 1))) & (
            (rows128 >> lev) != (cols128 >> lev)
        )
        xs = [split(x) for x in inv]
        ys = [mm3s(x, split(jnp.where(m, a, 0.0))) for x, a in zip(xs, diag)]
        inv = [x - mm3s(split(y), s) for x, y, s in zip(inv, ys, xs)]
    pair_inv = []
    for i in (0, 2):
        off = system(quarter[i + 1], quarter[i])
        low = -mm3(mm3(inv[i + 1], off), inv[i])
        top = jnp.concatenate([inv[i], jnp.zeros((128, 128), F32)], axis=1)
        bottom = jnp.concatenate([low, inv[i + 1]], axis=1)
        pair_inv.append(jnp.concatenate([top, bottom], axis=0))
    lo, hi = slice(0, half), slice(half, TOK)
    right = beta * jnp.concatenate([carry_in * key, value], axis=1)
    cross = system(hi, lo)
    wu_lo = mm3(pair_inv[0], right[lo])
    wu_lo_s = split(wu_lo)
    wu_hi = mm3(pair_inv[1], right[hi] - mm3s(split(cross), wu_lo_s))
    wu_hi_s = split(wu_hi)
    wu_s = tuple(jnp.concatenate([x, y], axis=0) for x, y in zip(wu_lo_s, wu_hi_s))
    tl = mm3s(split(tail_row * key_t), wu_s)
    tl_ref[:, :HD] = last_keep * eye128 - tl[:, :HD]
    tl_ref[:, HD:] = tl[:, HD:] * L_SCALE

    query_s = split(query)

    def probs(rows, cols):
        return masked_gram(query_s, key_ts, doc_col, doc_row, rows, cols, inclusive=True)

    out_lo = mm3s(split(probs(lo, lo)), part(wu_s, lo, EVERY))
    out_hi = mm3s(split(probs(hi, slice(0, TOK))), wu_s)
    b_ref[0, lo, :] = carry_in[lo] * query[lo] - out_lo[:, :HD]
    b_ref[0, hi, :] = carry_in[hi] * query[hi] - out_hi[:, :HD]
    b_ref[1, lo, :] = out_lo[:, HD:]
    b_ref[1, hi, :] = out_hi[:, HD:]


def finish_kernel(meta_ref, ds_ref, tl_ref, b_ref, out_ref):
    here = meta_ref[0]
    first = meta_ref[1] == 0
    half = TOK // 2
    start = jnp.int32(0)
    for j in range(ds_ref.shape[0]):
        pos = ds_ref[j]
        start = jnp.where(pos < here * TOK, jnp.maximum(start, pos // TOK), start)

    def fold(j, state):
        block = tl_ref[j]
        hi, lo = split(state)
        left = block[:, :HD]
        add = block[:, HD:].astype(F32) * (1.0 / L_SCALE)
        return dot(jnp.concatenate([left, left], axis=1), jnp.concatenate([hi, lo], axis=0)) + add

    state = lax.fori_loop(start, here, fold, jnp.zeros((HD, HD), F32))
    out = mm3(b_ref[0], state) + b_ref[1]
    out = out * lax.rsqrt(jnp.mean(out * out, axis=-1, keepdims=True) + 1e-05)
    low, high = out[:half], out[half:]
    out_ref[:half, :] = jnp.where(first, high, low).astype(BF16)
    out_ref[half:, :] = jnp.where(first, low, high).astype(BF16)


SMEM = pl.BlockSpec(memory_space=pltpu.SMEM)
VMEM = pl.BlockSpec(memory_space=pltpu.VMEM)


def call(kernel, scalars, arrays, outs, flops):
    return pl.pallas_call(
        kernel,
        out_shape=tuple(jax.ShapeDtypeStruct(s, d) for s, d in outs),
        in_specs=[SMEM] * len(scalars) + [VMEM] * len(arrays),
        out_specs=(VMEM,) * len(outs),
        compiler_params=pltpu.CompilerParams(vmem_limit_bytes=16 << 20),
        cost_estimate=pl.CostEstimate(flops=flops, bytes_accessed=1 << 20, transcendentals=0),
    )(*scalars, *arrays)


def swap(value):
    return lax.ppermute(value, "c", [(0, 1), (1, 0)])


def to_f16(value, scale):
    return (value.astype(F32) * scale).astype(F16)


def from_f16(value, scale):
    return (value.astype(F32) * (1.0 / scale)).astype(BF16)


def per_device(hidden_in, w_qkv, doc_starts, beta_codes, w_out):
    z = lax.axis_index("z")
    c = lax.axis_index("c")
    first = c == 0
    chips = lax.axis_size("z")
    heads = lax.axis_size("h")
    half = hidden_in.shape[0]
    meta = jnp.stack([z, c]).astype(jnp.int32)
    codes = beta_codes.T

    give, mine = call(
        pack_kernel,
        (meta,),
        (w_qkv, w_out, codes),
        [((HD, 5 * HD), BF16), ((HD, 4 * HD), BF16)],
        1 << 20,
    )
    got = swap(give)
    hidden_sib = swap(hidden_in)

    def chip(cols, axis):
        a, b = mine[:, cols], got[:, cols]
        return jnp.concatenate([jnp.where(first, a, b), jnp.where(first, b, a)], axis=axis)

    w_all = lax.all_gather(to_f16(chip(slice(0, 3 * HD), 0), W_SCALE), "z", axis=0, tiled=True)
    w_all = from_f16(w_all, W_SCALE)
    turned = [(i * heads + j, j * heads + i) for i in range(chips) for j in range(heads)]
    wo = lax.ppermute(chip(slice(3 * HD, 4 * HD), 1), ("z", "h"), turned)

    def project(hid):
        return jnp.dot(hid, w_all, preferred_element_type=F32).astype(BF16)

    tl, b = call(
        local_kernel,
        (meta, doc_starts),
        (project(hidden_in), project(hidden_sib), codes, got),
        [((HD, 2 * HD), F32), ((2, TOK, HD), F32)],
        3 << 30,
    )
    both = jnp.concatenate([tl.astype(F16), to_f16(wo, WO_SCALE)], axis=0)
    both = lax.all_gather(both, "z", axis=0)
    (normed,) = call(
        finish_kernel,
        (meta, doc_starts),
        (both[:, :HD].astype(BF16), b),
        [((TOK, HD), BF16)],
        1 << 28,
    )
    normed_all = from_f16(lax.all_gather(to_f16(normed, N_SCALE), "h", axis=0), N_SCALE)
    wo_cols = from_f16(both[:, HD:], WO_SCALE)

    def output(rows):
        return jnp.einsum("htf,hfn->tn", rows, wo_cols, preferred_element_type=F32)

    sent = swap(output(normed_all[:, :half]))
    return (output(normed_all[:, half:]) + sent).astype(BF16)


def solution(mesh):
    seq, head = mesh.devices.shape
    fine = Mesh(mesh.devices.reshape(seq // 2, 2, head), ("z", "c", "h"))
    tokens = ("z", "c")
    in_specs = (P(tokens, None), P(None, tokens, "h"), P(), P(tokens, "h"), P("h", tokens))
    return jax.shard_map(
        per_device, mesh=fine, in_specs=in_specs, out_specs=P(tokens, "h"), check_vma=False
    )
```

time: 200 us -> 164 us (0.82)
  waiting for transfers between devices: 36 us -> 1.15 us
  blocking collectives: 85.7 us -> 117 us
  between operations: 13.6 us -> 0.22 us
  starting transfers between devices: 37.2 us -> 30.5 us
  matrix products: 9.14 us -> 4.1 us
  Pallas kernels: 10.6 us -> 6.97 us
  other arithmetic: 4.07 us -> 0.96 us
    all_gather x2 -> x3, blocking collectives: 77.2 us -> 117 us  [the longest x1 58.8 us: per_device(): lax.all_gather(to_f16(chip(slice(0, 3 * HD), 0), W_SCALE), 'z', axis=0, t...]
    all_gather x1 -> x0, waiting for transfers between devices: 34.8 us -> none  [per_device(): wo_rows = lax.all_gather(wo_chip, 'z', axis=0)]
    all_to_all x2 -> x0, starting transfers between devices: 15.2 us -> none  [the longest x1 8.09 us: exchange(): return lax.all_to_all(blocks, 'z', 0, 0, axis_index_groups=groups)]
    all_to_all x1 -> x0, blocking collectives: 8.47 us -> none  [exchange(): return lax.all_to_all(blocks, 'z', 0, 0, axis_index_groups=groups)]
    ppermute x3, starting transfers between devices: 22 us -> 29.7 us  [swap(): return lax.ppermute(value, 'c', [(0, 1), (1, 0)])]
    dot_general x4 -> x2, matrix products: 7.6 us -> 2.54 us  [project(): return jnp.dot(hid, w_all, preferred_element_type=F32).astype(BF16)]
    pallas_call x5 -> x3, Pallas kernels: 10.6 us -> 6.97 us  [call(): pl.pallas_call(kernel, out_shape=tuple((jax.ShapeDtypeStruct(s, d) for s,...]
    convert_element_type x4 -> x6, other arithmetic: 3.32 us -> 0.8 us  [the longest x1 0.47 us: from_f16(): return (value.astype(F32) * (1.0 / scale)).astype(BF16)]
  transfers between devices with their start and end apart: 6 -> 4, of which waited for: 2 -> 1; matrix products, arithmetic and copies ran while one was open for 6% -> 1% of each run, Pallas kernels for 5% -> 0%
where the time goes in v4:
time: 164 us; the launch traced here: 163 us
  blocking collectives  117 us (71%)
  starting transfers between devices  30.5 us (19%)
  Pallas kernels  6.97 us (4%)
  matrix products  4.1 us (2%)
  local copies, waits for them, and re-layouts  2.47 us (2%)
    all_gather x1, blocking collectives, per_device(): lax.all_gather(to_f16(chip(slice(0, 3 * HD), 0), W_SCALE), 'z', axis=0, t...  58.8 us
    all_gather x1, blocking collectives, per_device(): both = lax.all_gather(both, 'z', axis=0)  34 us
    ppermute x3, starting transfers between devices, swap(): return lax.ppermute(value, 'c', [(0, 1), (1, 0)])  29.7 us
    all_gather x1, blocking collectives, per_device(): lax.all_gather(to_f16(normed, N_SCALE), 'h', axis=0)  24.3 us
    pallas_call x3, Pallas kernels, call(): pl.pallas_call(kernel, out_shape=tuple((jax.ShapeDtypeStruct(s, d) for s,...  6.97 us
  transfers between devices with their start and end apart: 4, of which 1 were waited for; matrix products, arithmetic and copies ran while one was open for 1% of the time, Pallas kernels for 0%

profile of v4, /device:TPU:1, one launch (start us, length us, event | category | flops | bytes accessed | tf_op | source)
XLA Modules:
  0.0 163.5 jit_solution(12776096926173574878)
XLA Ops:
  0.0 0.1 pad_add_fusion.meta_ref
  0.1 0.9 copy-done
  1.0 0.8 copy-done.1
  1.8 0.7 copy-done.2
  2.5 0.6 shard_map.55
  3.1 8.8 %collective-permute-start = (bf16[128,640]{1,0:T(8,128)(2,1)S(1)}, bf16[128,640]{1,0:T(8,128)(2,1)S(1)}, u32[]{:S(2)}, u32[]{:S(2)}) collective-permute-start(bf16[128,640]{1,0:T(8,128)(2,1)S(1)} %get-tuple-element.10), channel_id=1, source_target_pairs={{0,16},{16,0},{1,17},{17,1},{2,18},{18,2},{3,19},{19,3},{4,20},{20... | collective-permute-start | bytes 491528 | tf_op jit(solution)/shard_map/ppermute | solution.py:213
  11.9 1.9 %collective-permute-start.1 = (bf16[256,4096]{1,0:T(8,128)(2,1)}, bf16[256,4096]{1,0:T(8,128)(2,1)S(1)}, u32[]{:S(2)}, u32[]{:S(2)}) collective-permute-start(bf16[256,4096]{1,0:T(8,128)(2,1)} %param.5), channel_id=1, source_target_pairs={{0,16},{16,0},{1,17},{17,1},{2,18},{18,2},{3,19},{19,3},{4,20},{20... | collective-permute-start | bytes 6291464 | tf_op jit(solution)/shard_map/ppermute | solution.py:213
  13.9 0.0 copy-start.5
  13.9 0.8 collective-permute-start.2
  14.8 0.1 multiply_convert_fusion.15
  14.8 58.8 %all-gather.5 = f16[4096,384]{1,0:T(8,128)(2,1)S(1)} all-gather(f16[256,384]{1,0:T(8,128)(2,1)S(1)} %multiply_convert_fusion.15), channel_id=1, replica_groups=mesh['z'=16,'c'=2,'h'=16] {'z'}, dimensions={0}, use_global_device_ids=true | all-gather | bytes 3342336 | tf_op jit(solution)/shard_map/all_gather | solution.py:248
  73.6 1.3 fusion.6.own_ref
  74.9 0.0 copy-start.3
  75.0 1.3 fusion.7.sib_ref
  76.3 5.4 %shard_map.56 = (f32[128,256]{1,0:T(8,128)S(1)}, f32[2,512,128]{2,1,0:T(8,128)S(1)}) custom-call(s32[2]{0:T(128)S(1)} %pad_add_fusion.meta_ref, s32[9]{0:T(128)S(1)} %copy-done.4, bf16[256,384]{1,0:T(8,128)(2,1)S(1)} %fusion.6.own_ref, bf16[256,384]{1,0:T(8,128)(2,1)S(1)} %fusion.7.sib_ref, s32[2,256]{1,0:T(2,128)S(1)} %bitcast.20, ...), custom_call_target="tpu_custom_call" | custom-call | flops 3221225472 | bytes 1048576 | tf_op jit(solution)/shard_map/pallas_call | solution.py:202
  81.7 34.0 %all-gather.6 = f16[4096,256]{1,0:T(8,128)(2,1)S(1)} all-gather(f16[256,256]{1,0:T(8,128)(2,1)S(1)} %pad_maximum_fusion), channel_id=2, replica_groups=mesh['z'=16,'c'=2,'h'=16] {'z'}, dimensions={0}, use_global_device_ids=true | all-gather | bytes 2228224 | tf_op jit(solution)/shard_map/all_gather | solution.py:264
  115.7 0.2 slice_convert_fusion.tl_ref
  115.9 1.0 shard_map.57
  117.0 24.3 %all-gather.7 = f16[8192,128]{1,0:T(8,128)(2,1)S(1)} all-gather(f16[512,128]{1,0:T(8,128)(2,1)S(1)} %multiply_convert_fusion.16), channel_id=3, replica_groups=mesh['z'=16,'c'=2,'h'=16] {'h'}, dimensions={0}, use_global_device_ids=true | all-gather | bytes 2228224 | tf_op jit(solution)/shard_map/all_gather | solution.py:272
  141.3 0.5 multiply_convert_fusion.1
  141.7 0.5 convolution_bitcast_fusion
  142.2 19.0 %collective-permute-start.3 = (f32[256,256]{1,0:T(8,128)S(1)}, f32[256,256]{1,0:T(8,128)S(1)}, u32[]{:S(2)}, u32[]{:S(2)}) collective-permute-start(f32[256,256]{1,0:T(8,128)S(1)} %convolution_bitcast_fusion), channel_id=1, source_target_pairs={{0,16},{16,0},{1,17},{17,1},{2,18},{18,2},{3,19},{19,3},{4,20},{20... | collective-permute-start | bytes 786440 | tf_op jit(solution)/shard_map/ppermute | solution.py:213
  161.2 1.1 collective-permute-done.3
  162.3 1.1 fusion.5
  (17 shorter events, 0.2 us)
Async XLA Ops:
  0.1 0.9 copy-start
  1.0 0.8 copy-start.1
  1.8 0.7 copy-start.2
  3.1 10.7 %collective-permute-start = (bf16[128,640]{1,0:T(8,128)(2,1)S(1)}, bf16[128,640]{1,0:T(8,128)(2,1)S(1)}, u32[]{:S(2)}, u32[]{:S(2)}) collective-permute-start(bf16[128,640]{1,0:T(8,128)(2,1)S(1)} %get-tuple-element.10), channel_id=1, source_target_pairs={{0,16},{16,0},{1,17},{17,1},{2,18},{18,2},{3,19},{19,3},{4,20},{20... | collective-permute-start | bytes 491528 | tf_op jit(solution)/shard_map/ppermute | solution.py:213
  11.9 63.0 %collective-permute-start.1 = (bf16[256,4096]{1,0:T(8,128)(2,1)}, bf16[256,4096]{1,0:T(8,128)(2,1)S(1)}, u32[]{:S(2)}, u32[]{:S(2)}) collective-permute-start(bf16[256,4096]{1,0:T(8,128)(2,1)} %param.5), channel_id=1, source_target_pairs={{0,16},{16,0},{1,17},{17,1},{2,18},{18,2},{3,19},{19,3},{4,20},{20... | collective-permute-start | bytes 6291464 | tf_op jit(solution)/shard_map/ppermute | solution.py:213
  13.9 59.7 %copy-start.5 = (bf16[256,4096]{1,0:T(8,128)(2,1)S(1)}, bf16[256,4096]{1,0:T(8,128)(2,1)}, u32[]{:S(2)}) copy-start(bf16[256,4096]{1,0:T(8,128)(2,1)} %param.5) | copy-start | bytes 6291460
  13.9 61.0 %collective-permute-start.2 = (bf16[128,256]{1,0:T(8,128)(2,1)S(1)}, bf16[128,256]{1,0:T(8,128)(2,1)S(1)}, u32[]{:S(2)}, u32[]{:S(2)}) collective-permute-start(bf16[128,256]{1,0:T(8,128)(2,1)S(1)} %pad_maximum_fusion.1), channel_id=1, source_target_pairs={{0,0},{1,32},{2,64},{3,96},{4,128},{5,160},{6,192},{7,224},{8,256}... | collective-permute-start | bytes 196616 | tf_op jit(solution)/shard_map/ppermute | solution.py:251
  74.9 1.3 copy-start.3
  74.9 1.3 copy-start.4
  142.2 20.1 %collective-permute-start.3 = (f32[256,256]{1,0:T(8,128)S(1)}, f32[256,256]{1,0:T(8,128)S(1)}, u32[]{:S(2)}, u32[]{:S(2)}) collective-permute-start(f32[256,256]{1,0:T(8,128)S(1)} %convolution_bitcast_fusion), channel_id=1, source_target_pairs={{0,16},{16,0},{1,17},{17,1},{2,18},{18,2},{3,19},{19,3},{4,20},{20... | collective-permute-start | bytes 786440 | tf_op jit(solution)/shard_map/ppermute | solution.py:213

commit v5 on v4

--- a/solution.py
+++ b/solution.py
@@ -13,7 +13,6 @@
 TOK = 512
 W_SCALE = 2.0**19
 WO_SCALE = 2.0**18
-L_SCALE = 2.0**-6
 N_SCALE = 2.0**12
 NN = (((1,), (0,)), ((), ()))
 
@@ -95,7 +94,9 @@
     give_ref[:, 4 * HD :] = jnp.where(row == 0, other[:, :HD], other[:, HD:]).astype(BF16)
 
 
-def local_kernel(meta_ref, ds_ref, own_ref, sib_ref, codes_ref, got_ref, tl_ref, b_ref):
+def local_kernel(
+    meta_ref, ds_ref, own_ref, sib_ref, codes_ref, got_ref, tl_ref, tl16_ref, b_ref
+):
     first = meta_ref[1] == 0
     half = TOK // 2
     qkv = in_order(first, own_ref[...].astype(F32), sib_ref[...].astype(F32))
@@ -155,7 +156,8 @@
     wu_s = tuple(jnp.concatenate([x, y], axis=0) for x, y in zip(wu_lo_s, wu_hi_s))
     tl = mm3s(split(tail_row * key_t), wu_s)
     tl_ref[:, :HD] = last_keep * eye128 - tl[:, :HD]
-    tl_ref[:, HD:] = tl[:, HD:] * L_SCALE
+    tl_ref[:, HD:] = tl[:, HD:]
+    tl16_ref[...] = tl_ref[...].astype(BF16)
 
     query_s = split(query)
 
@@ -170,23 +172,28 @@
     b_ref[1, hi, :] = out_hi[:, HD:]
 
 
-def finish_kernel(meta_ref, ds_ref, tl_ref, b_ref, out_ref):
-    here = meta_ref[0]
+def after(later, earlier):
+    product = mm3(later[:, :HD], earlier)
+    return jnp.concatenate([product[:, :HD], product[:, HD:] + later[:, HD:]], axis=1)
+
+
+def pair_kernel(tl_ref, one_ref, two_ref):
+    two_ref[...] = after(tl_ref[...], one_ref[...].astype(F32)).astype(BF16)
+
+
+def window_kernel(tl_ref, one_ref, two_ref, pre_ref, four_t_ref, four_l_ref):
+    pre = after(one_ref[...].astype(F32), two_ref[...].astype(F32))
+    pre_ref[...] = pre
+    four = after(tl_ref[...], pre).astype(BF16)
+    four_t_ref[...] = four[:, :HD]
+    four_l_ref[...] = four[:, HD:]
+
+
+def finish_kernel(meta_ref, pre_ref, four_ref, extra_ref, b_ref, out_ref):
     first = meta_ref[1] == 0
     half = TOK // 2
-    start = jnp.int32(0)
-    for j in range(ds_ref.shape[0]):
-        pos = ds_ref[j]
-        start = jnp.where(pos < here * TOK, jnp.maximum(start, pos // TOK), start)
-
-    def fold(j, state):
-        block = tl_ref[j]
-        hi, lo = split(state)
-        left = block[:, :HD]
-        add = block[:, HD:].astype(F32) * (1.0 / L_SCALE)
-        return dot(jnp.concatenate([left, left], axis=1), jnp.concatenate([hi, lo], axis=0)) + add
-
-    state = lax.fori_loop(start, here, fold, jnp.zeros((HD, HD), F32))
+    state = four_ref[...].astype(F32) + extra_ref[...]
+    state = mm3(pre_ref[:, :HD], state) + pre_ref[:, HD:]
     out = mm3(b_ref[0], state) + b_ref[1]
     out = out * lax.rsqrt(jnp.mean(out * out, axis=-1, keepdims=True) + 1e-05)
     low, high = out[:half], out[half:]
@@ -213,6 +220,11 @@
     return lax.ppermute(value, "c", [(0, 1), (1, 0)])
 
 
+def ahead(value, steps):
+    chips = lax.axis_size("z")
+    return lax.ppermute(value, "z", [(i, i + steps) for i in range(chips - steps)])
+
+
 def to_f16(value, scale):
     return (value.astype(F32) * scale).astype(F16)
 
@@ -245,32 +257,59 @@
         a, b = mine[:, cols], got[:, cols]
         return jnp.concatenate([jnp.where(first, a, b), jnp.where(first, b, a)], axis=axis)
 
-    w_all = lax.all_gather(to_f16(chip(slice(0, 3 * HD), 0), W_SCALE), "z", axis=0, tiled=True)
-    w_all = from_f16(w_all, W_SCALE)
     turned = [(i * heads + j, j * heads + i) for i in range(chips) for j in range(heads)]
     wo = lax.ppermute(chip(slice(3 * HD, 4 * HD), 1), ("z", "h"), turned)
+    wo = jnp.concatenate([wo[:, :HD], wo[:, HD:]], axis=0)
+    both = jnp.concatenate(
+        [to_f16(chip(slice(0, 3 * HD), 0), W_SCALE), to_f16(wo, WO_SCALE)], axis=1
+    )
+    both = lax.all_gather(both, "z", axis=0, tiled=True)
+    w_all = from_f16(both[:, : 3 * HD], W_SCALE)
 
     def project(hid):
         return jnp.dot(hid, w_all, preferred_element_type=F32).astype(BF16)
 
-    tl, b = call(
+    tl, tl16, b = call(
         local_kernel,
         (meta, doc_starts),
         (project(hidden_in), project(hidden_sib), codes, got),
-        [((HD, 2 * HD), F32), ((2, TOK, HD), F32)],
+        [((HD, 2 * HD), F32), ((HD, 2 * HD), BF16), ((2, TOK, HD), F32)],
         3 << 30,
     )
-    both = jnp.concatenate([tl.astype(F16), to_f16(wo, WO_SCALE)], axis=0)
-    both = lax.all_gather(both, "z", axis=0)
+    one = ahead(tl16, 1)
+    (two,) = call(pair_kernel, (), (tl, one), [((HD, 2 * HD), BF16)], 1 << 26)
+    two = ahead(two, 2)
+    pre, four_t, four_l = call(
+        window_kernel,
+        (),
+        (tl, one, two),
+        [((HD, 2 * HD), F32), ((HD, HD), BF16), ((HD, HD), BF16)],
+        1 << 26,
+    )
+
+    here = jnp.arange(chips, dtype=jnp.int32)[:, None]
+    starts = doc_starts[None, :]
+    since = jnp.max(jnp.where(starts < here * TOK, starts // TOK, 0), axis=1)
+    reach_back = jnp.any(here[:, 0] - since > 7)
+
+    def fetch_far(t, add):
+        eight_t, eight_l, twelve = ahead(t, 8), ahead(add, 8), ahead(add, 12)
+        state = jnp.dot(eight_t, twelve, preferred_element_type=F32) + eight_l.astype(F32)
+        return jnp.dot(ahead(t, 4).astype(F32), state, precision=lax.Precision.HIGHEST)
+
+    extra = lax.cond(
+        reach_back, fetch_far, lambda t, add: jnp.zeros((HD, HD), F32), four_t, four_l
+    )
     (normed,) = call(
         finish_kernel,
-        (meta, doc_starts),
-        (both[:, :HD].astype(BF16), b),
+        (meta,),
+        (pre, ahead(four_l, 4), extra, b),
         [((TOK, HD), BF16)],
         1 << 28,
     )
     normed_all = from_f16(lax.all_gather(to_f16(normed, N_SCALE), "h", axis=0), N_SCALE)
-    wo_cols = from_f16(both[:, HD:], WO_SCALE)
+    wo_cols = from_f16(both[:, 3 * HD :], WO_SCALE).reshape(chips, 2, HD, HD)
+    wo_cols = wo_cols.transpose(0, 2, 1, 3).reshape(chips, HD, 2 * HD)
 
     def output(rows):
         return jnp.einsum("htf,hfn->tn", rows, wo_cols, preferred_element_type=F32)

time: 164 us -> 164 us (level)
  blocking collectives: 117 us -> 95.1 us
  starting transfers between devices: 30.5 us -> 45.2 us
  other arithmetic: 0.96 us -> 3.73 us
    all_gather x2 -> x1, blocking collectives: 92.8 us -> 70.4 us  [per_device(): both = lax.all_gather(both, 'z', axis=0, tiled=True)]
    ppermute x0 -> x3, starting transfers between devices: none -> 16.5 us  [ahead(): lax.ppermute(value, 'z', [(i, i + steps) for i in range(chips - steps)])]
    ppermute x3, starting transfers between devices: 29.7 us -> 27.9 us  [swap(): return lax.ppermute(value, 'c', [(0, 1), (1, 0)])]
    pallas_call x3 -> x5, Pallas kernels: 6.97 us -> 8.28 us  [call(): pl.pallas_call(kernel, out_shape=tuple((jax.ShapeDtypeStruct(s, d) for s,...]
  transfers between devices with their start and end apart: 4 -> 7, of which waited for: 1 -> 2; matrix products, arithmetic and copies ran while one was open for 1% -> 3% of each run, Pallas kernels for 0% -> 0%
where the time goes in v5:
time: 164 us; the launch traced here: 163 us
  blocking collectives  95.1 us (58%)
  starting transfers between devices  45.2 us (28%)
  Pallas kernels  8.28 us (5%)
  matrix products  4.12 us (3%)
  other arithmetic  3.73 us (2%)
  local copies, waits for them, and re-layouts  3.09 us (2%)
  waiting for transfers between devices  2.3 us (1%)
    all_gather x1, blocking collectives, per_device(): both = lax.all_gather(both, 'z', axis=0, tiled=True)  70.4 us
    ppermute x3, starting transfers between devices, swap(): return lax.ppermute(value, 'c', [(0, 1), (1, 0)])  27.9 us
    all_gather x1, blocking collectives, per_device(): lax.all_gather(to_f16(normed, N_SCALE), 'h', axis=0)  24.6 us
    ppermute x3, starting transfers between devices, ahead(): lax.ppermute(value, 'z', [(i, i + steps) for i in range(chips - steps)])  16.5 us
    pallas_call x5, Pallas kernels, call(): pl.pallas_call(kernel, out_shape=tuple((jax.ShapeDtypeStruct(s, d) for s,...  8.28 us
  transfers between devices with their start and end apart: 7, of which 2 were waited for; matrix products, arithmetic and copies ran while one was open for 3% of the time, Pallas kernels for 0%

profile of v5, /device:TPU:1, one launch (start us, length us, event | category | flops | bytes accessed | tf_op | source)
XLA Modules:
  0.0 162.8 jit_solution(12996674742133372471)
XLA Ops:
  0.1 0.9 copy-done
  1.0 0.8 copy-done.1
  1.8 0.7 copy-done.2
  3.1 8.8 %collective-permute-start.4 = (bf16[128,640]{1,0:T(8,128)(2,1)S(1)}, bf16[128,640]{1,0:T(8,128)(2,1)S(1)}, u32[]{:S(2)}, u32[]{:S(2)}) collective-permute-start(bf16[128,640]{1,0:T(8,128)(2,1)S(1)} %get-tuple-element.23), channel_id=1, source_target_pairs={{0,16},{16,0},{1,17},{17,1},{2,18},{18,2},{3,19},{19,3},{4,20},{20... | collective-permute-start | bytes 491528 | tf_op jit(solution)/shard_map/ppermute | solution.py:220
  11.9 1.9 %collective-permute-start.6 = (bf16[256,4096]{1,0:T(8,128)(2,1)}, bf16[256,4096]{1,0:T(8,128)(2,1)S(1)}, u32[]{:S(2)}, u32[]{:S(2)}) collective-permute-start(bf16[256,4096]{1,0:T(8,128)(2,1)} %param.7), channel_id=1, source_target_pairs={{0,16},{16,0},{1,17},{17,1},{2,18},{18,2},{3,19},{19,3},{4,20},{20... | collective-permute-start | bytes 6291464 | tf_op jit(solution)/shard_map/ppermute | solution.py:220
  13.9 0.7 and_select_fusion
  14.6 0.8 collective-permute-start.5
  15.6 70.4 %all-gather.3 = f16[4096,512]{1,0:T(8,128)(2,1)S(1)} all-gather(f16[256,512]{1,0:T(8,128)(2,1)S(1)} %pad_maximum_fusion), channel_id=1, replica_groups=mesh['z'=16,'c'=2,'h'=16] {'z'}, dimensions={0}, use_global_device_ids=true | all-gather | bytes 4456448 | tf_op jit(solution)/shard_map/all_gather | solution.py:266
  86.1 1.3 fusion.6.own_ref
  87.4 0.6 copy-done.5
  88.0 1.3 fusion.7.sib_ref
  89.3 5.4 %shard_map.56 = (f32[128,256]{1,0:T(8,128)S(1)}, bf16[128,256]{1,0:T(8,128)(2,1)S(1)}, f32[2,512,128]{2,1,0:T(8,128)S(1)}) custom-call(s32[2]{0:T(128)S(1)} %pad_add_fusion.meta_ref, s32[9]{0:T(128)S(1)} %copy-done.4, bf16[256,384]{1,0:T(8,128)(2,1)S(1)} %fusion.6.own_ref, bf16[256,384]{1,0:T(8,128)(2,1)S(1)} %fusion.7.sib_ref, s32[2,256]{1,0:T(2,128)S(1)} %bitcast.34, ...), custom_call_target="tpu_custom_call" | custom-call | flops 3221225472 | bytes 1048576 | tf_op jit(solution)/shard_map/pallas_call | solution.py:209
  94.7 3.5 %collective-permute-start.7 = (bf16[128,256]{1,0:T(8,128)(2,1)S(1)}, bf16[128,256]{1,0:T(8,128)(2,1)S(1)}, u32[]{:S(2)}, u32[]{:S(2)}) collective-permute-start(bf16[128,256]{1,0:T(8,128)(2,1)S(1)} %get-tuple-element.25), channel_id=1, source_target_pairs={{0,32},{32,64},{64,96},{96,128},{128,160},{160,192},{192,224},{224... | collective-permute-start | bytes 196616 | tf_op jit(solution)/shard_map/ppermute | solution.py:225
  98.4 1.1 collective-permute-done.7.one_ref
  99.7 3.4 %collective-permute-start.8 = (bf16[128,256]{1,0:T(8,128)(2,1)S(1)}, bf16[128,256]{1,0:T(8,128)(2,1)S(1)}, u32[]{:S(2)}, u32[]{:S(2)}) collective-permute-start(bf16[128,256]{1,0:T(8,128)(2,1)S(1)} %shard_map.57), channel_id=1, source_target_pairs={{0,64},{32,96},{64,128},{96,160},{128,192},{160,224},{192,256},{22... | collective-permute-start | bytes 196616 | tf_op jit(solution)/shard_map/ppermute | solution.py:225
  103.1 0.6 compare_reduce_fusion
  104.4 1.0 shard_map.58
  105.5 9.6 %collective-permute-start.9 = (bf16[128,128]{1,0:T(8,128)(2,1)}, bf16[128,128]{1,0:T(8,128)(2,1)S(1)}, u32[]{:S(2)}, u32[]{:S(2)}) collective-permute-start(bf16[128,128]{1,0:T(8,128)(2,1)} %get-tuple-element.27), channel_id=1, source_target_pairs={{0,128},{32,160},{64,192},{96,224},{128,256},{160,288},{192,320},{... | collective-permute-start | bytes 98312 | tf_op jit(solution)/shard_map/ppermute | solution.py:225
  115.1 1.5 multiply_convert_fusion.4
  116.6 1.1 shard_map.59
  117.7 24.6 %all-gather.4 = f16[8192,128]{1,0:T(8,128)(2,1)S(1)} all-gather(f16[512,128]{1,0:T(8,128)(2,1)S(1)} %multiply_convert_fusion.14), channel_id=2, replica_groups=mesh['z'=16,'c'=2,'h'=16] {'h'}, dimensions={0}, use_global_device_ids=true | all-gather | bytes 2228224 | tf_op jit(solution)/shard_map/all_gather | solution.py:310
  143.3 17.2 %collective-permute-start.10 = (f32[256,256]{1,0:T(8,128)S(1)}, f32[256,256]{1,0:T(8,128)S(1)}, u32[]{:S(2)}, u32[]{:S(2)}) collective-permute-start(f32[256,256]{1,0:T(8,128)S(1)} %convolution_bitcast_fusion.1), channel_id=1, source_target_pairs={{0,16},{16,0},{1,17},{17,1},{2,18},{18,2},{3,19},{19,3},{4,20},{20... | collective-permute-start | bytes 786440 | tf_op jit(solution)/shard_map/ppermute | solution.py:220
  160.5 1.1 collective-permute-done.10
  161.6 1.1 fusion.5
  (32 shorter events, 2.3 us)
Async XLA Ops:
  0.1 0.9 copy-start
  1.0 0.8 copy-start.1
  1.8 0.7 copy-start.2
  3.1 11.4 %collective-permute-start.4 = (bf16[128,640]{1,0:T(8,128)(2,1)S(1)}, bf16[128,640]{1,0:T(8,128)(2,1)S(1)}, u32[]{:S(2)}, u32[]{:S(2)}) collective-permute-start(bf16[128,640]{1,0:T(8,128)(2,1)S(1)} %get-tuple-element.23), channel_id=1, source_target_pairs={{0,16},{16,0},{1,17},{17,1},{2,18},{18,2},{3,19},{19,3},{4,20},{20... | collective-permute-start | bytes 491528 | tf_op jit(solution)/shard_map/ppermute | solution.py:220
  11.9 75.5 %collective-permute-start.6 = (bf16[256,4096]{1,0:T(8,128)(2,1)}, bf16[256,4096]{1,0:T(8,128)(2,1)S(1)}, u32[]{:S(2)}, u32[]{:S(2)}) collective-permute-start(bf16[256,4096]{1,0:T(8,128)(2,1)} %param.7), channel_id=1, source_target_pairs={{0,16},{16,0},{1,17},{17,1},{2,18},{18,2},{3,19},{19,3},{4,20},{20... | collective-permute-start | bytes 6291464 | tf_op jit(solution)/shard_map/ppermute | solution.py:220
  14.5 71.5 %copy-start.6 = (bf16[256,4096]{1,0:T(8,128)(2,1)S(1)}, bf16[256,4096]{1,0:T(8,128)(2,1)}, u32[]{:S(2)}) copy-start(bf16[256,4096]{1,0:T(8,128)(2,1)} %param.7) | copy-start | bytes 6291460
  14.6 0.9 collective-permute-start.5
  86.1 1.9 %copy-start.5 = (f16[4096,512]{1,0:T(8,128)(2,1)}, f16[4096,512]{1,0:T(8,128)(2,1)S(1)}, u32[]{:S(2)}) copy-start(f16[4096,512]{1,0:T(8,128)(2,1)S(1)} %all-gather.3) | copy-start | bytes 12582916
  87.4 1.9 %copy-start.3 = (s32[256,2]{0,1:T(2,128)S(1)}, s32[256,2]{0,1:T(2,128)}, u32[]{:S(2)}) copy-start(s32[256,2]{0,1:T(2,128)} %param.10) | copy-start | bytes 6148
  87.4 1.9 %copy-start.4 = (s32[9]{0:T(128)S(1)}, s32[9]{0:T(128)}, u32[]{:S(2)}) copy-start(s32[9]{0:T(128)} %ds_ref.1) | copy-start | bytes 112
  94.7 4.8 %collective-permute-start.7 = (bf16[128,256]{1,0:T(8,128)(2,1)S(1)}, bf16[128,256]{1,0:T(8,128)(2,1)S(1)}, u32[]{:S(2)}, u32[]{:S(2)}) collective-permute-start(bf16[128,256]{1,0:T(8,128)(2,1)S(1)} %get-tuple-element.25), channel_id=1, source_target_pairs={{0,32},{32,64},{64,96},{96,128},{128,160},{160,192},{192,224},{224... | collective-permute-start | bytes 196616 | tf_op jit(solution)/shard_map/ppermute | solution.py:225
  99.7 4.7 %collective-permute-start.8 = (bf16[128,256]{1,0:T(8,128)(2,1)S(1)}, bf16[128,256]{1,0:T(8,128)(2,1)S(1)}, u32[]{:S(2)}, u32[]{:S(2)}) collective-permute-start(bf16[128,256]{1,0:T(8,128)(2,1)S(1)} %shard_map.57), channel_id=1, source_target_pairs={{0,64},{32,96},{64,128},{96,160},{128,192},{160,224},{192,256},{22... | collective-permute-start | bytes 196616 | tf_op jit(solution)/shard_map/ppermute | solution.py:225
  105.5 11.1 %collective-permute-start.9 = (bf16[128,128]{1,0:T(8,128)(2,1)}, bf16[128,128]{1,0:T(8,128)(2,1)S(1)}, u32[]{:S(2)}, u32[]{:S(2)}) collective-permute-start(bf16[128,128]{1,0:T(8,128)(2,1)} %get-tuple-element.27), channel_id=1, source_target_pairs={{0,128},{32,160},{64,192},{96,224},{128,256},{160,288},{192,320},{... | collective-permute-start | bytes 98312 | tf_op jit(solution)/shard_map/ppermute | solution.py:225
  143.3 18.4 %collective-permute-start.10 = (f32[256,256]{1,0:T(8,128)S(1)}, f32[256,256]{1,0:T(8,128)S(1)}, u32[]{:S(2)}, u32[]{:S(2)}) collective-permute-start(f32[256,256]{1,0:T(8,128)S(1)} %convolution_bitcast_fusion.1), channel_id=1, source_target_pairs={{0,16},{16,0},{1,17},{17,1},{2,18},{18,2},{3,19},{19,3},{4,20},{20... | collective-permute-start | bytes 786440 | tf_op jit(solution)/shard_map/ppermute | solution.py:220

commit v6 on v5

--- a/solution.py
+++ b/solution.py
@@ -77,21 +77,34 @@
     return jnp.where(keep, gram, 0.0)
 
 
-def pack_kernel(meta_ref, w_ref, wo_ref, codes_ref, give_ref, mine_ref):
+def pack_kernel(
+    meta_ref, w_hbm, wo_hbm, codes_hbm, give_ref, mine_ref, w_ref, wo_ref, codes_ref, sems
+):
     first = meta_ref[1] == 0
+    copies = [
+        pltpu.make_async_copy(source, target, sems.at[i])
+        for i, (source, target) in enumerate(
+            ((codes_hbm, codes_ref), (w_hbm, w_ref), (wo_hbm, wo_ref))
+        )
+    ]
+    for copy in copies:
+        copy.start()
 
     def put(place, mine, other):
         cols = slice(HD * place, HD * place + HD)
         mine_ref[:, cols] = jnp.where(first, mine, other).astype(BF16)
         give_ref[:, cols] = jnp.where(first, other, mine).astype(BF16)
 
-    for p in range(3):
-        put(p, w_ref[p, :, :HD].astype(F32), w_ref[p, :, HD:].astype(F32))
-    put(3, wo_ref[:HD].astype(F32), wo_ref[HD:].astype(F32))
+    copies[0].wait()
     codes = codes_ref[...].astype(F32)
     other = jnp.where(first, codes[1:2], codes[0:1])
     row = lax.broadcasted_iota(jnp.int32, (HD, HD), 0)
     give_ref[:, 4 * HD :] = jnp.where(row == 0, other[:, :HD], other[:, HD:]).astype(BF16)
+    copies[1].wait()
+    for p in range(3):
+        put(p, w_ref[p, :, :HD].astype(F32), w_ref[p, :, HD:].astype(F32))
+    copies[2].wait()
+    put(3, wo_ref[:HD].astype(F32), wo_ref[HD:].astype(F32))
 
 
 def local_kernel(
@@ -243,13 +256,23 @@
     meta = jnp.stack([z, c]).astype(jnp.int32)
     codes = beta_codes.T
 
-    give, mine = call(
+    whole = pl.BlockSpec(memory_space=pltpu.HBM)
+    give, mine = pl.pallas_call(
         pack_kernel,
-        (meta,),
-        (w_qkv, w_out, codes),
-        [((HD, 5 * HD), BF16), ((HD, 4 * HD), BF16)],
-        1 << 20,
-    )
+        out_shape=(
+            jax.ShapeDtypeStruct((HD, 5 * HD), BF16),
+            jax.ShapeDtypeStruct((HD, 4 * HD), BF16),
+        ),
+        in_specs=[SMEM, whole, whole, whole],
+        out_specs=(VMEM, VMEM),
+        scratch_shapes=[
+            pltpu.VMEM(w_qkv.shape, BF16),
+            pltpu.VMEM(w_out.shape, BF16),
+            pltpu.VMEM(codes.shape, jnp.int32),
+            pltpu.SemaphoreType.DMA((3,)),
+        ],
+        compiler_params=pltpu.CompilerParams(vmem_limit_bytes=8 << 20),
+    )(meta, w_qkv, w_out, codes)
     got = swap(give)
     hidden_sib = swap(hidden_in)
 
@@ -307,11 +330,12 @@
         [((TOK, HD), BF16)],
         1 << 28,
     )
-    normed_all = from_f16(lax.all_gather(to_f16(normed, N_SCALE), "h", axis=0), N_SCALE)
+    normed_all = lax.all_gather(to_f16(normed, N_SCALE), "h", axis=0)
     wo_cols = from_f16(both[:, 3 * HD :], WO_SCALE).reshape(chips, 2, HD, HD)
     wo_cols = wo_cols.transpose(0, 2, 1, 3).reshape(chips, HD, 2 * HD)
 
     def output(rows):
+        rows = from_f16(rows, N_SCALE)
         return jnp.einsum("htf,hfn->tn", rows, wo_cols, preferred_element_type=F32)
 
     sent = swap(output(normed_all[:, :half]))

time: 164 us -> 164 us (level)
    pallas_call x5 -> x4, Pallas kernels: 8.28 us -> 7.68 us  [call(): pl.pallas_call(kernel, out_shape=tuple((jax.ShapeDtypeStruct(s, d) for s,...]
where the time goes in v6:
time: 164 us; the launch traced here: 163 us
  blocking collectives  95.2 us (58%)
  starting transfers between devices  45.1 us (28%)
  Pallas kernels  8.66 us (5%)
  matrix products  4.11 us (3%)
  other arithmetic  3.25 us (2%)
  local copies, waits for them, and re-layouts  3.09 us (2%)
  waiting for transfers between devices  2.3 us (1%)
    all_gather x1, blocking collectives, per_device(): both = lax.all_gather(both, 'z', axis=0, tiled=True)  70.6 us
    ppermute x3, starting transfers between devices, swap(): return lax.ppermute(value, 'c', [(0, 1), (1, 0)])  27.9 us
    all_gather x1, blocking collectives, per_device(): normed_all = lax.all_gather(to_f16(normed, N_SCALE), 'h', axis=0)  24.6 us
    ppermute x3, starting transfers between devices, ahead(): lax.ppermute(value, 'z', [(i, i + steps) for i in range(chips - steps)])  16.5 us
    pallas_call x4, Pallas kernels, call(): pl.pallas_call(kernel, out_shape=tuple((jax.ShapeDtypeStruct(s, d) for s,...  7.68 us
  transfers between devices with their start and end apart: 7, of which 2 were waited for; matrix products, arithmetic and copies ran while one was open for 3% of the time, Pallas kernels for 0%

profile of v6, /device:TPU:1, one launch (start us, length us, event | category | flops | bytes accessed | tf_op | source)
XLA Modules:
  0.0 162.6 jit_solution(15630948835768306340)
XLA Ops:
  0.1 0.9 copy-done
  1.0 0.8 copy-done.1
  1.8 0.7 copy-done.2
  2.5 1.0 shard_map.55
  3.5 8.8 %collective-permute-start.4 = (bf16[128,640]{1,0:T(8,128)(2,1)S(1)}, bf16[128,640]{1,0:T(8,128)(2,1)S(1)}, u32[]{:S(2)}, u32[]{:S(2)}) collective-permute-start(bf16[128,640]{1,0:T(8,128)(2,1)S(1)} %get-tuple-element.23), channel_id=1, source_target_pairs={{0,16},{16,0},{1,17},{17,1},{2,18},{18,2},{3,19},{19,3},{4,20},{20... | collective-permute-start | bytes 491528 | tf_op jit(solution)/shard_map/ppermute | solution.py:233
  12.3 1.9 %collective-permute-start.6 = (bf16[256,4096]{1,0:T(8,128)(2,1)}, bf16[256,4096]{1,0:T(8,128)(2,1)S(1)}, u32[]{:S(2)}, u32[]{:S(2)}) collective-permute-start(bf16[256,4096]{1,0:T(8,128)(2,1)} %param.7), channel_id=1, source_target_pairs={{0,16},{16,0},{1,17},{17,1},{2,18},{18,2},{3,19},{19,3},{4,20},{20... | collective-permute-start | bytes 6291464 | tf_op jit(solution)/shard_map/ppermute | solution.py:233
  14.2 0.7 and_select_fusion
  15.0 0.7 collective-permute-start.5
  15.9 70.6 %all-gather.3 = f16[4096,512]{1,0:T(8,128)(2,1)S(1)} all-gather(f16[256,512]{1,0:T(8,128)(2,1)S(1)} %pad_maximum_fusion), channel_id=1, replica_groups=mesh['z'=16,'c'=2,'h'=16] {'z'}, dimensions={0}, use_global_device_ids=true | all-gather | bytes 4456448 | tf_op jit(solution)/shard_map/all_gather | solution.py:289
  86.4 1.3 fusion.6.own_ref
  88.4 1.3 fusion.7.sib_ref
  89.7 5.4 %shard_map.56 = (f32[128,256]{1,0:T(8,128)S(1)}, bf16[128,256]{1,0:T(8,128)(2,1)S(1)}, f32[2,512,128]{2,1,0:T(8,128)S(1)}) custom-call(s32[2]{0:T(128)S(1)} %pad_add_fusion.meta_ref, s32[9]{0:T(128)S(1)} %copy-done.4, bf16[256,384]{1,0:T(8,128)(2,1)S(1)} %fusion.6.own_ref, bf16[256,384]{1,0:T(8,128)(2,1)S(1)} %fusion.7.sib_ref, s32[2,256]{1,0:T(2,128)S(1)} %bitcast.34, ...), custom_call_target="tpu_custom_call" | custom-call | flops 3221225472 | bytes 1048576 | tf_op jit(solution)/shard_map/pallas_call | solution.py:222
  95.1 3.5 %collective-permute-start.7 = (bf16[128,256]{1,0:T(8,128)(2,1)S(1)}, bf16[128,256]{1,0:T(8,128)(2,1)S(1)}, u32[]{:S(2)}, u32[]{:S(2)}) collective-permute-start(bf16[128,256]{1,0:T(8,128)(2,1)S(1)} %get-tuple-element.25), channel_id=1, source_target_pairs={{0,32},{32,64},{64,96},{96,128},{128,160},{160,192},{192,224},{224... | collective-permute-start | bytes 196616 | tf_op jit(solution)/shard_map/ppermute | solution.py:238
  98.7 1.1 collective-permute-done.7.one_ref
  100.0 3.4 %collective-permute-start.8 = (bf16[128,256]{1,0:T(8,128)(2,1)S(1)}, bf16[128,256]{1,0:T(8,128)(2,1)S(1)}, u32[]{:S(2)}, u32[]{:S(2)}) collective-permute-start(bf16[128,256]{1,0:T(8,128)(2,1)S(1)} %shard_map.57), channel_id=1, source_target_pairs={{0,64},{32,96},{64,128},{96,160},{128,192},{160,224},{192,256},{22... | collective-permute-start | bytes 196616 | tf_op jit(solution)/shard_map/ppermute | solution.py:238
  103.5 0.6 compare_reduce_fusion
  104.8 1.0 shard_map.58
  105.8 9.6 %collective-permute-start.9 = (bf16[128,128]{1,0:T(8,128)(2,1)}, bf16[128,128]{1,0:T(8,128)(2,1)S(1)}, u32[]{:S(2)}, u32[]{:S(2)}) collective-permute-start(bf16[128,128]{1,0:T(8,128)(2,1)} %get-tuple-element.27), channel_id=1, source_target_pairs={{0,128},{32,160},{64,192},{96,224},{128,256},{160,288},{192,320},{... | collective-permute-start | bytes 98312 | tf_op jit(solution)/shard_map/ppermute | solution.py:238
  115.5 1.5 multiply_convert_fusion.4
  117.0 1.1 shard_map.59
  118.1 24.6 %all-gather.4 = f16[8192,128]{1,0:T(8,128)(2,1)S(1)} all-gather(f16[512,128]{1,0:T(8,128)(2,1)S(1)} %multiply_convert_fusion.17), channel_id=2, replica_groups=mesh['z'=16,'c'=2,'h'=16] {'h'}, dimensions={0}, use_global_device_ids=true | all-gather | bytes 2228224 | tf_op jit(solution)/shard_map/all_gather | solution.py:333
  143.2 17.2 %collective-permute-start.10 = (f32[256,256]{1,0:T(8,128)S(1)}, f32[256,256]{1,0:T(8,128)S(1)}, u32[]{:S(2)}, u32[]{:S(2)}) collective-permute-start(f32[256,256]{1,0:T(8,128)S(1)} %convolution_bitcast_fusion.1), channel_id=1, source_target_pairs={{0,16},{16,0},{1,17},{17,1},{2,18},{18,2},{3,19},{19,3},{4,20},{20... | collective-permute-start | bytes 786440 | tf_op jit(solution)/shard_map/ppermute | solution.py:233
  160.4 1.1 collective-permute-done.10
  161.5 1.1 fusion.5
  (31 shorter events, 1.8 us)
Async XLA Ops:
  0.1 0.9 copy-start
  1.0 0.8 copy-start.1
  1.8 0.7 copy-start.2
  3.5 11.4 %collective-permute-start.4 = (bf16[128,640]{1,0:T(8,128)(2,1)S(1)}, bf16[128,640]{1,0:T(8,128)(2,1)S(1)}, u32[]{:S(2)}, u32[]{:S(2)}) collective-permute-start(bf16[128,640]{1,0:T(8,128)(2,1)S(1)} %get-tuple-element.23), channel_id=1, source_target_pairs={{0,16},{16,0},{1,17},{17,1},{2,18},{18,2},{3,19},{19,3},{4,20},{20... | collective-permute-start | bytes 491528 | tf_op jit(solution)/shard_map/ppermute | solution.py:233
  12.3 75.5 %collective-permute-start.6 = (bf16[256,4096]{1,0:T(8,128)(2,1)}, bf16[256,4096]{1,0:T(8,128)(2,1)S(1)}, u32[]{:S(2)}, u32[]{:S(2)}) collective-permute-start(bf16[256,4096]{1,0:T(8,128)(2,1)} %param.7), channel_id=1, source_target_pairs={{0,16},{16,0},{1,17},{17,1},{2,18},{18,2},{3,19},{19,3},{4,20},{20... | collective-permute-start | bytes 6291464 | tf_op jit(solution)/shard_map/ppermute | solution.py:233
  15.0 0.8 collective-permute-start.5
  15.8 70.6 %copy-start.6 = (bf16[256,4096]{1,0:T(8,128)(2,1)S(1)}, bf16[256,4096]{1,0:T(8,128)(2,1)}, u32[]{:S(2)}) copy-start(bf16[256,4096]{1,0:T(8,128)(2,1)} %param.7) | copy-start | bytes 6291460
  86.4 1.9 %copy-start.5 = (f16[4096,512]{1,0:T(8,128)(2,1)}, f16[4096,512]{1,0:T(8,128)(2,1)S(1)}, u32[]{:S(2)}) copy-start(f16[4096,512]{1,0:T(8,128)(2,1)S(1)} %all-gather.3) | copy-start | bytes 12582916
  87.7 1.9 %copy-start.3 = (s32[256,2]{0,1:T(2,128)S(1)}, s32[256,2]{0,1:T(2,128)}, u32[]{:S(2)}) copy-start(s32[256,2]{0,1:T(2,128)} %param.10) | copy-start | bytes 6148
  87.8 1.9 %copy-start.4 = (s32[9]{0:T(128)S(1)}, s32[9]{0:T(128)}, u32[]{:S(2)}) copy-start(s32[9]{0:T(128)} %ds_ref.1) | copy-start | bytes 112
  95.1 4.8 %collective-permute-start.7 = (bf16[128,256]{1,0:T(8,128)(2,1)S(1)}, bf16[128,256]{1,0:T(8,128)(2,1)S(1)}, u32[]{:S(2)}, u32[]{:S(2)}) collective-permute-start(bf16[128,256]{1,0:T(8,128)(2,1)S(1)} %get-tuple-element.25), channel_id=1, source_target_pairs={{0,32},{32,64},{64,96},{96,128},{128,160},{160,192},{192,224},{224... | collective-permute-start | bytes 196616 | tf_op jit(solution)/shard_map/ppermute | solution.py:238
  100.0 4.7 %collective-permute-start.8 = (bf16[128,256]{1,0:T(8,128)(2,1)S(1)}, bf16[128,256]{1,0:T(8,128)(2,1)S(1)}, u32[]{:S(2)}, u32[]{:S(2)}) collective-permute-start(bf16[128,256]{1,0:T(8,128)(2,1)S(1)} %shard_map.57), channel_id=1, source_target_pairs={{0,64},{32,96},{64,128},{96,160},{128,192},{160,224},{192,256},{22... | collective-permute-start | bytes 196616 | tf_op jit(solution)/shard_map/ppermute | solution.py:238
  105.8 11.1 %collective-permute-start.9 = (bf16[128,128]{1,0:T(8,128)(2,1)}, bf16[128,128]{1,0:T(8,128)(2,1)S(1)}, u32[]{:S(2)}, u32[]{:S(2)}) collective-permute-start(bf16[128,128]{1,0:T(8,128)(2,1)} %get-tuple-element.27), channel_id=1, source_target_pairs={{0,128},{32,160},{64,192},{96,224},{128,256},{160,288},{192,320},{... | collective-permute-start | bytes 98312 | tf_op jit(solution)/shard_map/ppermute | solution.py:238
  143.2 18.4 %collective-permute-start.10 = (f32[256,256]{1,0:T(8,128)S(1)}, f32[256,256]{1,0:T(8,128)S(1)}, u32[]{:S(2)}, u32[]{:S(2)}) collective-permute-start(f32[256,256]{1,0:T(8,128)S(1)} %convolution_bitcast_fusion.1), channel_id=1, source_target_pairs={{0,16},{16,0},{1,17},{17,1},{2,18},{18,2},{3,19},{19,3},{4,20},{20... | collective-permute-start | bytes 786440 | tf_op jit(solution)/shard_map/ppermute | solution.py:233

commit v7 on v6

--- a/solution.py
+++ b/solution.py
@@ -77,34 +77,26 @@
     return jnp.where(keep, gram, 0.0)
 
 
-def pack_kernel(
-    meta_ref, w_hbm, wo_hbm, codes_hbm, give_ref, mine_ref, w_ref, wo_ref, codes_ref, sems
-):
+def pack_kernel(meta_ref, w_hbm, codes_hbm, give_ref, mine_ref, w_ref, codes_ref, sems):
     first = meta_ref[1] == 0
     copies = [
-        pltpu.make_async_copy(source, target, sems.at[i])
-        for i, (source, target) in enumerate(
-            ((codes_hbm, codes_ref), (w_hbm, w_ref), (wo_hbm, wo_ref))
-        )
+        pltpu.make_async_copy(codes_hbm, codes_ref, sems.at[0]),
+        pltpu.make_async_copy(w_hbm, w_ref, sems.at[1]),
     ]
     for copy in copies:
         copy.start()
-
-    def put(place, mine, other):
-        cols = slice(HD * place, HD * place + HD)
-        mine_ref[:, cols] = jnp.where(first, mine, other).astype(BF16)
-        give_ref[:, cols] = jnp.where(first, other, mine).astype(BF16)
-
     copies[0].wait()
     codes = codes_ref[...].astype(F32)
     other = jnp.where(first, codes[1:2], codes[0:1])
     row = lax.broadcasted_iota(jnp.int32, (HD, HD), 0)
-    give_ref[:, 4 * HD :] = jnp.where(row == 0, other[:, :HD], other[:, HD:]).astype(BF16)
+    give_ref[:, 3 * HD :] = jnp.where(row == 0, other[:, :HD], other[:, HD:]).astype(BF16)
     copies[1].wait()
     for p in range(3):
-        put(p, w_ref[p, :, :HD].astype(F32), w_ref[p, :, HD:].astype(F32))
-    copies[2].wait()
-    put(3, wo_ref[:HD].astype(F32), wo_ref[HD:].astype(F32))
+        cols = slice(HD * p, HD * p + HD)
+        left = w_ref[p, :, :HD].astype(F32)
+        right = w_ref[p, :, HD:].astype(F32)
+        mine_ref[:, cols] = jnp.where(first, left, right).astype(BF16)
+        give_ref[:, cols] = jnp.where(first, right, left).astype(BF16)
 
 
 def local_kernel(
@@ -118,7 +110,7 @@
     value = qkv[:, 2 * HD :]
     codes = codes_ref[...].astype(F32)
     own_codes = jnp.where(first, codes[0:1], codes[1:2])
-    got = got_ref[0:8, 4 * HD :].astype(F32)
+    got = got_ref[0:8, 3 * HD :].astype(F32)
     sib_codes = jnp.concatenate([got[0:1], got[1:2]], axis=1)
     codes = jnp.concatenate(
         [jnp.where(first, own_codes, sib_codes), jnp.where(first, sib_codes, own_codes)], axis=1
@@ -256,35 +248,45 @@
     meta = jnp.stack([z, c]).astype(jnp.int32)
     codes = beta_codes.T
 
-    whole = pl.BlockSpec(memory_space=pltpu.HBM)
+    def turned(core):
+        pairs = [
+            ((i * 2 + k) * heads + j, (j * 2 + (k ^ core)) * heads + i)
+            for i in range(chips)
+            for k in range(2)
+            for j in range(heads)
+        ]
+        rows = lax.ppermute(w_out, ("z", "c", "h"), pairs)
+        return jnp.where(first, rows[:HD], rows[HD:])
+
+    wo_same, wo_cross = turned(0), turned(1)
+    wo = jnp.concatenate(
+        [jnp.where(first, wo_same, wo_cross), jnp.where(first, wo_cross, wo_same)], axis=0
+    )
+    whole = pl.BlockSpec(memory_space=pl.ANY)
     give, mine = pl.pallas_call(
         pack_kernel,
         out_shape=(
-            jax.ShapeDtypeStruct((HD, 5 * HD), BF16),
             jax.ShapeDtypeStruct((HD, 4 * HD), BF16),
+            jax.ShapeDtypeStruct((HD, 3 * HD), BF16),
         ),
-        in_specs=[SMEM, whole, whole, whole],
+        in_specs=[SMEM, whole, whole],
         out_specs=(VMEM, VMEM),
         scratch_shapes=[
             pltpu.VMEM(w_qkv.shape, BF16),
-            pltpu.VMEM(w_out.shape, BF16),
             pltpu.VMEM(codes.shape, jnp.int32),
-            pltpu.SemaphoreType.DMA((3,)),
+            pltpu.SemaphoreType.DMA((2,)),
         ],
-        compiler_params=pltpu.CompilerParams(vmem_limit_bytes=8 << 20),
-    )(meta, w_qkv, w_out, codes)
+        compiler_params=pltpu.CompilerParams(vmem_limit_bytes=60 << 20),
+    )(meta, w_qkv, codes)
     got = swap(give)
     hidden_sib = swap(hidden_in)
 
-    def chip(cols, axis):
-        a, b = mine[:, cols], got[:, cols]
-        return jnp.concatenate([jnp.where(first, a, b), jnp.where(first, b, a)], axis=axis)
-
-    turned = [(i * heads + j, j * heads + i) for i in range(chips) for j in range(heads)]
-    wo = lax.ppermute(chip(slice(3 * HD, 4 * HD), 1), ("z", "h"), turned)
-    wo = jnp.concatenate([wo[:, :HD], wo[:, HD:]], axis=0)
+    other = got[:, : 3 * HD]
+    w_chip = jnp.concatenate(
+        [jnp.where(first, mine, other), jnp.where(first, other, mine)], axis=0
+    )
     both = jnp.concatenate(
-        [to_f16(chip(slice(0, 3 * HD), 0), W_SCALE), to_f16(wo, WO_SCALE)], axis=1
+        [to_f16(w_chip, W_SCALE), to_f16(wo, WO_SCALE)], axis=1
     )
     both = lax.all_gather(both, "z", axis=0, tiled=True)
     w_all = from_f16(both[:, : 3 * HD], W_SCALE)

time: 164 us -> 168 us (1.024)
  blocking collectives: 95.2 us -> 99.7 us
  local copies, waits for them, and re-layouts: 3.09 us -> 0.64 us
    ppermute x1 -> x2, starting transfers between devices: 0.66 us -> 10.3 us  [turned(): rows = lax.ppermute(w_out, ('z', 'c', 'h'), pairs)]
    all_gather x1, blocking collectives: 70.6 us -> 77.5 us  [per_device(): both = lax.all_gather(both, 'z', axis=0, tiled=True)]
    ppermute x3, starting transfers between devices: 27.9 us -> 21.5 us  [swap(): return lax.ppermute(value, 'c', [(0, 1), (1, 0)])]
    ppermute x3, starting transfers between devices: 16.5 us -> 13.8 us  [ahead(): lax.ppermute(value, 'z', [(i, i + steps) for i in range(chips - steps)])]
    unnamed x14 -> x10, local copies, waits for them, and re-layouts: 3.07 us -> 0.64 us
    all_gather x1, blocking collectives: 24.6 us -> 22.2 us  [per_device(): normed_all = lax.all_gather(to_f16(normed, N_SCALE), 'h', axis=0)]
  transfers between devices with their start and end apart: 7 -> 8, of which waited for: 2 -> 2; matrix products, arithmetic and copies ran while one was open for 3% -> 4% of each run, Pallas kernels for 0% -> 1%
where the time goes in v7:
time: 168 us
  blocking collectives  99.7 us (59%)
  starting transfers between devices  45.6 us (27%)
  Pallas kernels  10 us (6%)
  other arithmetic  4.66 us (3%)
  matrix products  4.12 us (2%)
  waiting for transfers between devices  2.3 us (1%)
    all_gather x1, blocking collectives, per_device(): both = lax.all_gather(both, 'z', axis=0, tiled=True)  77.5 us
    all_gather x1, blocking collectives, per_device(): normed_all = lax.all_gather(to_f16(normed, N_SCALE), 'h', axis=0)  22.2 us
    ppermute x3, starting transfers between devices, swap(): return lax.ppermute(value, 'c', [(0, 1), (1, 0)])  21.5 us
    ppermute x3, starting transfers between devices, ahead(): lax.ppermute(value, 'z', [(i, i + steps) for i in range(chips - steps)])  13.8 us
    ppermute x2, starting transfers between devices, turned(): rows = lax.ppermute(w_out, ('z', 'c', 'h'), pairs)  10.3 us
    pallas_call x4, Pallas kernels, call(): pl.pallas_call(kernel, out_shape=tuple((jax.ShapeDtypeStruct(s, d) for s,...  7.68 us
  transfers between devices with their start and end apart: 8, of which 2 were waited for; matrix products, arithmetic and copies ran while one was open for 4% of the time, Pallas kernels for 1%

profile of v7, /device:TPU:1, one launch (start us, length us, event | category | flops | bytes accessed | tf_op | source)
XLA Modules:
  0.0 168.0 jit_solution(14670183359689710951)
XLA Ops:
  0.0 8.8 %collective-permute-start.6 = (bf16[256,128]{1,0:T(8,128)(2,1)}, bf16[256,128]{1,0:T(8,128)(2,1)S(1)}, u32[]{:S(2)}, u32[]{:S(2)}) collective-permute-start(bf16[256,128]{1,0:T(8,128)(2,1)} %param.11), channel_id=1, source_target_pairs={{0,16},{1,48},{2,80},{3,112},{4,144},{5,176},{6,208},{7,240},{8,27... | collective-permute-start | bytes 196616 | tf_op jit(solution)/shard_map/ppermute | solution.py:258
  8.8 1.5 collective-permute-start.5
  10.9 2.3 %shard_map.55 = (bf16[128,512]{1,0:T(8,128)(2,1)}, bf16[128,384]{1,0:T(8,128)(2,1)}) custom-call(s32[2]{0:T(128)} %pad_add_fusion.meta_ref, bf16[3,128,256]{2,1,0:T(8,128)(2,1)} %w_hbm.1, s32[2,256]{1,0:T(2,128)} %bitcast.33), custom_call_target="tpu_custom_call" | custom-call | tf_op jit(solution)/shard_map/pallas_call | solution.py:266
  13.2 1.9 %collective-permute-start.4 = (bf16[128,512]{1,0:T(8,128)(2,1)}, bf16[128,512]{1,0:T(8,128)(2,1)S(1)}, u32[]{:S(2)}, u32[]{:S(2)}) collective-permute-start(bf16[128,512]{1,0:T(8,128)(2,1)} %get-tuple-element.23), channel_id=1, source_target_pairs={{0,16},{16,0},{1,17},{17,1},{2,18},{18,2},{3,19},{19,3},{4,20},{20... | collective-permute-start | bytes 393224 | tf_op jit(solution)/shard_map/ppermute | solution.py:225
  15.2 2.4 %collective-permute-start.7 = (bf16[256,4096]{1,0:T(8,128)(2,1)}, bf16[256,4096]{1,0:T(8,128)(2,1)S(1)}, u32[]{:S(2)}, u32[]{:S(2)}) collective-permute-start(bf16[256,4096]{1,0:T(8,128)(2,1)} %param.7), channel_id=1, source_target_pairs={{0,16},{16,0},{1,17},{17,1},{2,18},{18,2},{3,19},{19,3},{4,20},{20... | collective-permute-start | bytes 6291464 | tf_op jit(solution)/shard_map/ppermute | solution.py:225
  17.6 0.7 and_select_fusion
  18.3 0.9 broadcast_select_fusion.1
  19.4 77.5 %all-gather.3 = f16[4096,512]{1,0:T(8,128)(2,1)S(1)} all-gather(f16[256,512]{1,0:T(8,128)(2,1)S(1)} %pad_maximum_fusion), channel_id=1, replica_groups=mesh['z'=16,'c'=2,'h'=16] {'z'}, dimensions={0}, use_global_device_ids=true | all-gather | bytes 4456448 | tf_op jit(solution)/shard_map/all_gather | solution.py:291
  96.9 1.3 fusion.6.own_ref
  98.3 0.6 copy-done.3
  98.9 1.3 fusion.7.sib_ref
  100.2 5.4 %shard_map.56 = (f32[128,256]{1,0:T(8,128)S(1)}, bf16[128,256]{1,0:T(8,128)(2,1)S(1)}, f32[2,512,128]{2,1,0:T(8,128)S(1)}) custom-call(s32[2]{0:T(128)S(1)} %copy-done.1, s32[9]{0:T(128)S(1)} %copy-done.2, bf16[256,384]{1,0:T(8,128)(2,1)S(1)} %fusion.6.own_ref, bf16[256,384]{1,0:T(8,128)(2,1)S(1)} %fusion.7.sib_ref, s32[2,256]{1,0:T(2,128)S(1)} %bitcast.34, ...), custom_call_target="tpu_custom_call" | custom-call | flops 3221225472 | bytes 1048576 | tf_op jit(solution)/shard_map/pallas_call | solution.py:214
  105.6 2.3 %collective-permute-start.8 = (bf16[128,256]{1,0:T(8,128)(2,1)S(1)}, bf16[128,256]{1,0:T(8,128)(2,1)S(1)}, u32[]{:S(2)}, u32[]{:S(2)}) collective-permute-start(bf16[128,256]{1,0:T(8,128)(2,1)S(1)} %get-tuple-element.25), channel_id=1, source_target_pairs={{0,32},{32,64},{64,96},{96,128},{128,160},{160,192},{192,224},{224... | collective-permute-start | bytes 196616 | tf_op jit(solution)/shard_map/ppermute | solution.py:230
  108.0 1.1 collective-permute-done.8.one_ref
  109.4 3.4 %collective-permute-start.9 = (bf16[128,256]{1,0:T(8,128)(2,1)S(1)}, bf16[128,256]{1,0:T(8,128)(2,1)S(1)}, u32[]{:S(2)}, u32[]{:S(2)}) collective-permute-start(bf16[128,256]{1,0:T(8,128)(2,1)S(1)} %shard_map.57), channel_id=1, source_target_pairs={{0,64},{32,96},{64,128},{96,160},{128,192},{160,224},{192,256},{22... | collective-permute-start | bytes 196616 | tf_op jit(solution)/shard_map/ppermute | solution.py:230
  112.8 0.6 compare_reduce_fusion
  114.1 1.0 shard_map.58
  115.1 8.1 %collective-permute-start.10 = (bf16[128,128]{1,0:T(8,128)(2,1)}, bf16[128,128]{1,0:T(8,128)(2,1)S(1)}, u32[]{:S(2)}, u32[]{:S(2)}) collective-permute-start(bf16[128,128]{1,0:T(8,128)(2,1)} %get-tuple-element.27), channel_id=1, source_target_pairs={{0,128},{32,160},{64,192},{96,224},{128,256},{160,288},{192,320},{... | collective-permute-start | bytes 98312 | tf_op jit(solution)/shard_map/ppermute | solution.py:230
  123.3 1.5 multiply_convert_fusion.4
  124.8 1.1 shard_map.59
  125.9 22.2 %all-gather.4 = f16[8192,128]{1,0:T(8,128)(2,1)S(1)} all-gather(f16[512,128]{1,0:T(8,128)(2,1)S(1)} %multiply_convert_fusion.17), channel_id=2, replica_groups=mesh['z'=16,'c'=2,'h'=16] {'h'}, dimensions={0}, use_global_device_ids=true | all-gather | bytes 2228224 | tf_op jit(solution)/shard_map/all_gather | solution.py:335
  148.6 17.1 %collective-permute-start.11 = (f32[256,256]{1,0:T(8,128)S(1)}, f32[256,256]{1,0:T(8,128)S(1)}, u32[]{:S(2)}, u32[]{:S(2)}) collective-permute-start(f32[256,256]{1,0:T(8,128)S(1)} %convolution_bitcast_fusion.1), channel_id=1, source_target_pairs={{0,16},{16,0},{1,17},{17,1},{2,18},{18,2},{3,19},{19,3},{4,20},{20... | collective-permute-start | bytes 786440 | tf_op jit(solution)/shard_map/ppermute | solution.py:225
  165.7 1.1 collective-permute-done.11
  166.9 1.1 fusion.5
  (27 shorter events, 1.7 us)
Async XLA Ops:
  0.0 18.3 %collective-permute-start.6 = (bf16[256,128]{1,0:T(8,128)(2,1)}, bf16[256,128]{1,0:T(8,128)(2,1)S(1)}, u32[]{:S(2)}, u32[]{:S(2)}) collective-permute-start(bf16[256,128]{1,0:T(8,128)(2,1)} %param.11), channel_id=1, source_target_pairs={{0,16},{1,48},{2,80},{3,112},{4,144},{5,176},{6,208},{7,240},{8,27... | collective-permute-start | bytes 196616 | tf_op jit(solution)/shard_map/ppermute | solution.py:258
  8.8 9.5 %collective-permute-start.5 = (bf16[256,128]{1,0:T(8,128)(2,1)}, bf16[256,128]{1,0:T(8,128)(2,1)S(1)}, u32[]{:S(2)}, u32[]{:S(2)}) collective-permute-start(bf16[256,128]{1,0:T(8,128)(2,1)} %param.11), channel_id=1, source_target_pairs={{0,0},{1,32},{2,64},{3,96},{4,128},{5,160},{6,192},{7,224},{8,256}... | collective-permute-start | bytes 196616 | tf_op jit(solution)/shard_map/ppermute | solution.py:258
  13.2 5.1 %collective-permute-start.4 = (bf16[128,512]{1,0:T(8,128)(2,1)}, bf16[128,512]{1,0:T(8,128)(2,1)S(1)}, u32[]{:S(2)}, u32[]{:S(2)}) collective-permute-start(bf16[128,512]{1,0:T(8,128)(2,1)} %get-tuple-element.23), channel_id=1, source_target_pairs={{0,16},{16,0},{1,17},{17,1},{2,18},{18,2},{3,19},{19,3},{4,20},{20... | collective-permute-start | bytes 393224 | tf_op jit(solution)/shard_map/ppermute | solution.py:225
  15.2 83.1 %collective-permute-start.7 = (bf16[256,4096]{1,0:T(8,128)(2,1)}, bf16[256,4096]{1,0:T(8,128)(2,1)S(1)}, u32[]{:S(2)}, u32[]{:S(2)}) collective-permute-start(bf16[256,4096]{1,0:T(8,128)(2,1)} %param.7), channel_id=1, source_target_pairs={{0,16},{16,0},{1,17},{17,1},{2,18},{18,2},{3,19},{19,3},{4,20},{20... | collective-permute-start | bytes 6291464 | tf_op jit(solution)/shard_map/ppermute | solution.py:225
  19.4 77.5 %copy-start.4 = (bf16[256,4096]{1,0:T(8,128)(2,1)S(1)}, bf16[256,4096]{1,0:T(8,128)(2,1)}, u32[]{:S(2)}) copy-start(bf16[256,4096]{1,0:T(8,128)(2,1)} %param.7) | copy-start | bytes 6291460
  96.9 2.0 %copy-start.3 = (f16[4096,512]{1,0:T(8,128)(2,1)}, f16[4096,512]{1,0:T(8,128)(2,1)S(1)}, u32[]{:S(2)}) copy-start(f16[4096,512]{1,0:T(8,128)(2,1)S(1)} %all-gather.3) | copy-start | bytes 12582916
  98.2 2.0 %copy-start = (s32[256,2]{0,1:T(2,128)S(1)}, s32[256,2]{0,1:T(2,128)}, u32[]{:S(2)}) copy-start(s32[256,2]{0,1:T(2,128)} %param.10) | copy-start | bytes 6148
  98.2 1.9 %copy-start.1 = (s32[2]{0:T(128)S(1)}, s32[2]{0:T(128)}, u32[]{:S(2)}) copy-start(s32[2]{0:T(128)} %pad_add_fusion.meta_ref) | copy-start | bytes 28
  98.2 1.9 %copy-start.2 = (s32[9]{0:T(128)S(1)}, s32[9]{0:T(128)}, u32[]{:S(2)}) copy-start(s32[9]{0:T(128)} %ds_ref.1) | copy-start | bytes 112
  105.6 3.6 %collective-permute-start.8 = (bf16[128,256]{1,0:T(8,128)(2,1)S(1)}, bf16[128,256]{1,0:T(8,128)(2,1)S(1)}, u32[]{:S(2)}, u32[]{:S(2)}) collective-permute-start(bf16[128,256]{1,0:T(8,128)(2,1)S(1)} %get-tuple-element.25), channel_id=1, source_target_pairs={{0,32},{32,64},{64,96},{96,128},{128,160},{160,192},{192,224},{224... | collective-permute-start | bytes 196616 | tf_op jit(solution)/shard_map/ppermute | solution.py:230
  109.4 4.7 %collective-permute-start.9 = (bf16[128,256]{1,0:T(8,128)(2,1)S(1)}, bf16[128,256]{1,0:T(8,128)(2,1)S(1)}, u32[]{:S(2)}, u32[]{:S(2)}) collective-permute-start(bf16[128,256]{1,0:T(8,128)(2,1)S(1)} %shard_map.57), channel_id=1, source_target_pairs={{0,64},{32,96},{64,128},{96,160},{128,192},{160,224},{192,256},{22... | collective-permute-start | bytes 196616 | tf_op jit(solution)/shard_map/ppermute | solution.py:230
  115.1 9.7 %collective-permute-start.10 = (bf16[128,128]{1,0:T(8,128)(2,1)}, bf16[128,128]{1,0:T(8,128)(2,1)S(1)}, u32[]{:S(2)}, u32[]{:S(2)}) collective-permute-start(bf16[128,128]{1,0:T(8,128)(2,1)} %get-tuple-element.27), channel_id=1, source_target_pairs={{0,128},{32,160},{64,192},{96,224},{128,256},{160,288},{192,320},{... | collective-permute-start | bytes 98312 | tf_op jit(solution)/shard_map/ppermute | solution.py:230
  148.6 18.3 %collective-permute-start.11 = (f32[256,256]{1,0:T(8,128)S(1)}, f32[256,256]{1,0:T(8,128)S(1)}, u32[]{:S(2)}, u32[]{:S(2)}) collective-permute-start(f32[256,256]{1,0:T(8,128)S(1)} %convolution_bitcast_fusion.1), channel_id=1, source_target_pairs={{0,16},{16,0},{1,17},{17,1},{2,18},{18,2},{3,19},{19,3},{4,20},{20... | collective-permute-start | bytes 786440 | tf_op jit(solution)/shard_map/ppermute | solution.py:225

commit v8 on v5

--- a/solution.py
+++ b/solution.py
@@ -77,21 +77,18 @@
     return jnp.where(keep, gram, 0.0)
 
 
-def pack_kernel(meta_ref, w_ref, wo_ref, codes_ref, give_ref, mine_ref):
+def pack_kernel(meta_ref, w_ref, codes_ref, give_ref, mine_ref):
     first = meta_ref[1] == 0
-
-    def put(place, mine, other):
-        cols = slice(HD * place, HD * place + HD)
-        mine_ref[:, cols] = jnp.where(first, mine, other).astype(BF16)
-        give_ref[:, cols] = jnp.where(first, other, mine).astype(BF16)
-
-    for p in range(3):
-        put(p, w_ref[p, :, :HD].astype(F32), w_ref[p, :, HD:].astype(F32))
-    put(3, wo_ref[:HD].astype(F32), wo_ref[HD:].astype(F32))
     codes = codes_ref[...].astype(F32)
     other = jnp.where(first, codes[1:2], codes[0:1])
     row = lax.broadcasted_iota(jnp.int32, (HD, HD), 0)
-    give_ref[:, 4 * HD :] = jnp.where(row == 0, other[:, :HD], other[:, HD:]).astype(BF16)
+    give_ref[:, 3 * HD :] = jnp.where(row == 0, other[:, :HD], other[:, HD:]).astype(BF16)
+    for p in range(3):
+        cols = slice(HD * p, HD * p + HD)
+        left = w_ref[p, :, :HD].astype(F32)
+        right = w_ref[p, :, HD:].astype(F32)
+        mine_ref[:, cols] = jnp.where(first, left, right).astype(BF16)
+        give_ref[:, cols] = jnp.where(first, right, left).astype(BF16)
 
 
 def local_kernel(
@@ -105,7 +102,7 @@
     value = qkv[:, 2 * HD :]
     codes = codes_ref[...].astype(F32)
     own_codes = jnp.where(first, codes[0:1], codes[1:2])
-    got = got_ref[0:8, 4 * HD :].astype(F32)
+    got = got_ref[0:8, 3 * HD :].astype(F32)
     sib_codes = jnp.concatenate([got[0:1], got[1:2]], axis=1)
     codes = jnp.concatenate(
         [jnp.where(first, own_codes, sib_codes), jnp.where(first, sib_codes, own_codes)], axis=1
@@ -243,28 +240,32 @@
     meta = jnp.stack([z, c]).astype(jnp.int32)
     codes = beta_codes.T
 
+    turned = [
+        ((i * 2 + k) * heads + j, (j * 2 + k) * heads + i)
+        for i in range(chips)
+        for k in range(2)
+        for j in range(heads)
+    ]
+    wo = lax.ppermute(w_out, ("z", "c", "h"), turned)
     give, mine = call(
         pack_kernel,
         (meta,),
-        (w_qkv, w_out, codes),
-        [((HD, 5 * HD), BF16), ((HD, 4 * HD), BF16)],
+        (w_qkv, codes),
+        [((HD, 4 * HD), BF16), ((HD, 3 * HD), BF16)],
         1 << 20,
     )
     got = swap(give)
     hidden_sib = swap(hidden_in)
 
-    def chip(cols, axis):
-        a, b = mine[:, cols], got[:, cols]
-        return jnp.concatenate([jnp.where(first, a, b), jnp.where(first, b, a)], axis=axis)
-
-    turned = [(i * heads + j, j * heads + i) for i in range(chips) for j in range(heads)]
-    wo = lax.ppermute(chip(slice(3 * HD, 4 * HD), 1), ("z", "h"), turned)
-    wo = jnp.concatenate([wo[:, :HD], wo[:, HD:]], axis=0)
+    other = got[:, : 3 * HD]
+    w_chip = jnp.concatenate(
+        [jnp.where(first, mine, other), jnp.where(first, other, mine)], axis=0
+    )
     both = jnp.concatenate(
-        [to_f16(chip(slice(0, 3 * HD), 0), W_SCALE), to_f16(wo, WO_SCALE)], axis=1
+        [to_f16(w_chip, W_SCALE), to_f16(wo, WO_SCALE)], axis=1
     )
     both = lax.all_gather(both, "z", axis=0, tiled=True)
-    w_all = from_f16(both[:, : 3 * HD], W_SCALE)
+    w_all, wo_all = from_f16(both[:, : 3 * HD], W_SCALE), both[:, 3 * HD :]
 
     def project(hid):
         return jnp.dot(hid, w_all, preferred_element_type=F32).astype(BF16)
@@ -279,6 +280,14 @@
     one = ahead(tl16, 1)
     (two,) = call(pair_kernel, (), (tl, one), [((HD, 2 * HD), BF16)], 1 << 26)
     two = ahead(two, 2)
+    wo_all, _ = lax.optimization_barrier((wo_all, one))
+    wo_all = wo_all.reshape(chips, 2, HD, HD)
+    wo_keep = from_f16(jnp.where(first, wo_all[:, 0], wo_all[:, 1]), WO_SCALE)
+    wo_sent = from_f16(jnp.where(first, wo_all[:, 1], wo_all[:, 0]), WO_SCALE)
+    wo_got = swap(wo_sent)
+    wo_cols = jnp.concatenate(
+        [jnp.where(first, wo_keep, wo_got), jnp.where(first, wo_got, wo_keep)], axis=2
+    )
     pre, four_t, four_l = call(
         window_kernel,
         (),
@@ -307,11 +316,9 @@
         [((TOK, HD), BF16)],
         1 << 28,
     )
-    normed_all = from_f16(lax.all_gather(to_f16(normed, N_SCALE), "h", axis=0), N_SCALE)
-    wo_cols = from_f16(both[:, 3 * HD :], WO_SCALE).reshape(chips, 2, HD, HD)
-    wo_cols = wo_cols.transpose(0, 2, 1, 3).reshape(chips, HD, 2 * HD)
-
+    normed_all = lax.all_gather(to_f16(normed, N_SCALE), "h", axis=0)
     def output(rows):
+        rows = from_f16(rows, N_SCALE)
         return jnp.einsum("htf,hfn->tn", rows, wo_cols, preferred_element_type=F32)
 
     sent = swap(output(normed_all[:, :half]))

time: 164 us -> 162 us (0.988)
  blocking collectives: 95.1 us -> 92.2 us
  starting transfers between devices: 45.2 us -> 47.2 us
    all_gather x1, blocking collectives: 70.4 us -> 68 us  [per_device(): both = lax.all_gather(both, 'z', axis=0, tiled=True)]
    convert_element_type x2 -> x1, other arithmetic: 1.94 us -> 0.23 us  [from_f16(): return (value.astype(F32) * (1.0 / scale)).astype(BF16)]
    ppermute x3 -> x4, starting transfers between devices: 27.9 us -> 27.9 us  [swap(): return lax.ppermute(value, 'c', [(0, 1), (1, 0)])]
  transfers between devices with their start and end apart: 7 -> 8, of which waited for: 2 -> 2; matrix products, arithmetic and copies ran while one was open for 3% -> 3% of each run, Pallas kernels for 0% -> 1%
where the time goes in v8:
time: 162 us; the launch traced here: 161 us
  blocking collectives  92.2 us (57%)
  starting transfers between devices  47.2 us (29%)
  Pallas kernels  8.27 us (5%)
  matrix products  4.09 us (3%)
  local copies, waits for them, and re-layouts  3.72 us (2%)
  other arithmetic  2.43 us (2%)
  waiting for transfers between devices  2.28 us (1%)
    all_gather x1, blocking collectives, per_device(): both = lax.all_gather(both, 'z', axis=0, tiled=True)  68 us
    ppermute x4, starting transfers between devices, swap(): return lax.ppermute(value, 'c', [(0, 1), (1, 0)])  27.9 us
    all_gather x1, blocking collectives, per_device(): normed_all = lax.all_gather(to_f16(normed, N_SCALE), 'h', axis=0)  24.2 us
    ppermute x3, starting transfers between devices, ahead(): lax.ppermute(value, 'z', [(i, i + steps) for i in range(chips - steps)])  17.8 us
    pallas_call x5, Pallas kernels, call(): pl.pallas_call(kernel, out_shape=tuple((jax.ShapeDtypeStruct(s, d) for s,...  8.27 us
  transfers between devices with their start and end apart: 8, of which 2 were waited for; matrix products, arithmetic and copies ran while one was open for 3% of the time, Pallas kernels for 1%

profile of v8, /device:TPU:1, one launch (start us, length us, event | category | flops | bytes accessed | tf_op | source)
XLA Modules:
  0.0 161.1 jit_solution(6167117911171312758)
XLA Ops:
  0.1 0.9 copy-done
  1.0 0.7 copy-done.1
  2.3 8.8 %collective-permute-start.4 = (bf16[128,512]{1,0:T(8,128)(2,1)S(1)}, bf16[128,512]{1,0:T(8,128)(2,1)S(1)}, u32[]{:S(2)}, u32[]{:S(2)}) collective-permute-start(bf16[128,512]{1,0:T(8,128)(2,1)S(1)} %get-tuple-element.24), channel_id=1, source_target_pairs={{0,16},{16,0},{1,17},{17,1},{2,18},{18,2},{3,19},{19,3},{4,20},{20... | collective-permute-start | bytes 393224 | tf_op jit(solution)/shard_map/ppermute | solution.py:217
  11.1 1.5 collective-permute-start.5
  12.6 1.9 %collective-permute-start.6 = (bf16[256,4096]{1,0:T(8,128)(2,1)}, bf16[256,4096]{1,0:T(8,128)(2,1)S(1)}, u32[]{:S(2)}, u32[]{:S(2)}) collective-permute-start(bf16[256,4096]{1,0:T(8,128)(2,1)} %param.7), channel_id=1, source_target_pairs={{0,16},{16,0},{1,17},{17,1},{2,18},{18,2},{3,19},{19,3},{4,20},{20... | collective-permute-start | bytes 6291464 | tf_op jit(solution)/shard_map/ppermute | solution.py:217
  14.5 0.7 and_select_fusion
  15.4 68.0 %all-gather.3 = f16[4096,512]{1,0:T(8,128)(2,1)S(1)} all-gather(f16[256,512]{1,0:T(8,128)(2,1)S(1)} %pad_maximum_fusion.3), channel_id=1, replica_groups=mesh['z'=16,'c'=2,'h'=16] {'z'}, dimensions={0}, use_global_device_ids=true | all-gather | bytes 4456448 | tf_op jit(solution)/shard_map/all_gather | solution.py:267
  83.4 1.3 fusion.6.own_ref
  84.7 0.7 copy-done.4
  85.3 1.3 fusion.7.sib_ref
  86.6 5.4 %shard_map.56 = (f32[128,256]{1,0:T(8,128)S(1)}, bf16[128,256]{1,0:T(8,128)(2,1)S(1)}, f32[2,512,128]{2,1,0:T(8,128)S(1)}) custom-call(s32[2]{0:T(128)S(1)} %pad_add_fusion.meta_ref, s32[9]{0:T(128)S(1)} %copy-done.3, bf16[256,384]{1,0:T(8,128)(2,1)S(1)} %fusion.6.own_ref, bf16[256,384]{1,0:T(8,128)(2,1)S(1)} %fusion.7.sib_ref, s32[2,256]{1,0:T(2,128)S(1)} %bitcast.54, ...), custom_call_target="tpu_custom_call" | custom-call | flops 3221225472 | bytes 1048576 | tf_op jit(solution)/shard_map/pallas_call | solution.py:206
  92.0 2.8 %collective-permute-start.7 = (bf16[128,256]{1,0:T(8,128)(2,1)S(1)}, bf16[128,256]{1,0:T(8,128)(2,1)S(1)}, u32[]{:S(2)}, u32[]{:S(2)}) collective-permute-start(bf16[128,256]{1,0:T(8,128)(2,1)S(1)} %get-tuple-element.26), channel_id=1, source_target_pairs={{0,32},{32,64},{64,96},{96,128},{128,160},{160,192},{192,224},{224... | collective-permute-start | bytes 196616 | tf_op jit(solution)/shard_map/ppermute | solution.py:222
  95.0 1.1 collective-permute-done.7.one_ref
  96.3 4.9 %collective-permute-start.8 = (bf16[128,256]{1,0:T(8,128)(2,1)S(1)}, bf16[128,256]{1,0:T(8,128)(2,1)S(1)}, u32[]{:S(2)}, u32[]{:S(2)}) collective-permute-start(bf16[128,256]{1,0:T(8,128)(2,1)S(1)} %shard_map.57), channel_id=1, source_target_pairs={{0,64},{32,96},{64,128},{96,160},{128,192},{160,224},{192,256},{22... | collective-permute-start | bytes 196616 | tf_op jit(solution)/shard_map/ppermute | solution.py:222
  101.2 0.6 compare_reduce_fusion
  102.5 1.4 slice.33
  103.9 1.0 shard_map.58
  105.0 10.2 %collective-permute-start.9 = (bf16[128,128]{1,0:T(8,128)(2,1)}, bf16[128,128]{1,0:T(8,128)(2,1)S(1)}, u32[]{:S(2)}, u32[]{:S(2)}) collective-permute-start(bf16[128,128]{1,0:T(8,128)(2,1)} %get-tuple-element.28), channel_id=1, source_target_pairs={{0,128},{32,160},{64,192},{96,224},{128,256},{160,288},{192,320},{... | collective-permute-start | bytes 98312 | tf_op jit(solution)/shard_map/ppermute | solution.py:222
  115.5 10.5 %collective-permute-start.10 = (bf16[16,128,128]{2,1,0:T(8,128)(2,1)S(1)}, bf16[16,128,128]{2,1,0:T(8,128)(2,1)S(1)}, u32[]{:S(2)}, u32[]{:S(2)}) collective-permute-start(bf16[16,128,128]{2,1,0:T(8,128)(2,1)S(1)} %fusion.13), channel_id=1, source_target_pairs={{0,16},{16,0},{1,17},{17,1},{2,18},{18,2},{3,19},{19,3},{4,20},{20... | collective-permute-start | bytes 1572872 | tf_op jit(solution)/shard_map/ppermute | solution.py:217
  126.0 1.1 shard_map.59
  127.1 24.2 %all-gather.4 = f16[8192,128]{1,0:T(8,128)(2,1)S(1)} all-gather(f16[512,128]{1,0:T(8,128)(2,1)S(1)} %multiply_convert_fusion.18), channel_id=2, replica_groups=mesh['z'=16,'c'=2,'h'=16] {'h'}, dimensions={0}, use_global_device_ids=true | all-gather | bytes 2228224 | tf_op jit(solution)/shard_map/all_gather | solution.py:319
  152.2 6.7 %collective-permute-start.11 = (f32[256,256]{1,0:T(8,128)S(1)}, f32[256,256]{1,0:T(8,128)S(1)}, u32[]{:S(2)}, u32[]{:S(2)}) collective-permute-start(f32[256,256]{1,0:T(8,128)S(1)} %convolution_bitcast_fusion.1), channel_id=1, source_target_pairs={{0,16},{16,0},{1,17},{17,1},{2,18},{18,2},{3,19},{19,3},{4,20},{20... | collective-permute-start | bytes 786440 | tf_op jit(solution)/shard_map/ppermute | solution.py:217
  158.9 1.1 collective-permute-done.11
  160.0 1.1 fusion.5
  (30 shorter events, 2.4 us)
Async XLA Ops:
  0.1 0.9 copy-start
  1.0 0.7 copy-start.1
  2.3 12.9 %collective-permute-start.4 = (bf16[128,512]{1,0:T(8,128)(2,1)S(1)}, bf16[128,512]{1,0:T(8,128)(2,1)S(1)}, u32[]{:S(2)}, u32[]{:S(2)}) collective-permute-start(bf16[128,512]{1,0:T(8,128)(2,1)S(1)} %get-tuple-element.24), channel_id=1, source_target_pairs={{0,16},{16,0},{1,17},{17,1},{2,18},{18,2},{3,19},{19,3},{4,20},{20... | collective-permute-start | bytes 393224 | tf_op jit(solution)/shard_map/ppermute | solution.py:217
  11.1 4.1 %collective-permute-start.5 = (bf16[256,128]{1,0:T(8,128)(2,1)}, bf16[256,128]{1,0:T(8,128)(2,1)S(1)}, u32[]{:S(2)}, u32[]{:S(2)}) collective-permute-start(bf16[256,128]{1,0:T(8,128)(2,1)} %param.11), channel_id=1, source_target_pairs={{0,0},{1,32},{2,64},{3,96},{4,128},{5,160},{6,192},{7,224},{8,256}... | collective-permute-start | bytes 196616 | tf_op jit(solution)/shard_map/ppermute | solution.py:249
  12.6 72.1 %collective-permute-start.6 = (bf16[256,4096]{1,0:T(8,128)(2,1)}, bf16[256,4096]{1,0:T(8,128)(2,1)S(1)}, u32[]{:S(2)}, u32[]{:S(2)}) collective-permute-start(bf16[256,4096]{1,0:T(8,128)(2,1)} %param.7), channel_id=1, source_target_pairs={{0,16},{16,0},{1,17},{17,1},{2,18},{18,2},{3,19},{19,3},{4,20},{20... | collective-permute-start | bytes 6291464 | tf_op jit(solution)/shard_map/ppermute | solution.py:217
  15.4 68.0 %copy-start.5 = (bf16[256,4096]{1,0:T(8,128)(2,1)S(1)}, bf16[256,4096]{1,0:T(8,128)(2,1)}, u32[]{:S(2)}) copy-start(bf16[256,4096]{1,0:T(8,128)(2,1)} %param.7) | copy-start | bytes 6291460
  83.4 2.0 %copy-start.4 = (f16[4096,512]{1,0:T(8,128)(2,1)}, f16[4096,512]{1,0:T(8,128)(2,1)S(1)}, u32[]{:S(2)}) copy-start(f16[4096,512]{1,0:T(8,128)(2,1)S(1)} %all-gather.3) | copy-start | bytes 12582916
  84.6 2.0 %copy-start.2 = (s32[256,2]{0,1:T(2,128)S(1)}, s32[256,2]{0,1:T(2,128)}, u32[]{:S(2)}) copy-start(s32[256,2]{0,1:T(2,128)} %param.10) | copy-start | bytes 6148
  84.7 2.0 %copy-start.3 = (s32[9]{0:T(128)S(1)}, s32[9]{0:T(128)}, u32[]{:S(2)}) copy-start(s32[9]{0:T(128)} %ds_ref.1) | copy-start | bytes 112
  92.0 4.1 %collective-permute-start.7 = (bf16[128,256]{1,0:T(8,128)(2,1)S(1)}, bf16[128,256]{1,0:T(8,128)(2,1)S(1)}, u32[]{:S(2)}, u32[]{:S(2)}) collective-permute-start(bf16[128,256]{1,0:T(8,128)(2,1)S(1)} %get-tuple-element.26), channel_id=1, source_target_pairs={{0,32},{32,64},{64,96},{96,128},{128,160},{160,192},{192,224},{224... | collective-permute-start | bytes 196616 | tf_op jit(solution)/shard_map/ppermute | solution.py:222
  96.3 7.6 %collective-permute-start.8 = (bf16[128,256]{1,0:T(8,128)(2,1)S(1)}, bf16[128,256]{1,0:T(8,128)(2,1)S(1)}, u32[]{:S(2)}, u32[]{:S(2)}) collective-permute-start(bf16[128,256]{1,0:T(8,128)(2,1)S(1)} %shard_map.57), channel_id=1, source_target_pairs={{0,64},{32,96},{64,128},{96,160},{128,192},{160,224},{192,256},{22... | collective-permute-start | bytes 196616 | tf_op jit(solution)/shard_map/ppermute | solution.py:222
  105.0 21.0 %collective-permute-start.9 = (bf16[128,128]{1,0:T(8,128)(2,1)}, bf16[128,128]{1,0:T(8,128)(2,1)S(1)}, u32[]{:S(2)}, u32[]{:S(2)}) collective-permute-start(bf16[128,128]{1,0:T(8,128)(2,1)} %get-tuple-element.28), channel_id=1, source_target_pairs={{0,128},{32,160},{64,192},{96,224},{128,256},{160,288},{192,320},{... | collective-permute-start | bytes 98312 | tf_op jit(solution)/shard_map/ppermute | solution.py:222
  115.5 35.8 %collective-permute-start.10 = (bf16[16,128,128]{2,1,0:T(8,128)(2,1)S(1)}, bf16[16,128,128]{2,1,0:T(8,128)(2,1)S(1)}, u32[]{:S(2)}, u32[]{:S(2)}) collective-permute-start(bf16[16,128,128]{2,1,0:T(8,128)(2,1)S(1)} %fusion.13), channel_id=1, source_target_pairs={{0,16},{16,0},{1,17},{17,1},{2,18},{18,2},{3,19},{19,3},{4,20},{20... | collective-permute-start | bytes 1572872 | tf_op jit(solution)/shard_map/ppermute | solution.py:217
  152.2 7.8 %collective-permute-start.11 = (f32[256,256]{1,0:T(8,128)S(1)}, f32[256,256]{1,0:T(8,128)S(1)}, u32[]{:S(2)}, u32[]{:S(2)}) collective-permute-start(f32[256,256]{1,0:T(8,128)S(1)} %convolution_bitcast_fusion.1), channel_id=1, source_target_pairs={{0,16},{16,0},{1,17},{17,1},{2,18},{18,2},{3,19},{19,3},{4,20},{20... | collective-permute-start | bytes 786440 | tf_op jit(solution)/shard_map/ppermute | solution.py:217

commit v9 on v8

--- a/solution.py
+++ b/solution.py
@@ -1,3 +1,5 @@
+import functools
+
 import jax
 import jax.numpy as jnp
 from jax import lax
@@ -10,7 +12,9 @@
 BF16 = jnp.bfloat16
 F16 = jnp.float16
 HD = 128
-TOK = 512
+VMEM_LIMIT = 12 << 20
+TOK_BITS = 9
+TOK = 1 << TOK_BITS
 W_SCALE = 2.0**19
 WO_SCALE = 2.0**18
 N_SCALE = 2.0**12
@@ -91,9 +95,21 @@
         give_ref[:, cols] = jnp.where(first, right, left).astype(BF16)
 
 
+def far_reach(ds_ref, chips):
+    reach = jnp.int32(0)
+    for z in range(8, chips):
+        since = jnp.int32(0)
+        for j in range(ds_ref.shape[0]):
+            pos = ds_ref[j]
+            since = jnp.where(pos < z * TOK, jnp.maximum(since, pos >> TOK_BITS), since)
+        reach = jnp.maximum(reach, (z - since > 7).astype(jnp.int32))
+    return reach
+
+
 def local_kernel(
-    meta_ref, ds_ref, own_ref, sib_ref, codes_ref, got_ref, tl_ref, tl16_ref, b_ref
+    chips, meta_ref, ds_ref, own_ref, sib_ref, codes_ref, got_ref, tl_ref, tl16_ref, b_ref, far_ref
 ):
+    far_ref[0] = far_reach(ds_ref, chips)
     first = meta_ref[1] == 0
     half = TOK // 2
     qkv = in_order(first, own_ref[...].astype(F32), sib_ref[...].astype(F32))
@@ -208,7 +224,7 @@
         out_shape=tuple(jax.ShapeDtypeStruct(s, d) for s, d in outs),
         in_specs=[SMEM] * len(scalars) + [VMEM] * len(arrays),
         out_specs=(VMEM,) * len(outs),
-        compiler_params=pltpu.CompilerParams(vmem_limit_bytes=16 << 20),
+        compiler_params=pltpu.CompilerParams(vmem_limit_bytes=VMEM_LIMIT),
         cost_estimate=pl.CostEstimate(flops=flops, bytes_accessed=1 << 20, transcendentals=0),
     )(*scalars, *arrays)
 
@@ -270,13 +286,19 @@
     def project(hid):
         return jnp.dot(hid, w_all, preferred_element_type=F32).astype(BF16)
 
-    tl, tl16, b = call(
-        local_kernel,
-        (meta, doc_starts),
-        (project(hidden_in), project(hidden_sib), codes, got),
-        [((HD, 2 * HD), F32), ((HD, 2 * HD), BF16), ((2, TOK, HD), F32)],
-        3 << 30,
-    )
+    tl, tl16, b, far = pl.pallas_call(
+        functools.partial(local_kernel, chips),
+        out_shape=(
+            jax.ShapeDtypeStruct((HD, 2 * HD), F32),
+            jax.ShapeDtypeStruct((HD, 2 * HD), BF16),
+            jax.ShapeDtypeStruct((2, TOK, HD), F32),
+            jax.ShapeDtypeStruct((1,), jnp.int32),
+        ),
+        in_specs=[SMEM, SMEM, VMEM, VMEM, VMEM, VMEM],
+        out_specs=(VMEM, VMEM, VMEM, SMEM),
+        compiler_params=pltpu.CompilerParams(vmem_limit_bytes=VMEM_LIMIT),
+        cost_estimate=pl.CostEstimate(flops=3 << 30, bytes_accessed=1 << 20, transcendentals=0),
+    )(meta, doc_starts, project(hidden_in), project(hidden_sib), codes, got)
     one = ahead(tl16, 1)
     (two,) = call(pair_kernel, (), (tl, one), [((HD, 2 * HD), BF16)], 1 << 26)
     two = ahead(two, 2)
@@ -296,18 +318,13 @@
         1 << 26,
     )
 
-    here = jnp.arange(chips, dtype=jnp.int32)[:, None]
-    starts = doc_starts[None, :]
-    since = jnp.max(jnp.where(starts < here * TOK, starts // TOK, 0), axis=1)
-    reach_back = jnp.any(here[:, 0] - since > 7)
-
     def fetch_far(t, add):
         eight_t, eight_l, twelve = ahead(t, 8), ahead(add, 8), ahead(add, 12)
         state = jnp.dot(eight_t, twelve, preferred_element_type=F32) + eight_l.astype(F32)
         return jnp.dot(ahead(t, 4).astype(F32), state, precision=lax.Precision.HIGHEST)
 
     extra = lax.cond(
-        reach_back, fetch_far, lambda t, add: jnp.zeros((HD, HD), F32), four_t, four_l
+        far[0] > 0, fetch_far, lambda t, add: jnp.zeros((HD, HD), F32), four_t, four_l
     )
     (normed,) = call(
         finish_kernel,

time: 162 us -> 156 us (0.963)
  blocking collectives: 92.2 us -> 89.8 us
  local copies, waits for them, and re-layouts: 3.72 us -> 1.84 us
    pallas_call x0 -> x1, Pallas kernels: none -> 5.95 us  [per_device(): pl.pallas_call(functools.partial(local_kernel, chips), out_shape=(jax.Sha...]
    pallas_call x5 -> x4, Pallas kernels: 8.27 us -> 2.88 us  [call(): pl.pallas_call(kernel, out_shape=tuple((jax.ShapeDtypeStruct(s, d) for s,...]
    ppermute x3, starting transfers between devices: 17.8 us -> 15.2 us  [ahead(): lax.ppermute(value, 'z', [(i, i + steps) for i in range(chips - steps)])]
  transfers between devices with their start and end apart: 8 -> 8, of which waited for: 2 -> 3; matrix products, arithmetic and copies ran while one was open for 3% -> 1% of each run, Pallas kernels for 1% -> 1%
where the time goes in v9:
time: 156 us; the launch traced here: 155 us
  blocking collectives  89.8 us (58%)
  starting transfers between devices  45.7 us (29%)
  Pallas kernels  8.82 us (6%)
  matrix products  4.08 us (3%)
  waiting for transfers between devices  2.91 us (2%)
  local copies, waits for them, and re-layouts  1.84 us (1%)
    all_gather x1, blocking collectives, per_device(): both = lax.all_gather(both, 'z', axis=0, tiled=True)  67.2 us
    ppermute x4, starting transfers between devices, swap(): return lax.ppermute(value, 'c', [(0, 1), (1, 0)])  29 us
    all_gather x1, blocking collectives, per_device(): normed_all = lax.all_gather(to_f16(normed, N_SCALE), 'h', axis=0)  22.6 us
    ppermute x3, starting transfers between devices, ahead(): lax.ppermute(value, 'z', [(i, i + steps) for i in range(chips - steps)])  15.2 us
    pallas_call x1, Pallas kernels, per_device(): pl.pallas_call(functools.partial(local_kernel, chips), out_shape=(jax.Sha...  5.95 us
  transfers between devices with their start and end apart: 8, of which 3 were waited for; matrix products, arithmetic and copies ran while one was open for 1% of the time, Pallas kernels for 1%

profile of v9, /device:TPU:1, one launch (start us, length us, event | category | flops | bytes accessed | tf_op | source)
XLA Modules:
  0.0 154.9 jit_solution(9028514404120000256)
XLA Ops:
  0.0 1.5 collective-permute-start.5
  1.6 0.9 copy-done
  2.5 0.7 copy-done.1
  3.2 0.6 shard_map.55
  3.8 8.8 %collective-permute-start.4 = (bf16[128,512]{1,0:T(8,128)(2,1)S(1)}, bf16[128,512]{1,0:T(8,128)(2,1)S(1)}, u32[]{:S(2)}, u32[]{:S(2)}) collective-permute-start(bf16[128,512]{1,0:T(8,128)(2,1)S(1)} %get-tuple-element.25), channel_id=1, source_target_pairs={{0,16},{16,0},{1,17},{17,1},{2,18},{18,2},{3,19},{19,3},{4,20},{20... | collective-permute-start | bytes 393224 | tf_op jit(solution)/shard_map/ppermute | solution.py:233
  12.6 1.9 %collective-permute-start.6 = (bf16[256,4096]{1,0:T(8,128)(2,1)}, bf16[256,4096]{1,0:T(8,128)(2,1)S(1)}, u32[]{:S(2)}, u32[]{:S(2)}) collective-permute-start(bf16[256,4096]{1,0:T(8,128)(2,1)} %param.7), channel_id=1, source_target_pairs={{0,16},{16,0},{1,17},{17,1},{2,18},{18,2},{3,19},{19,3},{4,20},{20... | collective-permute-start | bytes 6291464 | tf_op jit(solution)/shard_map/ppermute | solution.py:233
  14.7 67.2 %all-gather.3 = f16[4096,512]{1,0:T(8,128)(2,1)S(1)} all-gather(f16[256,512]{1,0:T(8,128)(2,1)S(1)} %pad_maximum_fusion.3), channel_id=1, replica_groups=mesh['z'=16,'c'=2,'h'=16] {'z'}, dimensions={0}, use_global_device_ids=true | all-gather | bytes 4456448 | tf_op jit(solution)/shard_map/all_gather | solution.py:283
  82.0 1.3 fusion.6.own_ref
  83.3 1.3 fusion.7.sib_ref
  84.6 5.9 %shard_map.56 = (f32[128,256]{1,0:T(8,128)S(1)}, bf16[128,256]{1,0:T(8,128)(2,1)S(1)}, f32[2,512,128]{2,1,0:T(8,128)S(1)}, s32[1]{0:T(128)}) custom-call(s32[2]{0:T(128)S(1)} %pad_add_fusion.meta_ref, s32[9]{0:T(128)S(1)} %copy-done.3, bf16[256,384]{1,0:T(8,128)(2,1)S(1)} %fusion.6.own_ref, bf16[256,384]{1,0:T(8,128)(2,1)S(1)} %fusion.7.sib_ref, ...), custom_call_target="tpu_custom_call" | custom-call | flops 3221225472 | bytes 1048576 | tf_op jit(solution)/shard_map/pallas_call | solution.py:289
  90.5 2.1 %collective-permute-start.7 = (bf16[128,256]{1,0:T(8,128)(2,1)S(1)}, bf16[128,256]{1,0:T(8,128)(2,1)S(1)}, u32[]{:S(2)}, u32[]{:S(2)}) collective-permute-start(bf16[128,256]{1,0:T(8,128)(2,1)S(1)} %get-tuple-element.27), channel_id=1, source_target_pairs={{0,32},{32,64},{64,96},{96,128},{128,160},{160,192},{192,224},{224... | collective-permute-start | bytes 196616 | tf_op jit(solution)/shard_map/ppermute | solution.py:238
  92.6 1.3 collective-permute-done.7.one_ref
  94.1 3.4 %collective-permute-start.8 = (bf16[128,256]{1,0:T(8,128)(2,1)S(1)}, bf16[128,256]{1,0:T(8,128)(2,1)S(1)}, u32[]{:S(2)}, u32[]{:S(2)}) collective-permute-start(bf16[128,256]{1,0:T(8,128)(2,1)S(1)} %shard_map.57), channel_id=1, source_target_pairs={{0,64},{32,96},{64,128},{96,160},{128,192},{160,224},{192,256},{22... | collective-permute-start | bytes 196616 | tf_op jit(solution)/shard_map/ppermute | solution.py:238
  98.4 0.4 collective-permute-done.8.two_ref
  98.9 1.0 shard_map.58
  99.9 9.7 %collective-permute-start.9 = (bf16[128,128]{1,0:T(8,128)(2,1)}, bf16[128,128]{1,0:T(8,128)(2,1)S(1)}, u32[]{:S(2)}, u32[]{:S(2)}) collective-permute-start(bf16[128,128]{1,0:T(8,128)(2,1)} %get-tuple-element.29), channel_id=1, source_target_pairs={{0,128},{32,160},{64,192},{96,224},{128,256},{160,288},{192,320},{... | collective-permute-start | bytes 98312 | tf_op jit(solution)/shard_map/ppermute | solution.py:238
  109.9 12.4 %collective-permute-start.10 = (bf16[16,128,128]{2,1,0:T(8,128)(2,1)S(1)}, bf16[16,128,128]{2,1,0:T(8,128)(2,1)S(1)}, u32[]{:S(2)}, u32[]{:S(2)}) collective-permute-start(bf16[16,128,128]{2,1,0:T(8,128)(2,1)S(1)} %fusion.13), channel_id=1, source_target_pairs={{0,16},{16,0},{1,17},{17,1},{2,18},{18,2},{3,19},{19,3},{4,20},{20... | collective-permute-start | bytes 1572872 | tf_op jit(solution)/shard_map/ppermute | solution.py:233
  122.2 1.1 shard_map.59
  123.4 22.6 %all-gather.4 = f16[8192,128]{1,0:T(8,128)(2,1)S(1)} all-gather(f16[512,128]{1,0:T(8,128)(2,1)S(1)} %multiply_convert_fusion.18), channel_id=2, replica_groups=mesh['z'=16,'c'=2,'h'=16] {'h'}, dimensions={0}, use_global_device_ids=true | all-gather | bytes 2228224 | tf_op jit(solution)/shard_map/all_gather | solution.py:336
  146.0 0.3 broadcast_select_fusion.1
  146.3 0.4 convolution_bitcast_fusion.1
  146.7 5.9 %collective-permute-start.11 = (f32[256,256]{1,0:T(8,128)S(1)}, f32[256,256]{1,0:T(8,128)S(1)}, u32[]{:S(2)}, u32[]{:S(2)}) collective-permute-start(f32[256,256]{1,0:T(8,128)S(1)} %convolution_bitcast_fusion.1), channel_id=1, source_target_pairs={{0,16},{16,0},{1,17},{17,1},{2,18},{18,2},{3,19},{19,3},{4,20},{20... | collective-permute-start | bytes 786440 | tf_op jit(solution)/shard_map/ppermute | solution.py:233
  152.7 1.1 collective-permute-done.11
  153.8 1.1 fusion.5
  (24 shorter events, 1.0 us)
Async XLA Ops:
  0.0 14.5 %collective-permute-start.5 = (bf16[256,128]{1,0:T(8,128)(2,1)}, bf16[256,128]{1,0:T(8,128)(2,1)S(1)}, u32[]{:S(2)}, u32[]{:S(2)}) collective-permute-start(bf16[256,128]{1,0:T(8,128)(2,1)} %param.11), channel_id=1, source_target_pairs={{0,0},{1,32},{2,64},{3,96},{4,128},{5,160},{6,192},{7,224},{8,256}... | collective-permute-start | bytes 196616 | tf_op jit(solution)/shard_map/ppermute | solution.py:265
  1.6 0.9 copy-start
  2.5 0.7 copy-start.1
  3.8 10.8 %collective-permute-start.4 = (bf16[128,512]{1,0:T(8,128)(2,1)S(1)}, bf16[128,512]{1,0:T(8,128)(2,1)S(1)}, u32[]{:S(2)}, u32[]{:S(2)}) collective-permute-start(bf16[128,512]{1,0:T(8,128)(2,1)S(1)} %get-tuple-element.25), channel_id=1, source_target_pairs={{0,16},{16,0},{1,17},{17,1},{2,18},{18,2},{3,19},{19,3},{4,20},{20... | collective-permute-start | bytes 393224 | tf_op jit(solution)/shard_map/ppermute | solution.py:233
  12.6 70.7 %collective-permute-start.6 = (bf16[256,4096]{1,0:T(8,128)(2,1)}, bf16[256,4096]{1,0:T(8,128)(2,1)S(1)}, u32[]{:S(2)}, u32[]{:S(2)}) collective-permute-start(bf16[256,4096]{1,0:T(8,128)(2,1)} %param.7), channel_id=1, source_target_pairs={{0,16},{16,0},{1,17},{17,1},{2,18},{18,2},{3,19},{19,3},{4,20},{20... | collective-permute-start | bytes 6291464 | tf_op jit(solution)/shard_map/ppermute | solution.py:233
  14.7 67.3 %copy-start.4 = (bf16[256,4096]{1,0:T(8,128)(2,1)S(1)}, bf16[256,4096]{1,0:T(8,128)(2,1)}, u32[]{:S(2)}) copy-start(bf16[256,4096]{1,0:T(8,128)(2,1)} %param.7) | copy-start | bytes 6291460
  83.3 1.3 copy-start.2
  83.3 1.3 copy-start.3
  90.5 3.4 %collective-permute-start.7 = (bf16[128,256]{1,0:T(8,128)(2,1)S(1)}, bf16[128,256]{1,0:T(8,128)(2,1)S(1)}, u32[]{:S(2)}, u32[]{:S(2)}) collective-permute-start(bf16[128,256]{1,0:T(8,128)(2,1)S(1)} %get-tuple-element.27), channel_id=1, source_target_pairs={{0,32},{32,64},{64,96},{96,128},{128,160},{160,192},{192,224},{224... | collective-permute-start | bytes 196616 | tf_op jit(solution)/shard_map/ppermute | solution.py:238
  94.1 4.7 %collective-permute-start.8 = (bf16[128,256]{1,0:T(8,128)(2,1)S(1)}, bf16[128,256]{1,0:T(8,128)(2,1)S(1)}, u32[]{:S(2)}, u32[]{:S(2)}) collective-permute-start(bf16[128,256]{1,0:T(8,128)(2,1)S(1)} %shard_map.57), channel_id=1, source_target_pairs={{0,64},{32,96},{64,128},{96,160},{128,192},{160,224},{192,256},{22... | collective-permute-start | bytes 196616 | tf_op jit(solution)/shard_map/ppermute | solution.py:238
  99.9 22.3 %collective-permute-start.9 = (bf16[128,128]{1,0:T(8,128)(2,1)}, bf16[128,128]{1,0:T(8,128)(2,1)S(1)}, u32[]{:S(2)}, u32[]{:S(2)}) collective-permute-start(bf16[128,128]{1,0:T(8,128)(2,1)} %get-tuple-element.29), channel_id=1, source_target_pairs={{0,128},{32,160},{64,192},{96,224},{128,256},{160,288},{192,320},{... | collective-permute-start | bytes 98312 | tf_op jit(solution)/shard_map/ppermute | solution.py:238
  109.9 36.1 %collective-permute-start.10 = (bf16[16,128,128]{2,1,0:T(8,128)(2,1)S(1)}, bf16[16,128,128]{2,1,0:T(8,128)(2,1)S(1)}, u32[]{:S(2)}, u32[]{:S(2)}) collective-permute-start(bf16[16,128,128]{2,1,0:T(8,128)(2,1)S(1)} %fusion.13), channel_id=1, source_target_pairs={{0,16},{16,0},{1,17},{17,1},{2,18},{18,2},{3,19},{19,3},{4,20},{20... | collective-permute-start | bytes 1572872 | tf_op jit(solution)/shard_map/ppermute | solution.py:233
  146.7 7.1 %collective-permute-start.11 = (f32[256,256]{1,0:T(8,128)S(1)}, f32[256,256]{1,0:T(8,128)S(1)}, u32[]{:S(2)}, u32[]{:S(2)}) collective-permute-start(f32[256,256]{1,0:T(8,128)S(1)} %convolution_bitcast_fusion.1), channel_id=1, source_target_pairs={{0,16},{16,0},{1,17},{17,1},{2,18},{18,2},{3,19},{19,3},{4,20},{20... | collective-permute-start | bytes 786440 | tf_op jit(solution)/shard_map/ppermute | solution.py:233

commit v10 on v9

--- a/solution.py
+++ b/solution.py
@@ -96,14 +96,12 @@
 
 
 def far_reach(ds_ref, chips):
-    reach = jnp.int32(0)
-    for z in range(8, chips):
-        since = jnp.int32(0)
-        for j in range(ds_ref.shape[0]):
-            pos = ds_ref[j]
-            since = jnp.where(pos < z * TOK, jnp.maximum(since, pos >> TOK_BITS), since)
-        reach = jnp.maximum(reach, (z - since > 7).astype(jnp.int32))
-    return reach
+    count = ds_ref.shape[0]
+    blocks = [ds_ref[j] >> TOK_BITS for j in range(count)]
+    gap = chips - 1 - blocks[count - 1]
+    for j in range(count - 1):
+        gap = jnp.maximum(gap, blocks[j + 1] - blocks[j])
+    return (gap > 7).astype(jnp.int32)
 
 
 def local_kernel(
@@ -302,7 +300,7 @@
     one = ahead(tl16, 1)
     (two,) = call(pair_kernel, (), (tl, one), [((HD, 2 * HD), BF16)], 1 << 26)
     two = ahead(two, 2)
-    wo_all, _ = lax.optimization_barrier((wo_all, one))
+    wo_all, _ = lax.optimization_barrier((wo_all, tl16))
     wo_all = wo_all.reshape(chips, 2, HD, HD)
     wo_keep = from_f16(jnp.where(first, wo_all[:, 0], wo_all[:, 1]), WO_SCALE)
     wo_sent = from_f16(jnp.where(first, wo_all[:, 1], wo_all[:, 0]), WO_SCALE)
@@ -339,7 +337,8 @@
         return jnp.einsum("htf,hfn->tn", rows, wo_cols, preferred_element_type=F32)
 
     sent = swap(output(normed_all[:, :half]))
-    return (output(normed_all[:, half:]) + sent).astype(BF16)
+    kept = lax.optimization_barrier(output(normed_all[:, half:]))
+    return (kept + sent).astype(BF16)
 
 
 def solution(mesh):

time: 156 us -> 155 us (level)
  transfers between devices with their start and end apart: 8 -> 8, of which waited for: 3 -> 3; matrix products, arithmetic and copies ran while one was open for 1% -> 2% of each run, Pallas kernels for 1% -> 1%
where the time goes in v10:
time: 155 us
  blocking collectives  89.9 us (58%)
  starting transfers between devices  45.6 us (29%)
  Pallas kernels  8.28 us (5%)
  matrix products  3.42 us (2%)
  waiting for transfers between devices  3.11 us (2%)
  local copies, waits for them, and re-layouts  1.84 us (1%)
    all_gather x1, blocking collectives, per_device(): both = lax.all_gather(both, 'z', axis=0, tiled=True)  67.2 us
    ppermute x4, starting transfers between devices, swap(): return lax.ppermute(value, 'c', [(0, 1), (1, 0)])  28.9 us
    all_gather x1, blocking collectives, per_device(): normed_all = lax.all_gather(to_f16(normed, N_SCALE), 'h', axis=0)  22.6 us
    ppermute x3, starting transfers between devices, ahead(): lax.ppermute(value, 'z', [(i, i + steps) for i in range(chips - steps)])  15.2 us
    pallas_call x1, Pallas kernels, per_device(): pl.pallas_call(functools.partial(local_kernel, chips), out_shape=(jax.Sha...  5.4 us
  transfers between devices with their start and end apart: 8, of which 3 were waited for; matrix products, arithmetic and copies ran while one was open for 2% of the time, Pallas kernels for 1%

profile of v10, /device:TPU:1, one launch (start us, length us, event | category | flops | bytes accessed | tf_op | source)
XLA Modules:
  0.0 154.6 jit_solution(9313983084963203416)
XLA Ops:
  0.0 1.5 collective-permute-start.5
  1.6 0.9 copy-done
  2.5 0.7 copy-done.1
  3.2 0.6 shard_map.55
  3.8 8.8 %collective-permute-start.4 = (bf16[128,512]{1,0:T(8,128)(2,1)S(1)}, bf16[128,512]{1,0:T(8,128)(2,1)S(1)}, u32[]{:S(2)}, u32[]{:S(2)}) collective-permute-start(bf16[128,512]{1,0:T(8,128)(2,1)S(1)} %get-tuple-element.25), channel_id=1, source_target_pairs={{0,16},{16,0},{1,17},{17,1},{2,18},{18,2},{3,19},{19,3},{4,20},{20... | collective-permute-start | bytes 393224 | tf_op jit(solution)/shard_map/ppermute | solution.py:231
  12.6 1.9 %collective-permute-start.6 = (bf16[256,4096]{1,0:T(8,128)(2,1)}, bf16[256,4096]{1,0:T(8,128)(2,1)S(1)}, u32[]{:S(2)}, u32[]{:S(2)}) collective-permute-start(bf16[256,4096]{1,0:T(8,128)(2,1)} %param.7), channel_id=1, source_target_pairs={{0,16},{16,0},{1,17},{17,1},{2,18},{18,2},{3,19},{19,3},{4,20},{20... | collective-permute-start | bytes 6291464 | tf_op jit(solution)/shard_map/ppermute | solution.py:231
  14.7 67.2 %all-gather.3 = f16[4096,512]{1,0:T(8,128)(2,1)S(1)} all-gather(f16[256,512]{1,0:T(8,128)(2,1)S(1)} %pad_maximum_fusion.3), channel_id=1, replica_groups=mesh['z'=16,'c'=2,'h'=16] {'z'}, dimensions={0}, use_global_device_ids=true | all-gather | bytes 4456448 | tf_op jit(solution)/shard_map/all_gather | solution.py:281
  82.0 1.3 fusion.4.own_ref
  83.3 1.3 fusion.5.sib_ref
  84.6 5.4 %shard_map.56 = (f32[128,256]{1,0:T(8,128)S(1)}, bf16[128,256]{1,0:T(8,128)(2,1)S(1)}, f32[2,512,128]{2,1,0:T(8,128)S(1)}, s32[1]{0:T(128)}) custom-call(s32[2]{0:T(128)S(1)} %pad_add_fusion.meta_ref, s32[9]{0:T(128)S(1)} %copy-done.3, bf16[256,384]{1,0:T(8,128)(2,1)S(1)} %fusion.4.own_ref, bf16[256,384]{1,0:T(8,128)(2,1)S(1)} %fusion.5.sib_ref, ...), custom_call_target="tpu_custom_call" | custom-call | flops 3221225472 | bytes 1048576 | tf_op jit(solution)/shard_map/pallas_call | solution.py:287
  90.0 2.1 %collective-permute-start.7 = (bf16[128,256]{1,0:T(8,128)(2,1)S(1)}, bf16[128,256]{1,0:T(8,128)(2,1)S(1)}, u32[]{:S(2)}, u32[]{:S(2)}) collective-permute-start(bf16[128,256]{1,0:T(8,128)(2,1)S(1)} %get-tuple-element.27), channel_id=1, source_target_pairs={{0,32},{32,64},{64,96},{96,128},{128,160},{160,192},{192,224},{224... | collective-permute-start | bytes 196616 | tf_op jit(solution)/shard_map/ppermute | solution.py:236
  92.1 1.3 collective-permute-done.7.one_ref
  93.6 3.4 %collective-permute-start.8 = (bf16[128,256]{1,0:T(8,128)(2,1)S(1)}, bf16[128,256]{1,0:T(8,128)(2,1)S(1)}, u32[]{:S(2)}, u32[]{:S(2)}) collective-permute-start(bf16[128,256]{1,0:T(8,128)(2,1)S(1)} %shard_map.57), channel_id=1, source_target_pairs={{0,64},{32,96},{64,128},{96,160},{128,192},{160,224},{192,256},{22... | collective-permute-start | bytes 196616 | tf_op jit(solution)/shard_map/ppermute | solution.py:236
  97.2 1.1 collective-permute-done.8.two_ref
  98.3 1.0 shard_map.58
  99.4 9.7 %collective-permute-start.9 = (bf16[128,128]{1,0:T(8,128)(2,1)}, bf16[128,128]{1,0:T(8,128)(2,1)S(1)}, u32[]{:S(2)}, u32[]{:S(2)}) collective-permute-start(bf16[128,128]{1,0:T(8,128)(2,1)} %get-tuple-element.29), channel_id=1, source_target_pairs={{0,128},{32,160},{64,192},{96,224},{128,256},{160,288},{192,320},{... | collective-permute-start | bytes 98312 | tf_op jit(solution)/shard_map/ppermute | solution.py:236
  110.0 12.3 %collective-permute-start.10 = (bf16[16,128,128]{2,1,0:T(8,128)(2,1)S(1)}, bf16[16,128,128]{2,1,0:T(8,128)(2,1)S(1)}, u32[]{:S(2)}, u32[]{:S(2)}) collective-permute-start(bf16[16,128,128]{2,1,0:T(8,128)(2,1)S(1)} %fusion.11), channel_id=1, source_target_pairs={{0,16},{16,0},{1,17},{17,1},{2,18},{18,2},{3,19},{19,3},{4,20},{20... | collective-permute-start | bytes 1572872 | tf_op jit(solution)/shard_map/ppermute | solution.py:231
  122.3 1.1 shard_map.59
  123.4 22.6 %all-gather.4 = f16[8192,128]{1,0:T(8,128)(2,1)S(1)} all-gather(f16[512,128]{1,0:T(8,128)(2,1)S(1)} %multiply_convert_fusion.18), channel_id=2, replica_groups=mesh['z'=16,'c'=2,'h'=16] {'h'}, dimensions={0}, use_global_device_ids=true | all-gather | bytes 2228224 | tf_op jit(solution)/shard_map/all_gather | solution.py:334
  146.4 0.4 convolution_bitcast_fusion.1
  146.8 5.9 %collective-permute-start.11 = (f32[256,256]{1,0:T(8,128)S(1)}, f32[256,256]{1,0:T(8,128)S(1)}, u32[]{:S(2)}, u32[]{:S(2)}) collective-permute-start(f32[256,256]{1,0:T(8,128)S(1)} %convolution_bitcast_fusion.1), channel_id=1, source_target_pairs={{0,16},{16,0},{1,17},{17,1},{2,18},{18,2},{3,19},{19,3},{4,20},{20... | collective-permute-start | bytes 786440 | tf_op jit(solution)/shard_map/ppermute | solution.py:231
  152.7 0.4 convolution_bitcast_fusion.2
  153.2 0.7 collective-permute-done.11
  153.9 0.7 add_convert_fusion
  (25 shorter events, 1.3 us)
Async XLA Ops:
  0.0 14.5 %collective-permute-start.5 = (bf16[256,128]{1,0:T(8,128)(2,1)}, bf16[256,128]{1,0:T(8,128)(2,1)S(1)}, u32[]{:S(2)}, u32[]{:S(2)}) collective-permute-start(bf16[256,128]{1,0:T(8,128)(2,1)} %param.11), channel_id=1, source_target_pairs={{0,0},{1,32},{2,64},{3,96},{4,128},{5,160},{6,192},{7,224},{8,256}... | collective-permute-start | bytes 196616 | tf_op jit(solution)/shard_map/ppermute | solution.py:263
  1.6 0.9 copy-start
  2.5 0.7 copy-start.1
  3.8 10.8 %collective-permute-start.4 = (bf16[128,512]{1,0:T(8,128)(2,1)S(1)}, bf16[128,512]{1,0:T(8,128)(2,1)S(1)}, u32[]{:S(2)}, u32[]{:S(2)}) collective-permute-start(bf16[128,512]{1,0:T(8,128)(2,1)S(1)} %get-tuple-element.25), channel_id=1, source_target_pairs={{0,16},{16,0},{1,17},{17,1},{2,18},{18,2},{3,19},{19,3},{4,20},{20... | collective-permute-start | bytes 393224 | tf_op jit(solution)/shard_map/ppermute | solution.py:231
  12.6 70.7 %collective-permute-start.6 = (bf16[256,4096]{1,0:T(8,128)(2,1)}, bf16[256,4096]{1,0:T(8,128)(2,1)S(1)}, u32[]{:S(2)}, u32[]{:S(2)}) collective-permute-start(bf16[256,4096]{1,0:T(8,128)(2,1)} %param.7), channel_id=1, source_target_pairs={{0,16},{16,0},{1,17},{17,1},{2,18},{18,2},{3,19},{19,3},{4,20},{20... | collective-permute-start | bytes 6291464 | tf_op jit(solution)/shard_map/ppermute | solution.py:231
  14.7 67.3 %copy-start.4 = (bf16[256,4096]{1,0:T(8,128)(2,1)S(1)}, bf16[256,4096]{1,0:T(8,128)(2,1)}, u32[]{:S(2)}) copy-start(bf16[256,4096]{1,0:T(8,128)(2,1)} %param.7) | copy-start | bytes 6291460
  83.3 1.3 copy-start.2
  83.3 1.3 copy-start.3
  90.0 3.4 %collective-permute-start.7 = (bf16[128,256]{1,0:T(8,128)(2,1)S(1)}, bf16[128,256]{1,0:T(8,128)(2,1)S(1)}, u32[]{:S(2)}, u32[]{:S(2)}) collective-permute-start(bf16[128,256]{1,0:T(8,128)(2,1)S(1)} %get-tuple-element.27), channel_id=1, source_target_pairs={{0,32},{32,64},{64,96},{96,128},{128,160},{160,192},{192,224},{224... | collective-permute-start | bytes 196616 | tf_op jit(solution)/shard_map/ppermute | solution.py:236
  93.6 4.7 %collective-permute-start.8 = (bf16[128,256]{1,0:T(8,128)(2,1)S(1)}, bf16[128,256]{1,0:T(8,128)(2,1)S(1)}, u32[]{:S(2)}, u32[]{:S(2)}) collective-permute-start(bf16[128,256]{1,0:T(8,128)(2,1)S(1)} %shard_map.57), channel_id=1, source_target_pairs={{0,64},{32,96},{64,128},{96,160},{128,192},{160,224},{192,256},{22... | collective-permute-start | bytes 196616 | tf_op jit(solution)/shard_map/ppermute | solution.py:236
  99.4 22.9 %collective-permute-start.9 = (bf16[128,128]{1,0:T(8,128)(2,1)}, bf16[128,128]{1,0:T(8,128)(2,1)S(1)}, u32[]{:S(2)}, u32[]{:S(2)}) collective-permute-start(bf16[128,128]{1,0:T(8,128)(2,1)} %get-tuple-element.29), channel_id=1, source_target_pairs={{0,128},{32,160},{64,192},{96,224},{128,256},{160,288},{192,320},{... | collective-permute-start | bytes 98312 | tf_op jit(solution)/shard_map/ppermute | solution.py:236
  110.0 36.1 %collective-permute-start.10 = (bf16[16,128,128]{2,1,0:T(8,128)(2,1)S(1)}, bf16[16,128,128]{2,1,0:T(8,128)(2,1)S(1)}, u32[]{:S(2)}, u32[]{:S(2)}) collective-permute-start(bf16[16,128,128]{2,1,0:T(8,128)(2,1)S(1)} %fusion.11), channel_id=1, source_target_pairs={{0,16},{16,0},{1,17},{17,1},{2,18},{18,2},{3,19},{19,3},{4,20},{20... | collective-permute-start | bytes 1572872 | tf_op jit(solution)/shard_map/ppermute | solution.py:231
  146.8 7.1 %collective-permute-start.11 = (f32[256,256]{1,0:T(8,128)S(1)}, f32[256,256]{1,0:T(8,128)S(1)}, u32[]{:S(2)}, u32[]{:S(2)}) collective-permute-start(f32[256,256]{1,0:T(8,128)S(1)} %convolution_bitcast_fusion.1), channel_id=1, source_target_pairs={{0,16},{16,0},{1,17},{17,1},{2,18},{18,2},{3,19},{19,3},{4,20},{20... | collective-permute-start | bytes 786440 | tf_op jit(solution)/shard_map/ppermute | solution.py:231

commit v11 on v10

--- a/solution.py
+++ b/solution.py
@@ -105,13 +105,23 @@
 
 
 def local_kernel(
-    chips, meta_ref, ds_ref, own_ref, sib_ref, codes_ref, got_ref, tl_ref, tl16_ref, b_ref, far_ref
+    chips,
+    meta_ref,
+    ds_ref,
+    own_ref,
+    sib_ref,
+    codes_ref,
+    got_ref,
+    tl_ref,
+    tl16_ref,
+    wu_ref,
+    kt_ref,
+    far_ref,
 ):
     far_ref[0] = far_reach(ds_ref, chips)
     first = meta_ref[1] == 0
     half = TOK // 2
     qkv = in_order(first, own_ref[...].astype(F32), sib_ref[...].astype(F32))
-    query = unit_rows(qkv[:, :HD])
     key = unit_rows(qkv[:, HD : 2 * HD])
     value = qkv[:, 2 * HD :]
     codes = codes_ref[...].astype(F32)
@@ -129,6 +139,7 @@
 
     key_s = split(key)
     key_t = jnp.transpose(key)
+    kt_ref[...] = key_t
     key_ts = split(key_t)
 
     def system(rows, cols):
@@ -169,8 +180,20 @@
     tl_ref[:, :HD] = last_keep * eye128 - tl[:, :HD]
     tl_ref[:, HD:] = tl[:, HD:]
     tl16_ref[...] = tl_ref[...].astype(BF16)
-
+    wu_ref[lo, :] = wu_lo
+    wu_ref[hi, :] = wu_hi
+
+
+def query_kernel(meta_ref, ds_ref, own_ref, sib_ref, kt_ref, wu_ref, b_ref):
+    first = meta_ref[1] == 0
+    half = TOK // 2
+    query = unit_rows(in_order(first, own_ref[:, :HD].astype(F32), sib_ref[:, :HD].astype(F32)))
+    doc_col, doc_row, prev_doc, _ = doc_info(meta_ref, ds_ref)
+    carry_in = (doc_col == prev_doc).astype(F32)
     query_s = split(query)
+    key_ts = split(kt_ref[...])
+    wu_s = split(wu_ref[...])
+    lo, hi = slice(0, half), slice(half, TOK)
 
     def probs(rows, cols):
         return masked_gram(query_s, key_ts, doc_col, doc_row, rows, cols, inclusive=True)
@@ -189,11 +212,17 @@
 
 
 def pair_kernel(tl_ref, one_ref, two_ref):
-    two_ref[...] = after(tl_ref[...], one_ref[...].astype(F32)).astype(BF16)
+    later = tl_ref[...]
+    hi, lo = split(later[:, :HD])
+    one = one_ref[...]
+    product = dot(jnp.concatenate([hi, lo], axis=1), jnp.concatenate([one, one], axis=0))
+    two_ref[:, :HD] = product[:, :HD].astype(BF16)
+    two_ref[:, HD:] = (product[:, HD:] + later[:, HD:]).astype(BF16)
 
 
 def window_kernel(tl_ref, one_ref, two_ref, pre_ref, four_t_ref, four_l_ref):
-    pre = after(one_ref[...].astype(F32), two_ref[...].astype(F32))
+    product = dot(one_ref[:, :HD], two_ref[...])
+    pre = jnp.concatenate([product[:, :HD], product[:, HD:] + one_ref[:, HD:].astype(F32)], axis=1)
     pre_ref[...] = pre
     four = after(tl_ref[...], pre).astype(BF16)
     four_t_ref[...] = four[:, :HD]
@@ -284,19 +313,28 @@
     def project(hid):
         return jnp.dot(hid, w_all, preferred_element_type=F32).astype(BF16)
 
-    tl, tl16, b, far = pl.pallas_call(
+    own, sib = project(hidden_in), project(hidden_sib)
+    tl, tl16, wu, key_t, far = pl.pallas_call(
         functools.partial(local_kernel, chips),
         out_shape=(
             jax.ShapeDtypeStruct((HD, 2 * HD), F32),
             jax.ShapeDtypeStruct((HD, 2 * HD), BF16),
-            jax.ShapeDtypeStruct((2, TOK, HD), F32),
+            jax.ShapeDtypeStruct((TOK, 2 * HD), F32),
+            jax.ShapeDtypeStruct((HD, TOK), F32),
             jax.ShapeDtypeStruct((1,), jnp.int32),
         ),
         in_specs=[SMEM, SMEM, VMEM, VMEM, VMEM, VMEM],
-        out_specs=(VMEM, VMEM, VMEM, SMEM),
+        out_specs=(VMEM, VMEM, VMEM, VMEM, SMEM),
         compiler_params=pltpu.CompilerParams(vmem_limit_bytes=VMEM_LIMIT),
         cost_estimate=pl.CostEstimate(flops=3 << 30, bytes_accessed=1 << 20, transcendentals=0),
-    )(meta, doc_starts, project(hidden_in), project(hidden_sib), codes, got)
+    )(meta, doc_starts, own, sib, codes, got)
+    (b,) = call(
+        query_kernel,
+        (meta, doc_starts),
+        (own, sib, key_t, wu),
+        [((2, TOK, HD), F32)],
+        1 << 30,
+    )
     one = ahead(tl16, 1)
     (two,) = call(pair_kernel, (), (tl, one), [((HD, 2 * HD), BF16)], 1 << 26)
     two = ahead(two, 2)

time: 155 us -> 154 us (level)
  starting transfers between devices: 45.6 us -> 43.9 us
    ppermute x3, starting transfers between devices: 15.2 us -> 10.4 us  [ahead(): lax.ppermute(value, 'z', [(i, i + steps) for i in range(chips - steps)])]
    ppermute x4, starting transfers between devices: 28.9 us -> 32.1 us  [swap(): return lax.ppermute(value, 'c', [(0, 1), (1, 0)])]
    pallas_call x4 -> x5, Pallas kernels: 2.88 us -> 4.53 us  [call(): pl.pallas_call(kernel, out_shape=tuple((jax.ShapeDtypeStruct(s, d) for s,...]
  transfers between devices with their start and end apart: 8 -> 8, of which waited for: 3 -> 2; matrix products, arithmetic and copies ran while one was open for 2% -> 2% of each run, Pallas kernels for 1% -> 3%
where the time goes in v11:
time: 154 us; the launch traced here: 153 us
  blocking collectives  90.1 us (59%)
  starting transfers between devices  43.9 us (29%)
  Pallas kernels  9.49 us (6%)
  matrix products  3.42 us (2%)
  local copies, waits for them, and re-layouts  1.84 us (1%)
  waiting for transfers between devices  1.81 us (1%)
  other arithmetic  1.56 us (1%)
    all_gather x1, blocking collectives, per_device(): both = lax.all_gather(both, 'z', axis=0, tiled=True)  67.2 us
    ppermute x4, starting transfers between devices, swap(): return lax.ppermute(value, 'c', [(0, 1), (1, 0)])  32.1 us
    all_gather x1, blocking collectives, per_device(): normed_all = lax.all_gather(to_f16(normed, N_SCALE), 'h', axis=0)  22.9 us
    ppermute x3, starting transfers between devices, ahead(): lax.ppermute(value, 'z', [(i, i + steps) for i in range(chips - steps)])  10.4 us
    pallas_call x1, Pallas kernels, per_device(): pl.pallas_call(functools.partial(local_kernel, chips), out_shape=(jax.Sha...  4.96 us
    pallas_call x5, Pallas kernels, call(): pl.pallas_call(kernel, out_shape=tuple((jax.ShapeDtypeStruct(s, d) for s,...  4.53 us
  transfers between devices with their start and end apart: 8, of which 2 were waited for; matrix products, arithmetic and copies ran while one was open for 2% of the time, Pallas kernels for 3%

profile of v11, /device:TPU:1, one launch (start us, length us, event | category | flops | bytes accessed | tf_op | source)
XLA Modules:
  0.0 153.1 jit_solution(7569352756442430859)
XLA Ops:
  0.0 1.5 collective-permute-start.5
  1.6 0.9 copy-done
  2.5 0.7 copy-done.1
  3.2 0.6 shard_map.55
  3.8 8.8 %collective-permute-start.4 = (bf16[128,512]{1,0:T(8,128)(2,1)S(1)}, bf16[128,512]{1,0:T(8,128)(2,1)S(1)}, u32[]{:S(2)}, u32[]{:S(2)}) collective-permute-start(bf16[128,512]{1,0:T(8,128)(2,1)S(1)} %get-tuple-element.26), channel_id=1, source_target_pairs={{0,16},{16,0},{1,17},{17,1},{2,18},{18,2},{3,19},{19,3},{4,20},{20... | collective-permute-start | bytes 393224 | tf_op jit(solution)/shard_map/ppermute | solution.py:260
  12.6 1.9 %collective-permute-start.6 = (bf16[256,4096]{1,0:T(8,128)(2,1)}, bf16[256,4096]{1,0:T(8,128)(2,1)S(1)}, u32[]{:S(2)}, u32[]{:S(2)}) collective-permute-start(bf16[256,4096]{1,0:T(8,128)(2,1)} %param.7), channel_id=1, source_target_pairs={{0,16},{16,0},{1,17},{17,1},{2,18},{18,2},{3,19},{19,3},{4,20},{20... | collective-permute-start | bytes 6291464 | tf_op jit(solution)/shard_map/ppermute | solution.py:260
  14.7 67.2 %all-gather.3 = f16[4096,512]{1,0:T(8,128)(2,1)S(1)} all-gather(f16[256,512]{1,0:T(8,128)(2,1)S(1)} %pad_maximum_fusion.3), channel_id=1, replica_groups=mesh['z'=16,'c'=2,'h'=16] {'z'}, dimensions={0}, use_global_device_ids=true | all-gather | bytes 4456448 | tf_op jit(solution)/shard_map/all_gather | solution.py:310
  82.0 1.3 fusion.4.own_ref
  83.3 1.3 fusion.5.sib_ref
  84.6 5.0 %shard_map.56 = (f32[128,256]{1,0:T(8,128)S(1)}, bf16[128,256]{1,0:T(8,128)(2,1)S(1)}, f32[512,256]{1,0:T(8,128)S(1)}, f32[128,512]{1,0:T(8,128)S(1)}, s32[1]{0:T(128)}) custom-call(s32[2]{0:T(128)S(1)} %pad_add_fusion.meta_ref, s32[9]{0:T(128)S(1)} %copy-done.3, bf16[256,384]{1,0:T(8,128)(2,1)S(1)} %fusion.4.own_ref, bf16[256,384]{1,0:T(8,128)(2,1)S(1)} %fusion.5.sib_ref, ...), custom_call_target="tpu_custom_call" | custom-call | flops 3221225472 | bytes 1048576 | tf_op jit(solution)/shard_map/pallas_call | solution.py:317
  89.6 2.1 %collective-permute-start.7 = (bf16[128,256]{1,0:T(8,128)(2,1)S(1)}, bf16[128,256]{1,0:T(8,128)(2,1)S(1)}, u32[]{:S(2)}, u32[]{:S(2)}) collective-permute-start(bf16[128,256]{1,0:T(8,128)(2,1)S(1)} %get-tuple-element.28), channel_id=1, source_target_pairs={{0,32},{32,64},{64,96},{96,128},{128,160},{160,192},{192,224},{224... | collective-permute-start | bytes 196616 | tf_op jit(solution)/shard_map/ppermute | solution.py:265
  91.9 1.1 collective-permute-done.7.one_ref
  93.1 3.4 %collective-permute-start.8 = (bf16[128,256]{1,0:T(8,128)(2,1)S(1)}, bf16[128,256]{1,0:T(8,128)(2,1)S(1)}, u32[]{:S(2)}, u32[]{:S(2)}) collective-permute-start(bf16[128,256]{1,0:T(8,128)(2,1)S(1)} %shard_map.57), channel_id=1, source_target_pairs={{0,64},{32,96},{64,128},{96,160},{128,192},{160,224},{192,256},{22... | collective-permute-start | bytes 196616 | tf_op jit(solution)/shard_map/ppermute | solution.py:265
  96.8 11.5 %collective-permute-start.10 = (bf16[16,128,128]{2,1,0:T(8,128)(2,1)S(1)}, bf16[16,128,128]{2,1,0:T(8,128)(2,1)S(1)}, u32[]{:S(2)}, u32[]{:S(2)}) collective-permute-start(bf16[16,128,128]{2,1,0:T(8,128)(2,1)S(1)} %fusion.11), channel_id=1, source_target_pairs={{0,16},{16,0},{1,17},{17,1},{2,18},{18,2},{3,19},{19,3},{4,20},{20... | collective-permute-start | bytes 1572872 | tf_op jit(solution)/shard_map/ppermute | solution.py:260
  109.0 1.0 shard_map.58
  109.9 4.8 %collective-permute-start.9 = (bf16[128,128]{1,0:T(8,128)(2,1)}, bf16[128,128]{1,0:T(8,128)(2,1)S(1)}, u32[]{:S(2)}, u32[]{:S(2)}) collective-permute-start(bf16[128,128]{1,0:T(8,128)(2,1)} %get-tuple-element.30), channel_id=1, source_target_pairs={{0,128},{32,160},{64,192},{96,224},{128,256},{160,288},{192,320},{... | collective-permute-start | bytes 98312 | tf_op jit(solution)/shard_map/ppermute | solution.py:265
  114.8 1.7 %shard_map.59.b_ref = f32[2,512,128]{2,1,0:T(8,128)S(1)} custom-call(s32[2]{0:T(128)S(1)} %pad_add_fusion.meta_ref, s32[9]{0:T(128)S(1)} %copy-done.3, bf16[256,384]{1,0:T(8,128)(2,1)S(1)} %fusion.4.own_ref, bf16[256,384]{1,0:T(8,128)(2,1)S(1)} %fusion.5.sib_ref, f32[128,512]{1,0:T(8,128)S(1)} %get-tuple-element.33.kt_ref, ...), custom_call_target="tpu_custom_call" | custom-call | flops 1073741824 | bytes 1048576 | tf_op jit(solution)/shard_map/pallas_call | solution.py:249
  116.5 1.1 shard_map.60
  117.7 22.9 %all-gather.4 = f16[8192,128]{1,0:T(8,128)(2,1)S(1)} all-gather(f16[512,128]{1,0:T(8,128)(2,1)S(1)} %multiply_convert_fusion.18), channel_id=2, replica_groups=mesh['z'=16,'c'=2,'h'=16] {'h'}, dimensions={0}, use_global_device_ids=true | all-gather | bytes 2228224 | tf_op jit(solution)/shard_map/all_gather | solution.py:372
  141.0 0.4 convolution_bitcast_fusion.1
  141.4 9.8 %collective-permute-start.11 = (f32[256,256]{1,0:T(8,128)S(1)}, f32[256,256]{1,0:T(8,128)S(1)}, u32[]{:S(2)}, u32[]{:S(2)}) collective-permute-start(f32[256,256]{1,0:T(8,128)S(1)} %convolution_bitcast_fusion.1), channel_id=1, source_target_pairs={{0,16},{16,0},{1,17},{17,1},{2,18},{18,2},{3,19},{19,3},{4,20},{20... | collective-permute-start | bytes 786440 | tf_op jit(solution)/shard_map/ppermute | solution.py:260
  151.3 0.4 convolution_bitcast_fusion.2
  151.7 0.7 collective-permute-done.11
  152.4 0.7 add_convert_fusion
  (26 shorter events, 1.3 us)
Async XLA Ops:
  0.0 14.5 %collective-permute-start.5 = (bf16[256,128]{1,0:T(8,128)(2,1)}, bf16[256,128]{1,0:T(8,128)(2,1)S(1)}, u32[]{:S(2)}, u32[]{:S(2)}) collective-permute-start(bf16[256,128]{1,0:T(8,128)(2,1)} %param.11), channel_id=1, source_target_pairs={{0,0},{1,32},{2,64},{3,96},{4,128},{5,160},{6,192},{7,224},{8,256}... | collective-permute-start | bytes 196616 | tf_op jit(solution)/shard_map/ppermute | solution.py:292
  1.6 0.9 copy-start
  2.5 0.7 copy-start.1
  3.8 10.8 %collective-permute-start.4 = (bf16[128,512]{1,0:T(8,128)(2,1)S(1)}, bf16[128,512]{1,0:T(8,128)(2,1)S(1)}, u32[]{:S(2)}, u32[]{:S(2)}) collective-permute-start(bf16[128,512]{1,0:T(8,128)(2,1)S(1)} %get-tuple-element.26), channel_id=1, source_target_pairs={{0,16},{16,0},{1,17},{17,1},{2,18},{18,2},{3,19},{19,3},{4,20},{20... | collective-permute-start | bytes 393224 | tf_op jit(solution)/shard_map/ppermute | solution.py:260
  12.6 70.7 %collective-permute-start.6 = (bf16[256,4096]{1,0:T(8,128)(2,1)}, bf16[256,4096]{1,0:T(8,128)(2,1)S(1)}, u32[]{:S(2)}, u32[]{:S(2)}) collective-permute-start(bf16[256,4096]{1,0:T(8,128)(2,1)} %param.7), channel_id=1, source_target_pairs={{0,16},{16,0},{1,17},{17,1},{2,18},{18,2},{3,19},{19,3},{4,20},{20... | collective-permute-start | bytes 6291464 | tf_op jit(solution)/shard_map/ppermute | solution.py:260
  14.7 67.3 %copy-start.4 = (bf16[256,4096]{1,0:T(8,128)(2,1)S(1)}, bf16[256,4096]{1,0:T(8,128)(2,1)}, u32[]{:S(2)}) copy-start(bf16[256,4096]{1,0:T(8,128)(2,1)} %param.7) | copy-start | bytes 6291460
  83.2 1.3 copy-start.2
  83.3 1.3 copy-start.3
  89.6 3.4 %collective-permute-start.7 = (bf16[128,256]{1,0:T(8,128)(2,1)S(1)}, bf16[128,256]{1,0:T(8,128)(2,1)S(1)}, u32[]{:S(2)}, u32[]{:S(2)}) collective-permute-start(bf16[128,256]{1,0:T(8,128)(2,1)S(1)} %get-tuple-element.28), channel_id=1, source_target_pairs={{0,32},{32,64},{64,96},{96,128},{128,160},{160,192},{192,224},{224... | collective-permute-start | bytes 196616 | tf_op jit(solution)/shard_map/ppermute | solution.py:265
  93.1 15.8 %collective-permute-start.8 = (bf16[128,256]{1,0:T(8,128)(2,1)S(1)}, bf16[128,256]{1,0:T(8,128)(2,1)S(1)}, u32[]{:S(2)}, u32[]{:S(2)}) collective-permute-start(bf16[128,256]{1,0:T(8,128)(2,1)S(1)} %shard_map.57), channel_id=1, source_target_pairs={{0,64},{32,96},{64,128},{96,160},{128,192},{160,224},{192,256},{22... | collective-permute-start | bytes 196616 | tf_op jit(solution)/shard_map/ppermute | solution.py:265
  96.8 43.8 %collective-permute-start.10 = (bf16[16,128,128]{2,1,0:T(8,128)(2,1)S(1)}, bf16[16,128,128]{2,1,0:T(8,128)(2,1)S(1)}, u32[]{:S(2)}, u32[]{:S(2)}) collective-permute-start(bf16[16,128,128]{2,1,0:T(8,128)(2,1)S(1)} %fusion.11), channel_id=1, source_target_pairs={{0,16},{16,0},{1,17},{17,1},{2,18},{18,2},{3,19},{19,3},{4,20},{20... | collective-permute-start | bytes 1572872 | tf_op jit(solution)/shard_map/ppermute | solution.py:260
  109.9 6.6 %collective-permute-start.9 = (bf16[128,128]{1,0:T(8,128)(2,1)}, bf16[128,128]{1,0:T(8,128)(2,1)S(1)}, u32[]{:S(2)}, u32[]{:S(2)}) collective-permute-start(bf16[128,128]{1,0:T(8,128)(2,1)} %get-tuple-element.30), channel_id=1, source_target_pairs={{0,128},{32,160},{64,192},{96,224},{128,256},{160,288},{192,320},{... | collective-permute-start | bytes 98312 | tf_op jit(solution)/shard_map/ppermute | solution.py:265
  141.4 11.0 %collective-permute-start.11 = (f32[256,256]{1,0:T(8,128)S(1)}, f32[256,256]{1,0:T(8,128)S(1)}, u32[]{:S(2)}, u32[]{:S(2)}) collective-permute-start(f32[256,256]{1,0:T(8,128)S(1)} %convolution_bitcast_fusion.1), channel_id=1, source_target_pairs={{0,16},{16,0},{1,17},{17,1},{2,18},{18,2},{3,19},{19,3},{4,20},{20... | collective-permute-start | bytes 786440 | tf_op jit(solution)/shard_map/ppermute | solution.py:260

commit v12 on v11

--- a/solution.py
+++ b/solution.py
@@ -121,9 +121,9 @@
     far_ref[0] = far_reach(ds_ref, chips)
     first = meta_ref[1] == 0
     half = TOK // 2
-    qkv = in_order(first, own_ref[...].astype(F32), sib_ref[...].astype(F32))
-    key = unit_rows(qkv[:, HD : 2 * HD])
-    value = qkv[:, 2 * HD :]
+    kv = in_order(first, own_ref[...].astype(F32), sib_ref[...].astype(F32))
+    key = unit_rows(kv[:, :HD])
+    value = kv[:, HD:]
     codes = codes_ref[...].astype(F32)
     own_codes = jnp.where(first, codes[0:1], codes[1:2])
     got = got_ref[0:8, 3 * HD :].astype(F32)
@@ -187,7 +187,7 @@
 def query_kernel(meta_ref, ds_ref, own_ref, sib_ref, kt_ref, wu_ref, b_ref):
     first = meta_ref[1] == 0
     half = TOK // 2
-    query = unit_rows(in_order(first, own_ref[:, :HD].astype(F32), sib_ref[:, :HD].astype(F32)))
+    query = unit_rows(in_order(first, own_ref[...].astype(F32), sib_ref[...].astype(F32)))
     doc_col, doc_row, prev_doc, _ = doc_info(meta_ref, ds_ref)
     carry_in = (doc_col == prev_doc).astype(F32)
     query_s = split(query)
@@ -308,12 +308,12 @@
         [to_f16(w_chip, W_SCALE), to_f16(wo, WO_SCALE)], axis=1
     )
     both = lax.all_gather(both, "z", axis=0, tiled=True)
-    w_all, wo_all = from_f16(both[:, : 3 * HD], W_SCALE), both[:, 3 * HD :]
-
-    def project(hid):
-        return jnp.dot(hid, w_all, preferred_element_type=F32).astype(BF16)
-
-    own, sib = project(hidden_in), project(hidden_sib)
+    q_all, kv_all, wo_all = both[:, :HD], both[:, HD : 3 * HD], both[:, 3 * HD :]
+
+    def project(hid, weights):
+        weights = from_f16(weights, W_SCALE)
+        return jnp.dot(hid, weights, preferred_element_type=F32).astype(BF16)
+
     tl, tl16, wu, key_t, far = pl.pallas_call(
         functools.partial(local_kernel, chips),
         out_shape=(
@@ -327,18 +327,26 @@
         out_specs=(VMEM, VMEM, VMEM, VMEM, SMEM),
         compiler_params=pltpu.CompilerParams(vmem_limit_bytes=VMEM_LIMIT),
         cost_estimate=pl.CostEstimate(flops=3 << 30, bytes_accessed=1 << 20, transcendentals=0),
-    )(meta, doc_starts, own, sib, codes, got)
+    )(
+        meta,
+        doc_starts,
+        project(hidden_in, kv_all),
+        project(hidden_sib, kv_all),
+        codes,
+        got,
+    )
+    q_all, _ = lax.optimization_barrier((q_all, tl16))
     (b,) = call(
         query_kernel,
         (meta, doc_starts),
-        (own, sib, key_t, wu),
+        (project(hidden_in, q_all), project(hidden_sib, q_all), key_t, wu),
         [((2, TOK, HD), F32)],
         1 << 30,
     )
     one = ahead(tl16, 1)
     (two,) = call(pair_kernel, (), (tl, one), [((HD, 2 * HD), BF16)], 1 << 26)
     two = ahead(two, 2)
-    wo_all, _ = lax.optimization_barrier((wo_all, tl16))
+    wo_all, _ = lax.optimization_barrier((wo_all, one))
     wo_all = wo_all.reshape(chips, 2, HD, HD)
     wo_keep = from_f16(jnp.where(first, wo_all[:, 0], wo_all[:, 1]), WO_SCALE)
     wo_sent = from_f16(jnp.where(first, wo_all[:, 1], wo_all[:, 0]), WO_SCALE)

time: 154 us -> 157 us (1.019)
  matrix products: 3.42 us -> 7.17 us
    dot_general x2 -> x4, matrix products: 2.55 us -> 6.3 us  [project(): return jnp.dot(hid, weights, preferred_element_type=F32).astype(BF16)]
    ppermute x4, starting transfers between devices: 32.1 us -> 28.8 us  [swap(): return lax.ppermute(value, 'c', [(0, 1), (1, 0)])]
    ppermute x3, starting transfers between devices: 10.4 us -> 13 us  [ahead(): lax.ppermute(value, 'z', [(i, i + steps) for i in range(chips - steps)])]
  transfers between devices with their start and end apart: 8 -> 8, of which waited for: 2 -> 1; matrix products, arithmetic and copies ran while one was open for 2% -> 3% of each run, Pallas kernels for 3% -> 2%
where the time goes in v12:
time: 157 us; the launch traced here: 156 us
  blocking collectives  90.9 us (58%)
  starting transfers between devices  43.3 us (28%)
  Pallas kernels  9.5 us (6%)
  matrix products  7.17 us (5%)
  local copies, waits for them, and re-layouts  2.04 us (1%)
    all_gather x1, blocking collectives, per_device(): both = lax.all_gather(both, 'z', axis=0, tiled=True)  67.2 us
    ppermute x4, starting transfers between devices, swap(): return lax.ppermute(value, 'c', [(0, 1), (1, 0)])  28.8 us
    all_gather x1, blocking collectives, per_device(): normed_all = lax.all_gather(to_f16(normed, N_SCALE), 'h', axis=0)  23.7 us
    ppermute x3, starting transfers between devices, ahead(): lax.ppermute(value, 'z', [(i, i + steps) for i in range(chips - steps)])  13 us
    dot_general x4, matrix products, project(): return jnp.dot(hid, weights, preferred_element_type=F32).astype(BF16)  6.3 us
    pallas_call x1, Pallas kernels, per_device(): pl.pallas_call(functools.partial(local_kernel, chips), out_shape=(jax.Sha...  4.98 us
    pallas_call x5, Pallas kernels, call(): pl.pallas_call(kernel, out_shape=tuple((jax.ShapeDtypeStruct(s, d) for s,...  4.52 us
  transfers between devices with their start and end apart: 8, of which 1 were waited for; matrix products, arithmetic and copies ran while one was open for 3% of the time, Pallas kernels for 2%

profile of v12, /device:TPU:1, one launch (start us, length us, event | category | flops | bytes accessed | tf_op | source)
XLA Modules:
  0.0 156.1 jit_solution(6217280045210968148)
XLA Ops:
  0.0 1.5 collective-permute-start.5
  1.6 0.9 copy-done
  2.5 0.7 copy-done.1
  3.2 0.6 shard_map.55
  3.8 8.8 %collective-permute-start.4 = (bf16[128,512]{1,0:T(8,128)(2,1)S(1)}, bf16[128,512]{1,0:T(8,128)(2,1)S(1)}, u32[]{:S(2)}, u32[]{:S(2)}) collective-permute-start(bf16[128,512]{1,0:T(8,128)(2,1)S(1)} %get-tuple-element.27), channel_id=1, source_target_pairs={{0,16},{16,0},{1,17},{17,1},{2,18},{18,2},{3,19},{19,3},{4,20},{20... | collective-permute-start | bytes 393224 | tf_op jit(solution)/shard_map/ppermute | solution.py:260
  12.6 1.9 %collective-permute-start.6 = (bf16[256,4096]{1,0:T(8,128)(2,1)}, bf16[256,4096]{1,0:T(8,128)(2,1)}, u32[]{:S(2)}, u32[]{:S(2)}) collective-permute-start(bf16[256,4096]{1,0:T(8,128)(2,1)} %param.7), channel_id=1, source_target_pairs={{0,16},{16,0},{1,17},{17,1},{2,18},{18,2},{3,19},{19,3},{4,20},{20... | collective-permute-start | bytes 6291464 | tf_op jit(solution)/shard_map/ppermute | solution.py:260
  14.7 67.2 %all-gather.3 = f16[4096,512]{1,0:T(8,128)(2,1)S(1)} all-gather(f16[256,512]{1,0:T(8,128)(2,1)S(1)} %pad_maximum_fusion.3), channel_id=1, replica_groups=mesh['z'=16,'c'=2,'h'=16] {'z'}, dimensions={0}, use_global_device_ids=true | all-gather | bytes 4456448 | tf_op jit(solution)/shard_map/all_gather | solution.py:310
  82.0 0.8 fusion.4.own_ref
  83.2 2.4 %fusion.5.sib_ref = bf16[256,256]{1,0:T(8,128)(2,1)S(1)} fusion(bf16[256,4096]{1,0:T(8,128)(2,1)} %collective-permute-done.6, f16[4096,512]{1,0:T(8,128)(2,1)S(1)} %all-gather.3), kind=kOutput, calls=%fused_computation.13 | convolution fusion | flops 540082176 | bytes 4325376 | tf_op jit(solution)/shard_map/dot_general | solution.py:315
  85.7 5.0 %shard_map.56 = (f32[128,256]{1,0:T(8,128)S(1)}, bf16[128,256]{1,0:T(8,128)(2,1)S(1)}, f32[512,256]{1,0:T(8,128)S(1)}, f32[128,512]{1,0:T(8,128)S(1)}, s32[1]{0:T(128)}) custom-call(s32[2]{0:T(128)S(1)} %pad_add_fusion.meta_ref, s32[9]{0:T(128)S(1)} %copy-done.3, bf16[256,256]{1,0:T(8,128)(2,1)S(1)} %fusion.4.own_ref, bf16[256,256]{1,0:T(8,128)(2,1)S(1)} %fusion.5.sib_ref, ...), custom_call_target="tpu_custom_call" | custom-call | flops 3221225472 | bytes 1048576 | tf_op jit(solution)/shard_map/pallas_call | solution.py:317
  90.7 2.1 %collective-permute-start.7 = (bf16[128,256]{1,0:T(8,128)(2,1)S(1)}, bf16[128,256]{1,0:T(8,128)(2,1)S(1)}, u32[]{:S(2)}, u32[]{:S(2)}) collective-permute-start(bf16[128,256]{1,0:T(8,128)(2,1)S(1)} %get-tuple-element.29), channel_id=1, source_target_pairs={{0,32},{32,64},{64,96},{96,128},{128,160},{160,192},{192,224},{224... | collective-permute-start | bytes 196616 | tf_op jit(solution)/shard_map/ppermute | solution.py:265
  92.7 0.8 fusion.6.own_ref
  93.5 2.3 %fusion.7.sib_ref = bf16[256,128]{1,0:T(8,128)(2,1)S(1)} fusion(bf16[256,4096]{1,0:T(8,128)(2,1)} %collective-permute-done.6, f16[4096,128]{1,0:T(8,128)(2,1)S(1)} %get-tuple-element.34), kind=kOutput, calls=%fused_computation.17 | convolution fusion | flops 270041088 | bytes 3211264 | tf_op jit(solution)/shard_map/dot_general | solution.py:315
  96.7 1.6 %collective-permute-start.8 = (bf16[128,256]{1,0:T(8,128)(2,1)S(1)}, bf16[128,256]{1,0:T(8,128)(2,1)S(1)}, u32[]{:S(2)}, u32[]{:S(2)}) collective-permute-start(bf16[128,256]{1,0:T(8,128)(2,1)S(1)} %shard_map.57), channel_id=1, source_target_pairs={{0,64},{32,96},{64,128},{96,160},{128,192},{160,224},{192,256},{22... | collective-permute-start | bytes 196616 | tf_op jit(solution)/shard_map/ppermute | solution.py:265
  98.3 1.7 %shard_map.59.b_ref = f32[2,512,128]{2,1,0:T(8,128)S(1)} custom-call(s32[2]{0:T(128)S(1)} %pad_add_fusion.meta_ref, s32[9]{0:T(128)S(1)} %copy-done.3, bf16[256,128]{1,0:T(8,128)(2,1)S(1)} %fusion.6.own_ref, bf16[256,128]{1,0:T(8,128)(2,1)S(1)} %fusion.7.sib_ref, f32[128,512]{1,0:T(8,128)S(1)} %get-tuple-element.35.kt_ref, ...), custom_call_target="tpu_custom_call" | custom-call | flops 1073741824 | bytes 1048576 | tf_op jit(solution)/shard_map/pallas_call | solution.py:249
  100.0 1.0 shard_map.58
  101.0 9.3 %collective-permute-start.9 = (bf16[128,128]{1,0:T(8,128)(2,1)}, bf16[128,128]{1,0:T(8,128)(2,1)S(1)}, u32[]{:S(2)}, u32[]{:S(2)}) collective-permute-start(bf16[128,128]{1,0:T(8,128)(2,1)} %get-tuple-element.31), channel_id=1, source_target_pairs={{0,128},{32,160},{64,192},{96,224},{128,256},{160,288},{192,320},{... | collective-permute-start | bytes 98312 | tf_op jit(solution)/shard_map/ppermute | solution.py:265
  110.6 12.1 %collective-permute-start.10 = (bf16[16,128,128]{2,1,0:T(8,128)(2,1)S(1)}, bf16[16,128,128]{2,1,0:T(8,128)(2,1)S(1)}, u32[]{:S(2)}, u32[]{:S(2)}) collective-permute-start(bf16[16,128,128]{2,1,0:T(8,128)(2,1)S(1)} %fusion.13), channel_id=1, source_target_pairs={{0,16},{16,0},{1,17},{17,1},{2,18},{18,2},{3,19},{19,3},{4,20},{20... | collective-permute-start | bytes 1572872 | tf_op jit(solution)/shard_map/ppermute | solution.py:260
  122.8 1.1 shard_map.60
  123.9 23.7 %all-gather.4 = f16[8192,128]{1,0:T(8,128)(2,1)S(1)} all-gather(f16[512,128]{1,0:T(8,128)(2,1)S(1)} %multiply_convert_fusion.21), channel_id=2, replica_groups=mesh['z'=16,'c'=2,'h'=16] {'h'}, dimensions={0}, use_global_device_ids=true | all-gather | bytes 2228224 | tf_op jit(solution)/shard_map/all_gather | solution.py:380
  148.4 5.9 %collective-permute-start.11 = (f32[256,256]{1,0:T(8,128)S(1)}, f32[256,256]{1,0:T(8,128)S(1)}, u32[]{:S(2)}, u32[]{:S(2)}) collective-permute-start(f32[256,256]{1,0:T(8,128)S(1)} %convolution_bitcast_fusion.1), channel_id=1, source_target_pairs={{0,16},{16,0},{1,17},{17,1},{2,18},{18,2},{3,19},{19,3},{4,20},{20... | collective-permute-start | bytes 786440 | tf_op jit(solution)/shard_map/ppermute | solution.py:260
  154.3 0.4 convolution_bitcast_fusion.2
  154.7 0.7 collective-permute-done.11
  155.4 0.7 add_convert_fusion
  (28 shorter events, 1.9 us)
Async XLA Ops:
  0.0 14.5 %collective-permute-start.5 = (bf16[256,128]{1,0:T(8,128)(2,1)}, bf16[256,128]{1,0:T(8,128)(2,1)S(1)}, u32[]{:S(2)}, u32[]{:S(2)}) collective-permute-start(bf16[256,128]{1,0:T(8,128)(2,1)} %param.11), channel_id=1, source_target_pairs={{0,0},{1,32},{2,64},{3,96},{4,128},{5,160},{6,192},{7,224},{8,256}... | collective-permute-start | bytes 196616 | tf_op jit(solution)/shard_map/ppermute | solution.py:292
  1.6 0.9 copy-start
  2.5 0.7 copy-start.1
  3.8 10.8 %collective-permute-start.4 = (bf16[128,512]{1,0:T(8,128)(2,1)S(1)}, bf16[128,512]{1,0:T(8,128)(2,1)S(1)}, u32[]{:S(2)}, u32[]{:S(2)}) collective-permute-start(bf16[128,512]{1,0:T(8,128)(2,1)S(1)} %get-tuple-element.27), channel_id=1, source_target_pairs={{0,16},{16,0},{1,17},{17,1},{2,18},{18,2},{3,19},{19,3},{4,20},{20... | collective-permute-start | bytes 393224 | tf_op jit(solution)/shard_map/ppermute | solution.py:260
  12.6 70.7 %collective-permute-start.6 = (bf16[256,4096]{1,0:T(8,128)(2,1)}, bf16[256,4096]{1,0:T(8,128)(2,1)}, u32[]{:S(2)}, u32[]{:S(2)}) collective-permute-start(bf16[256,4096]{1,0:T(8,128)(2,1)} %param.7), channel_id=1, source_target_pairs={{0,16},{16,0},{1,17},{17,1},{2,18},{18,2},{3,19},{19,3},{4,20},{20... | collective-permute-start | bytes 6291464 | tf_op jit(solution)/shard_map/ppermute | solution.py:260
  14.7 67.3 %copy-start.4 = (bf16[256,4096]{1,0:T(8,128)(2,1)S(1)}, bf16[256,4096]{1,0:T(8,128)(2,1)}, u32[]{:S(2)}) copy-start(bf16[256,4096]{1,0:T(8,128)(2,1)} %param.7) | copy-start | bytes 6291460
  83.2 2.5 %copy-start.2 = (s32[256,2]{0,1:T(2,128)S(1)}, s32[256,2]{0,1:T(2,128)}, u32[]{:S(2)}) copy-start(s32[256,2]{0,1:T(2,128)} %param.10) | copy-start | bytes 6148
  83.2 2.5 %copy-start.3 = (s32[9]{0:T(128)S(1)}, s32[9]{0:T(128)}, u32[]{:S(2)}) copy-start(s32[9]{0:T(128)} %ds_ref.3) | copy-start | bytes 112
  90.7 5.8 %collective-permute-start.7 = (bf16[128,256]{1,0:T(8,128)(2,1)S(1)}, bf16[128,256]{1,0:T(8,128)(2,1)S(1)}, u32[]{:S(2)}, u32[]{:S(2)}) collective-permute-start(bf16[128,256]{1,0:T(8,128)(2,1)S(1)} %get-tuple-element.29), channel_id=1, source_target_pairs={{0,32},{32,64},{64,96},{96,128},{128,160},{160,192},{192,224},{224... | collective-permute-start | bytes 196616 | tf_op jit(solution)/shard_map/ppermute | solution.py:265
  96.7 3.3 %collective-permute-start.8 = (bf16[128,256]{1,0:T(8,128)(2,1)S(1)}, bf16[128,256]{1,0:T(8,128)(2,1)S(1)}, u32[]{:S(2)}, u32[]{:S(2)}) collective-permute-start(bf16[128,256]{1,0:T(8,128)(2,1)S(1)} %shard_map.57), channel_id=1, source_target_pairs={{0,64},{32,96},{64,128},{96,160},{128,192},{160,224},{192,256},{22... | collective-permute-start | bytes 196616 | tf_op jit(solution)/shard_map/ppermute | solution.py:265
  101.0 21.8 %collective-permute-start.9 = (bf16[128,128]{1,0:T(8,128)(2,1)}, bf16[128,128]{1,0:T(8,128)(2,1)S(1)}, u32[]{:S(2)}, u32[]{:S(2)}) collective-permute-start(bf16[128,128]{1,0:T(8,128)(2,1)} %get-tuple-element.31), channel_id=1, source_target_pairs={{0,128},{32,160},{64,192},{96,224},{128,256},{160,288},{192,320},{... | collective-permute-start | bytes 98312 | tf_op jit(solution)/shard_map/ppermute | solution.py:265
  110.6 37.0 %collective-permute-start.10 = (bf16[16,128,128]{2,1,0:T(8,128)(2,1)S(1)}, bf16[16,128,128]{2,1,0:T(8,128)(2,1)S(1)}, u32[]{:S(2)}, u32[]{:S(2)}) collective-permute-start(bf16[16,128,128]{2,1,0:T(8,128)(2,1)S(1)} %fusion.13), channel_id=1, source_target_pairs={{0,16},{16,0},{1,17},{17,1},{2,18},{18,2},{3,19},{19,3},{4,20},{20... | collective-permute-start | bytes 1572872 | tf_op jit(solution)/shard_map/ppermute | solution.py:260
  148.4 7.1 %collective-permute-start.11 = (f32[256,256]{1,0:T(8,128)S(1)}, f32[256,256]{1,0:T(8,128)S(1)}, u32[]{:S(2)}, u32[]{:S(2)}) collective-permute-start(f32[256,256]{1,0:T(8,128)S(1)} %convolution_bitcast_fusion.1), channel_id=1, source_target_pairs={{0,16},{16,0},{1,17},{17,1},{2,18},{18,2},{3,19},{19,3},{4,20},{20... | collective-permute-start | bytes 786440 | tf_op jit(solution)/shard_map/ppermute | solution.py:260

commit v13 on v11

--- a/solution.py
+++ b/solution.py
@@ -101,7 +101,7 @@
     gap = chips - 1 - blocks[count - 1]
     for j in range(count - 1):
         gap = jnp.maximum(gap, blocks[j + 1] - blocks[j])
-    return (gap > 7).astype(jnp.int32)
+    return (gap > 7).astype(jnp.int32) + (gap > 11).astype(jnp.int32)
 
 
 def local_kernel(
@@ -354,14 +354,21 @@
         1 << 26,
     )
 
-    def fetch_far(t, add):
+    def through_four(t, state):
+        return jnp.dot(ahead(t, 4).astype(F32), state, precision=lax.Precision.HIGHEST)
+
+    def fetch_none(t, add):
+        return jnp.zeros((HD, HD), F32)
+
+    def fetch_eight(t, add):
+        return through_four(t, ahead(add, 8).astype(F32))
+
+    def fetch_twelve(t, add):
         eight_t, eight_l, twelve = ahead(t, 8), ahead(add, 8), ahead(add, 12)
         state = jnp.dot(eight_t, twelve, preferred_element_type=F32) + eight_l.astype(F32)
-        return jnp.dot(ahead(t, 4).astype(F32), state, precision=lax.Precision.HIGHEST)
-
-    extra = lax.cond(
-        far[0] > 0, fetch_far, lambda t, add: jnp.zeros((HD, HD), F32), four_t, four_l
-    )
+        return through_four(t, state)
+
+    extra = lax.switch(far[0], (fetch_none, fetch_eight, fetch_twelve), four_t, four_l)
     (normed,) = call(
         finish_kernel,
         (meta,),

time: 154 us -> 154 us (level)
  no operation moved by 1% of the time
where the time goes in v13:
time: 154 us; the launch traced here: 153 us
  blocking collectives  90.1 us (59%)
  starting transfers between devices  43.9 us (29%)
  Pallas kernels  9.49 us (6%)
  matrix products  3.42 us (2%)
  local copies, waits for them, and re-layouts  1.84 us (1%)
  waiting for transfers between devices  1.81 us (1%)
    all_gather x1, blocking collectives, per_device(): both = lax.all_gather(both, 'z', axis=0, tiled=True)  67.2 us
    ppermute x4, starting transfers between devices, swap(): return lax.ppermute(value, 'c', [(0, 1), (1, 0)])  32.1 us
    all_gather x1, blocking collectives, per_device(): normed_all = lax.all_gather(to_f16(normed, N_SCALE), 'h', axis=0)  22.9 us
    ppermute x3, starting transfers between devices, ahead(): lax.ppermute(value, 'z', [(i, i + steps) for i in range(chips - steps)])  10.4 us
    pallas_call x1, Pallas kernels, per_device(): pl.pallas_call(functools.partial(local_kernel, chips), out_shape=(jax.Sha...  4.97 us
    pallas_call x5, Pallas kernels, call(): pl.pallas_call(kernel, out_shape=tuple((jax.ShapeDtypeStruct(s, d) for s,...  4.53 us
  transfers between devices with their start and end apart: 8, of which 2 were waited for; matrix products, arithmetic and copies ran while one was open for 2% of the time, Pallas kernels for 3%

profile of v13, /device:TPU:1, one launch (start us, length us, event | category | flops | bytes accessed | tf_op | source)
XLA Modules:
  0.0 153.0 jit_solution(17090264035640007147)
XLA Ops:
  0.0 1.5 collective-permute-start.7
  1.6 0.9 copy-done
  2.5 0.7 copy-done.1
  3.2 0.6 shard_map.55
  3.8 8.8 %collective-permute-start.6 = (bf16[128,512]{1,0:T(8,128)(2,1)S(1)}, bf16[128,512]{1,0:T(8,128)(2,1)S(1)}, u32[]{:S(2)}, u32[]{:S(2)}) collective-permute-start(bf16[128,512]{1,0:T(8,128)(2,1)S(1)} %get-tuple-element.33), channel_id=1, source_target_pairs={{0,16},{16,0},{1,17},{17,1},{2,18},{18,2},{3,19},{19,3},{4,20},{20... | collective-permute-start | bytes 393224 | tf_op jit(solution)/shard_map/ppermute | solution.py:260
  12.6 1.9 %collective-permute-start.8 = (bf16[256,4096]{1,0:T(8,128)(2,1)}, bf16[256,4096]{1,0:T(8,128)(2,1)S(1)}, u32[]{:S(2)}, u32[]{:S(2)}) collective-permute-start(bf16[256,4096]{1,0:T(8,128)(2,1)} %param.8), channel_id=1, source_target_pairs={{0,16},{16,0},{1,17},{17,1},{2,18},{18,2},{3,19},{19,3},{4,20},{20... | collective-permute-start | bytes 6291464 | tf_op jit(solution)/shard_map/ppermute | solution.py:260
  14.7 67.2 %all-gather.3 = f16[4096,512]{1,0:T(8,128)(2,1)S(1)} all-gather(f16[256,512]{1,0:T(8,128)(2,1)S(1)} %pad_maximum_fusion.3), channel_id=1, replica_groups=mesh['z'=16,'c'=2,'h'=16] {'z'}, dimensions={0}, use_global_device_ids=true | all-gather | bytes 4456448 | tf_op jit(solution)/shard_map/all_gather | solution.py:310
  82.0 1.3 fusion.4.own_ref
  83.3 1.3 fusion.5.sib_ref
  84.6 5.0 %shard_map.56 = (f32[128,256]{1,0:T(8,128)S(1)}, bf16[128,256]{1,0:T(8,128)(2,1)S(1)}, f32[512,256]{1,0:T(8,128)S(1)}, f32[128,512]{1,0:T(8,128)S(1)}, s32[1]{0:T(128)}) custom-call(s32[2]{0:T(128)S(1)} %pad_add_fusion.meta_ref, s32[9]{0:T(128)S(1)} %copy-done.3, bf16[256,384]{1,0:T(8,128)(2,1)S(1)} %fusion.4.own_ref, bf16[256,384]{1,0:T(8,128)(2,1)S(1)} %fusion.5.sib_ref, ...), custom_call_target="tpu_custom_call" | custom-call | flops 3221225472 | bytes 1048576 | tf_op jit(solution)/shard_map/pallas_call | solution.py:317
  89.6 2.1 %collective-permute-start.9 = (bf16[128,256]{1,0:T(8,128)(2,1)S(1)}, bf16[128,256]{1,0:T(8,128)(2,1)S(1)}, u32[]{:S(2)}, u32[]{:S(2)}) collective-permute-start(bf16[128,256]{1,0:T(8,128)(2,1)S(1)} %get-tuple-element.35), channel_id=1, source_target_pairs={{0,32},{32,64},{64,96},{96,128},{128,160},{160,192},{192,224},{224... | collective-permute-start | bytes 196616 | tf_op jit(solution)/shard_map/ppermute | solution.py:265
  91.9 1.1 collective-permute-done.9.one_ref
  93.1 3.4 %collective-permute-start.10 = (bf16[128,256]{1,0:T(8,128)(2,1)S(1)}, bf16[128,256]{1,0:T(8,128)(2,1)S(1)}, u32[]{:S(2)}, u32[]{:S(2)}) collective-permute-start(bf16[128,256]{1,0:T(8,128)(2,1)S(1)} %shard_map.57), channel_id=1, source_target_pairs={{0,64},{32,96},{64,128},{96,160},{128,192},{160,224},{192,256},{22... | collective-permute-start | bytes 196616 | tf_op jit(solution)/shard_map/ppermute | solution.py:265
  96.8 11.5 %collective-permute-start.12 = (bf16[16,128,128]{2,1,0:T(8,128)(2,1)S(1)}, bf16[16,128,128]{2,1,0:T(8,128)(2,1)S(1)}, u32[]{:S(2)}, u32[]{:S(2)}) collective-permute-start(bf16[16,128,128]{2,1,0:T(8,128)(2,1)S(1)} %fusion.11), channel_id=1, source_target_pairs={{0,16},{16,0},{1,17},{17,1},{2,18},{18,2},{3,19},{19,3},{4,20},{20... | collective-permute-start | bytes 1572872 | tf_op jit(solution)/shard_map/ppermute | solution.py:260
  109.0 1.0 shard_map.58
  109.9 4.8 %collective-permute-start.11 = (bf16[128,128]{1,0:T(8,128)(2,1)}, bf16[128,128]{1,0:T(8,128)(2,1)S(1)}, u32[]{:S(2)}, u32[]{:S(2)}) collective-permute-start(bf16[128,128]{1,0:T(8,128)(2,1)} %get-tuple-element.37), channel_id=1, source_target_pairs={{0,128},{32,160},{64,192},{96,224},{128,256},{160,288},{192,320},{... | collective-permute-start | bytes 98312 | tf_op jit(solution)/shard_map/ppermute | solution.py:265
  114.8 1.7 %shard_map.59.b_ref = f32[2,512,128]{2,1,0:T(8,128)S(1)} custom-call(s32[2]{0:T(128)S(1)} %pad_add_fusion.meta_ref, s32[9]{0:T(128)S(1)} %copy-done.3, bf16[256,384]{1,0:T(8,128)(2,1)S(1)} %fusion.4.own_ref, bf16[256,384]{1,0:T(8,128)(2,1)S(1)} %fusion.5.sib_ref, f32[128,512]{1,0:T(8,128)S(1)} %get-tuple-element.40.kt_ref, ...), custom_call_target="tpu_custom_call" | custom-call | flops 1073741824 | bytes 1048576 | tf_op jit(solution)/shard_map/pallas_call | solution.py:249
  116.5 1.1 shard_map.60
  117.7 22.9 %all-gather.4 = f16[8192,128]{1,0:T(8,128)(2,1)S(1)} all-gather(f16[512,128]{1,0:T(8,128)(2,1)S(1)} %multiply_convert_fusion.18), channel_id=2, replica_groups=mesh['z'=16,'c'=2,'h'=16] {'h'}, dimensions={0}, use_global_device_ids=true | all-gather | bytes 2228224 | tf_op jit(solution)/shard_map/all_gather | solution.py:379
  140.9 0.4 convolution_bitcast_fusion.1
  141.3 9.8 %collective-permute-start.13 = (f32[256,256]{1,0:T(8,128)S(1)}, f32[256,256]{1,0:T(8,128)S(1)}, u32[]{:S(2)}, u32[]{:S(2)}) collective-permute-start(f32[256,256]{1,0:T(8,128)S(1)} %convolution_bitcast_fusion.1), channel_id=1, source_target_pairs={{0,16},{16,0},{1,17},{17,1},{2,18},{18,2},{3,19},{19,3},{4,20},{20... | collective-permute-start | bytes 786440 | tf_op jit(solution)/shard_map/ppermute | solution.py:260
  151.2 0.4 convolution_bitcast_fusion.2
  151.6 0.7 collective-permute-done.13
  152.3 0.7 add_convert_fusion
  (26 shorter events, 1.2 us)
Async XLA Ops:
  0.0 14.5 %collective-permute-start.7 = (bf16[256,128]{1,0:T(8,128)(2,1)}, bf16[256,128]{1,0:T(8,128)(2,1)S(1)}, u32[]{:S(2)}, u32[]{:S(2)}) collective-permute-start(bf16[256,128]{1,0:T(8,128)(2,1)} %param.12), channel_id=1, source_target_pairs={{0,0},{1,32},{2,64},{3,96},{4,128},{5,160},{6,192},{7,224},{8,256}... | collective-permute-start | bytes 196616 | tf_op jit(solution)/shard_map/ppermute | solution.py:292
  1.6 0.9 copy-start
  2.5 0.7 copy-start.1
  3.8 10.8 %collective-permute-start.6 = (bf16[128,512]{1,0:T(8,128)(2,1)S(1)}, bf16[128,512]{1,0:T(8,128)(2,1)S(1)}, u32[]{:S(2)}, u32[]{:S(2)}) collective-permute-start(bf16[128,512]{1,0:T(8,128)(2,1)S(1)} %get-tuple-element.33), channel_id=1, source_target_pairs={{0,16},{16,0},{1,17},{17,1},{2,18},{18,2},{3,19},{19,3},{4,20},{20... | collective-permute-start | bytes 393224 | tf_op jit(solution)/shard_map/ppermute | solution.py:260
  12.6 70.7 %collective-permute-start.8 = (bf16[256,4096]{1,0:T(8,128)(2,1)}, bf16[256,4096]{1,0:T(8,128)(2,1)S(1)}, u32[]{:S(2)}, u32[]{:S(2)}) collective-permute-start(bf16[256,4096]{1,0:T(8,128)(2,1)} %param.8), channel_id=1, source_target_pairs={{0,16},{16,0},{1,17},{17,1},{2,18},{18,2},{3,19},{19,3},{4,20},{20... | collective-permute-start | bytes 6291464 | tf_op jit(solution)/shard_map/ppermute | solution.py:260
  14.7 67.3 %copy-start.4 = (bf16[256,4096]{1,0:T(8,128)(2,1)S(1)}, bf16[256,4096]{1,0:T(8,128)(2,1)}, u32[]{:S(2)}) copy-start(bf16[256,4096]{1,0:T(8,128)(2,1)} %param.8) | copy-start | bytes 6291460
  83.2 1.3 copy-start.2
  83.3 1.3 copy-start.3
  89.6 3.4 %collective-permute-start.9 = (bf16[128,256]{1,0:T(8,128)(2,1)S(1)}, bf16[128,256]{1,0:T(8,128)(2,1)S(1)}, u32[]{:S(2)}, u32[]{:S(2)}) collective-permute-start(bf16[128,256]{1,0:T(8,128)(2,1)S(1)} %get-tuple-element.35), channel_id=1, source_target_pairs={{0,32},{32,64},{64,96},{96,128},{128,160},{160,192},{192,224},{224... | collective-permute-start | bytes 196616 | tf_op jit(solution)/shard_map/ppermute | solution.py:265
  93.1 15.8 %collective-permute-start.10 = (bf16[128,256]{1,0:T(8,128)(2,1)S(1)}, bf16[128,256]{1,0:T(8,128)(2,1)S(1)}, u32[]{:S(2)}, u32[]{:S(2)}) collective-permute-start(bf16[128,256]{1,0:T(8,128)(2,1)S(1)} %shard_map.57), channel_id=1, source_target_pairs={{0,64},{32,96},{64,128},{96,160},{128,192},{160,224},{192,256},{22... | collective-permute-start | bytes 196616 | tf_op jit(solution)/shard_map/ppermute | solution.py:265
  96.8 43.8 %collective-permute-start.12 = (bf16[16,128,128]{2,1,0:T(8,128)(2,1)S(1)}, bf16[16,128,128]{2,1,0:T(8,128)(2,1)S(1)}, u32[]{:S(2)}, u32[]{:S(2)}) collective-permute-start(bf16[16,128,128]{2,1,0:T(8,128)(2,1)S(1)} %fusion.11), channel_id=1, source_target_pairs={{0,16},{16,0},{1,17},{17,1},{2,18},{18,2},{3,19},{19,3},{4,20},{20... | collective-permute-start | bytes 1572872 | tf_op jit(solution)/shard_map/ppermute | solution.py:260
  109.9 6.6 %collective-permute-start.11 = (bf16[128,128]{1,0:T(8,128)(2,1)}, bf16[128,128]{1,0:T(8,128)(2,1)S(1)}, u32[]{:S(2)}, u32[]{:S(2)}) collective-permute-start(bf16[128,128]{1,0:T(8,128)(2,1)} %get-tuple-element.37), channel_id=1, source_target_pairs={{0,128},{32,160},{64,192},{96,224},{128,256},{160,288},{192,320},{... | collective-permute-start | bytes 98312 | tf_op jit(solution)/shard_map/ppermute | solution.py:265
  141.3 11.0 %collective-permute-start.13 = (f32[256,256]{1,0:T(8,128)S(1)}, f32[256,256]{1,0:T(8,128)S(1)}, u32[]{:S(2)}, u32[]{:S(2)}) collective-permute-start(f32[256,256]{1,0:T(8,128)S(1)} %convolution_bitcast_fusion.1), channel_id=1, source_target_pairs={{0,16},{16,0},{1,17},{17,1},{2,18},{18,2},{3,19},{19,3},{4,20},{20... | collective-permute-start | bytes 786440 | tf_op jit(solution)/shard_map/ppermute | solution.py:260

commit v14 on v11

--- a/solution.py
+++ b/solution.py
@@ -374,7 +374,7 @@
         rows = from_f16(rows, N_SCALE)
         return jnp.einsum("htf,hfn->tn", rows, wo_cols, preferred_element_type=F32)
 
-    sent = swap(output(normed_all[:, :half]))
+    sent = swap(output(normed_all[:, :half]).astype(BF16)).astype(F32)
     kept = lax.optimization_barrier(output(normed_all[:, half:]))
     return (kept + sent).astype(BF16)
 

time: 154 us -> 154 us (level)
  no operation moved by 1% of the time
where the time goes in v14:
time: 154 us; the launch traced here: 153 us
  blocking collectives  90.1 us (59%)
  starting transfers between devices  43.9 us (29%)
  Pallas kernels  9.49 us (6%)
  matrix products  3.43 us (2%)
  local copies, waits for them, and re-layouts  1.84 us (1%)
  waiting for transfers between devices  1.63 us (1%)
  other arithmetic  1.56 us (1%)
    all_gather x1, blocking collectives, per_device(): both = lax.all_gather(both, 'z', axis=0, tiled=True)  67.2 us
    ppermute x4, starting transfers between devices, swap(): return lax.ppermute(value, 'c', [(0, 1), (1, 0)])  32.1 us
    all_gather x1, blocking collectives, per_device(): normed_all = lax.all_gather(to_f16(normed, N_SCALE), 'h', axis=0)  22.9 us
    ppermute x3, starting transfers between devices, ahead(): lax.ppermute(value, 'z', [(i, i + steps) for i in range(chips - steps)])  10.4 us
    pallas_call x1, Pallas kernels, per_device(): pl.pallas_call(functools.partial(local_kernel, chips), out_shape=(jax.Sha...  4.96 us
    pallas_call x5, Pallas kernels, call(): pl.pallas_call(kernel, out_shape=tuple((jax.ShapeDtypeStruct(s, d) for s,...  4.53 us
  transfers between devices with their start and end apart: 8, of which 2 were waited for; matrix products, arithmetic and copies ran while one was open for 2% of the time, Pallas kernels for 3%

profile of v14, /device:TPU:1, one launch (start us, length us, event | category | flops | bytes accessed | tf_op | source)
XLA Modules:
  0.0 152.9 jit_solution(9236634466199738776)
XLA Ops:
  0.0 1.5 collective-permute-start.5
  1.6 0.9 copy-done
  2.5 0.7 copy-done.1
  3.2 0.6 shard_map.55
  3.8 8.8 %collective-permute-start.4 = (bf16[128,512]{1,0:T(8,128)(2,1)S(1)}, bf16[128,512]{1,0:T(8,128)(2,1)S(1)}, u32[]{:S(2)}, u32[]{:S(2)}) collective-permute-start(bf16[128,512]{1,0:T(8,128)(2,1)S(1)} %get-tuple-element.26), channel_id=1, source_target_pairs={{0,16},{16,0},{1,17},{17,1},{2,18},{18,2},{3,19},{19,3},{4,20},{20... | collective-permute-start | bytes 393224 | tf_op jit(solution)/shard_map/ppermute | solution.py:260
  12.6 1.9 %collective-permute-start.6 = (bf16[256,4096]{1,0:T(8,128)(2,1)}, bf16[256,4096]{1,0:T(8,128)(2,1)S(1)}, u32[]{:S(2)}, u32[]{:S(2)}) collective-permute-start(bf16[256,4096]{1,0:T(8,128)(2,1)} %param.7), channel_id=1, source_target_pairs={{0,16},{16,0},{1,17},{17,1},{2,18},{18,2},{3,19},{19,3},{4,20},{20... | collective-permute-start | bytes 6291464 | tf_op jit(solution)/shard_map/ppermute | solution.py:260
  14.7 67.2 %all-gather.3 = f16[4096,512]{1,0:T(8,128)(2,1)S(1)} all-gather(f16[256,512]{1,0:T(8,128)(2,1)S(1)} %pad_maximum_fusion.3), channel_id=1, replica_groups=mesh['z'=16,'c'=2,'h'=16] {'z'}, dimensions={0}, use_global_device_ids=true | all-gather | bytes 4456448 | tf_op jit(solution)/shard_map/all_gather | solution.py:310
  82.0 1.3 fusion.4.own_ref
  83.3 1.3 fusion.5.sib_ref
  84.6 5.0 %shard_map.56 = (f32[128,256]{1,0:T(8,128)S(1)}, bf16[128,256]{1,0:T(8,128)(2,1)S(1)}, f32[512,256]{1,0:T(8,128)S(1)}, f32[128,512]{1,0:T(8,128)S(1)}, s32[1]{0:T(128)}) custom-call(s32[2]{0:T(128)S(1)} %pad_add_fusion.meta_ref, s32[9]{0:T(128)S(1)} %copy-done.3, bf16[256,384]{1,0:T(8,128)(2,1)S(1)} %fusion.4.own_ref, bf16[256,384]{1,0:T(8,128)(2,1)S(1)} %fusion.5.sib_ref, ...), custom_call_target="tpu_custom_call" | custom-call | flops 3221225472 | bytes 1048576 | tf_op jit(solution)/shard_map/pallas_call | solution.py:317
  89.6 2.1 %collective-permute-start.7 = (bf16[128,256]{1,0:T(8,128)(2,1)S(1)}, bf16[128,256]{1,0:T(8,128)(2,1)S(1)}, u32[]{:S(2)}, u32[]{:S(2)}) collective-permute-start(bf16[128,256]{1,0:T(8,128)(2,1)S(1)} %get-tuple-element.28), channel_id=1, source_target_pairs={{0,32},{32,64},{64,96},{96,128},{128,160},{160,192},{192,224},{224... | collective-permute-start | bytes 196616 | tf_op jit(solution)/shard_map/ppermute | solution.py:265
  91.9 1.1 collective-permute-done.7.one_ref
  93.1 3.4 %collective-permute-start.8 = (bf16[128,256]{1,0:T(8,128)(2,1)S(1)}, bf16[128,256]{1,0:T(8,128)(2,1)S(1)}, u32[]{:S(2)}, u32[]{:S(2)}) collective-permute-start(bf16[128,256]{1,0:T(8,128)(2,1)S(1)} %shard_map.57), channel_id=1, source_target_pairs={{0,64},{32,96},{64,128},{96,160},{128,192},{160,224},{192,256},{22... | collective-permute-start | bytes 196616 | tf_op jit(solution)/shard_map/ppermute | solution.py:265
  96.8 11.5 %collective-permute-start.10 = (bf16[16,128,128]{2,1,0:T(8,128)(2,1)S(1)}, bf16[16,128,128]{2,1,0:T(8,128)(2,1)S(1)}, u32[]{:S(2)}, u32[]{:S(2)}) collective-permute-start(bf16[16,128,128]{2,1,0:T(8,128)(2,1)S(1)} %fusion.12), channel_id=1, source_target_pairs={{0,16},{16,0},{1,17},{17,1},{2,18},{18,2},{3,19},{19,3},{4,20},{20... | collective-permute-start | bytes 1572872 | tf_op jit(solution)/shard_map/ppermute | solution.py:260
  109.0 1.0 shard_map.58
  109.9 4.8 %collective-permute-start.9 = (bf16[128,128]{1,0:T(8,128)(2,1)}, bf16[128,128]{1,0:T(8,128)(2,1)S(1)}, u32[]{:S(2)}, u32[]{:S(2)}) collective-permute-start(bf16[128,128]{1,0:T(8,128)(2,1)} %get-tuple-element.30), channel_id=1, source_target_pairs={{0,128},{32,160},{64,192},{96,224},{128,256},{160,288},{192,320},{... | collective-permute-start | bytes 98312 | tf_op jit(solution)/shard_map/ppermute | solution.py:265
  114.8 1.7 %shard_map.59.b_ref = f32[2,512,128]{2,1,0:T(8,128)S(1)} custom-call(s32[2]{0:T(128)S(1)} %pad_add_fusion.meta_ref, s32[9]{0:T(128)S(1)} %copy-done.3, bf16[256,384]{1,0:T(8,128)(2,1)S(1)} %fusion.4.own_ref, bf16[256,384]{1,0:T(8,128)(2,1)S(1)} %fusion.5.sib_ref, f32[128,512]{1,0:T(8,128)S(1)} %get-tuple-element.33.kt_ref, ...), custom_call_target="tpu_custom_call" | custom-call | flops 1073741824 | bytes 1048576 | tf_op jit(solution)/shard_map/pallas_call | solution.py:249
  116.5 1.1 shard_map.60
  117.7 22.9 %all-gather.4 = f16[8192,128]{1,0:T(8,128)(2,1)S(1)} all-gather(f16[512,128]{1,0:T(8,128)(2,1)S(1)} %multiply_convert_fusion.18), channel_id=2, replica_groups=mesh['z'=16,'c'=2,'h'=16] {'h'}, dimensions={0}, use_global_device_ids=true | all-gather | bytes 2228224 | tf_op jit(solution)/shard_map/all_gather | solution.py:372
  141.0 0.4 fusion.6
  141.4 9.8 %collective-permute-start.11 = (bf16[256,256]{1,0:T(8,128)(2,1)S(1)}, bf16[256,256]{1,0:T(8,128)(2,1)S(1)}, u32[]{:S(2)}, u32[]{:S(2)}) collective-permute-start(bf16[256,256]{1,0:T(8,128)(2,1)S(1)} %fusion.6), channel_id=1, source_target_pairs={{0,16},{16,0},{1,17},{17,1},{2,18},{18,2},{3,19},{19,3},{4,20},{20... | collective-permute-start | bytes 393224 | tf_op jit(solution)/shard_map/ppermute | solution.py:260
  151.3 0.4 convolution_bitcast_fusion.2
  151.7 0.5 collective-permute-done.11
  152.2 0.7 add_convert_fusion
  (26 shorter events, 1.3 us)
Async XLA Ops:
  0.0 14.5 %collective-permute-start.5 = (bf16[256,128]{1,0:T(8,128)(2,1)}, bf16[256,128]{1,0:T(8,128)(2,1)S(1)}, u32[]{:S(2)}, u32[]{:S(2)}) collective-permute-start(bf16[256,128]{1,0:T(8,128)(2,1)} %param.11), channel_id=1, source_target_pairs={{0,0},{1,32},{2,64},{3,96},{4,128},{5,160},{6,192},{7,224},{8,256}... | collective-permute-start | bytes 196616 | tf_op jit(solution)/shard_map/ppermute | solution.py:292
  1.6 0.9 copy-start
  2.5 0.7 copy-start.1
  3.8 10.8 %collective-permute-start.4 = (bf16[128,512]{1,0:T(8,128)(2,1)S(1)}, bf16[128,512]{1,0:T(8,128)(2,1)S(1)}, u32[]{:S(2)}, u32[]{:S(2)}) collective-permute-start(bf16[128,512]{1,0:T(8,128)(2,1)S(1)} %get-tuple-element.26), channel_id=1, source_target_pairs={{0,16},{16,0},{1,17},{17,1},{2,18},{18,2},{3,19},{19,3},{4,20},{20... | collective-permute-start | bytes 393224 | tf_op jit(solution)/shard_map/ppermute | solution.py:260
  12.6 70.7 %collective-permute-start.6 = (bf16[256,4096]{1,0:T(8,128)(2,1)}, bf16[256,4096]{1,0:T(8,128)(2,1)S(1)}, u32[]{:S(2)}, u32[]{:S(2)}) collective-permute-start(bf16[256,4096]{1,0:T(8,128)(2,1)} %param.7), channel_id=1, source_target_pairs={{0,16},{16,0},{1,17},{17,1},{2,18},{18,2},{3,19},{19,3},{4,20},{20... | collective-permute-start | bytes 6291464 | tf_op jit(solution)/shard_map/ppermute | solution.py:260
  14.7 67.3 %copy-start.4 = (bf16[256,4096]{1,0:T(8,128)(2,1)S(1)}, bf16[256,4096]{1,0:T(8,128)(2,1)}, u32[]{:S(2)}) copy-start(bf16[256,4096]{1,0:T(8,128)(2,1)} %param.7) | copy-start | bytes 6291460
  83.2 1.3 copy-start.2
  83.3 1.3 copy-start.3
  89.6 3.4 %collective-permute-start.7 = (bf16[128,256]{1,0:T(8,128)(2,1)S(1)}, bf16[128,256]{1,0:T(8,128)(2,1)S(1)}, u32[]{:S(2)}, u32[]{:S(2)}) collective-permute-start(bf16[128,256]{1,0:T(8,128)(2,1)S(1)} %get-tuple-element.28), channel_id=1, source_target_pairs={{0,32},{32,64},{64,96},{96,128},{128,160},{160,192},{192,224},{224... | collective-permute-start | bytes 196616 | tf_op jit(solution)/shard_map/ppermute | solution.py:265
  93.1 15.8 %collective-permute-start.8 = (bf16[128,256]{1,0:T(8,128)(2,1)S(1)}, bf16[128,256]{1,0:T(8,128)(2,1)S(1)}, u32[]{:S(2)}, u32[]{:S(2)}) collective-permute-start(bf16[128,256]{1,0:T(8,128)(2,1)S(1)} %shard_map.57), channel_id=1, source_target_pairs={{0,64},{32,96},{64,128},{96,160},{128,192},{160,224},{192,256},{22... | collective-permute-start | bytes 196616 | tf_op jit(solution)/shard_map/ppermute | solution.py:265
  96.8 43.8 %collective-permute-start.10 = (bf16[16,128,128]{2,1,0:T(8,128)(2,1)S(1)}, bf16[16,128,128]{2,1,0:T(8,128)(2,1)S(1)}, u32[]{:S(2)}, u32[]{:S(2)}) collective-permute-start(bf16[16,128,128]{2,1,0:T(8,128)(2,1)S(1)} %fusion.12), channel_id=1, source_target_pairs={{0,16},{16,0},{1,17},{17,1},{2,18},{18,2},{3,19},{19,3},{4,20},{20... | collective-permute-start | bytes 1572872 | tf_op jit(solution)/shard_map/ppermute | solution.py:260
  109.9 6.6 %collective-permute-start.9 = (bf16[128,128]{1,0:T(8,128)(2,1)}, bf16[128,128]{1,0:T(8,128)(2,1)S(1)}, u32[]{:S(2)}, u32[]{:S(2)}) collective-permute-start(bf16[128,128]{1,0:T(8,128)(2,1)} %get-tuple-element.30), channel_id=1, source_target_pairs={{0,128},{32,160},{64,192},{96,224},{128,256},{160,288},{192,320},{... | collective-permute-start | bytes 98312 | tf_op jit(solution)/shard_map/ppermute | solution.py:265
  141.4 10.8 %collective-permute-start.11 = (bf16[256,256]{1,0:T(8,128)(2,1)S(1)}, bf16[256,256]{1,0:T(8,128)(2,1)S(1)}, u32[]{:S(2)}, u32[]{:S(2)}) collective-permute-start(bf16[256,256]{1,0:T(8,128)(2,1)S(1)} %fusion.6), channel_id=1, source_target_pairs={{0,16},{16,0},{1,17},{17,1},{2,18},{18,2},{3,19},{19,3},{4,20},{20... | collective-permute-start | bytes 393224 | tf_op jit(solution)/shard_map/ppermute | solution.py:260
